TPU v7x, 32 devices: a whole 2x2x4 slice. The times are simulated.
32 devices in a mesh: batch: 16 (over z, y, x), tensor: 2 (over core).
Axes of the slice: x: 2, y: 2, z: 4, core: 2. Of those that a mesh axis runs over, the one named last changes fastest.
Arguments:
- features: bfloat16 [16, 1024, 1024], P('batch', 'tensor'), may hold values from -6 to 6
- lengths: int32 [16], P('batch'), may hold values from 256 to 1024, as said below
- norm_gains: bfloat16 [5, 1024], replicated, may hold values from 0.5 to 1.5
- norm_shifts: bfloat16 [5, 1024], replicated, may hold values from -3 to 3
- first_up: bfloat16 [1024, 4096], P(None, 'tensor'), may hold values from -0.1875 to 0.1875
- first_down: bfloat16 [4096, 1024], P('tensor'), may hold values from -0.1875 to 0.1875
- attention_in: bfloat16 [3, 1024, 1024], P(None, None, 'tensor'), may hold values from -0.1875 to 0.1875
- position_proj: bfloat16 [1024, 1024], P(None, 'tensor'), may hold values from -0.1875 to 0.1875
- position_bias: bfloat16 [2, 8, 128], P(None, 'tensor'), may hold values from -3 to 3
- attention_out: bfloat16 [1024, 1024], P('tensor'), may hold values from -0.75 to 0.75
- pointwise_in: bfloat16 [1024, 2, 1024], P(None, None, 'tensor'), may hold values from -0.1875 to 0.1875
- depthwise: bfloat16 [5, 1024], P(None, 'tensor'), may hold values from -2.5 to 2.5
- batch_gain: bfloat16 [1024], P('tensor'), may hold values from 0.5 to 1.5
- batch_shift: bfloat16 [1024], P('tensor'), may hold values from -3 to 3
- pointwise_out: bfloat16 [1024, 1024], P('tensor'), may hold values from -0.25 to 0.25
- second_up: bfloat16 [1024, 4096], P(None, 'tensor'), may hold values from -0.1875 to 0.1875
- second_down: bfloat16 [4096, 1024], P('tensor'), may hold values from -0.1875 to 0.1875
- cotangent: bfloat16 [16, 1024, 1024], P('batch', 'tensor'), may hold values from -6 to 6
Outputs:
- output: bfloat16 [16, 1024, 1024], P('batch', 'tensor')
- input_grad: float32 [16, 1024, 1024], P('batch', 'tensor')
- grad_norm_gains: float32 [5, 1024], replicated
- grad_norm_shifts: float32 [5, 1024], replicated
- grad_first_up: float32 [1024, 4096], P('batch', 'tensor')
- grad_first_down: float32 [4096, 1024], P('tensor', 'batch')
- grad_attention_in: float32 [3, 1024, 1024], P(None, 'batch', 'tensor')
- grad_position_proj: float32 [1024, 1024], P('batch', 'tensor')
- grad_position_bias: float32 [2, 8, 128], P(None, 'tensor')
- grad_attention_out: float32 [1024, 1024], P('tensor', 'batch')
- grad_pointwise_in: float32 [1024, 2, 1024], P('batch', None, 'tensor')
- grad_depthwise: float32 [5, 1024], P(None, 'tensor')
- grad_batch_gain: float32 [1024], P('tensor')
- grad_batch_shift: float32 [1024], P('tensor')
- grad_pointwise_out: float32 [1024, 1024], P('tensor', 'batch')
- grad_second_up: float32 [1024, 4096], P('batch', 'tensor')
- grad_second_down: float32 [4096, 1024], P('tensor', 'batch')
Inputs may be any that keep to these rules, and one draw needn't show every extreme that they name: Frames from lengths[r] on are padding; in every draw some slot is full, holding 1024 frames, and some slot holds 256 frames.
All inputs are finite; a program needn't handle non-finite values.
Results may differ from a plain program's by a relative error of at most 0.03.
Values may be sent and summed in bfloat16 or wider, within the bound.
A program may use at most 320 MiB of HBM per device.

v0:
```python
import math

import jax
import jax.numpy as jnp
from jax import lax
from jax.sharding import PartitionSpec as P

eps_norm = 1e-05
eps_batch = 1e-05


def contract_rows(left, right):
    return lax.dot_general(
        left, right, (((0,), (0,)), ((), ())), preferred_element_type=jnp.float32
    )


def times_transposed(left, right):
    return lax.dot_general(
        left, right, (((1,), (1,)), ((), ())), preferred_element_type=jnp.float32
    )


def norm_forward(values, norm_gain, norm_shift):
    center = values - jnp.mean(values, axis=-1, keepdims=True)
    inv_std = lax.rsqrt(jnp.mean(center * center, axis=-1, keepdims=True) + eps_norm)
    scaled = center * inv_std
    return (scaled * norm_gain + norm_shift, scaled, inv_std)


def norm_backward(grad_out, scaled, inv_std, norm_gain):
    grad_scaled = grad_out * norm_gain
    grad_in = inv_std * (
        grad_scaled
        - jnp.mean(grad_scaled, axis=-1, keepdims=True)
        - scaled * jnp.mean(grad_scaled * scaled, axis=-1, keepdims=True)
    )
    return (grad_in, jnp.sum(grad_out * scaled, axis=(0, 1)), jnp.sum(grad_out, axis=(0, 1)))


def widen(normed):
    return lax.all_gather(normed.astype(jnp.bfloat16), "tensor", axis=1, tiled=True)


def narrow(partial_out):
    return lax.psum_scatter(
        partial_out.astype(jnp.bfloat16), "tensor", scatter_dimension=1, tiled=True
    ).astype(jnp.float32)


def widen_grad(grad_half):
    return lax.all_gather(grad_half.astype(jnp.bfloat16), "tensor", axis=1, tiled=True)


def narrow_grad(partial_grad):
    return lax.psum_scatter(
        partial_grad.astype(jnp.bfloat16), "tensor", scatter_dimension=1, tiled=True
    ).astype(jnp.float32)


def relative_table(slot_frames, model_width):
    offsets = (slot_frames - 1 - jnp.arange(2 * slot_frames - 1)).astype(jnp.float32)
    column = jnp.arange(model_width // 2).astype(jnp.float32)
    freqs = jnp.exp(column * (-2.0 * math.log(10000.0) / model_width))
    angles = offsets[:, None] * freqs[None, :]
    return jnp.stack([jnp.sin(angles), jnp.cos(angles)], axis=-1).reshape(
        2 * slot_frames - 1, model_width
    )


def skew(wide, slot_frames):
    head_count, block_size, window_len = wide.shape
    flat_wide = wide.reshape(head_count, block_size * window_len)
    flat_wide = lax.slice_in_dim(
        flat_wide, block_size - 1, block_size - 1 + block_size * (window_len - 1), axis=1
    )
    return flat_wide.reshape(head_count, block_size, window_len - 1)[:, :, :slot_frames]


def unskew(grad_raw, window_len):
    head_count, block_size, slot_frames = grad_raw.shape
    padded = jnp.pad(grad_raw, ((0, 0), (0, 0), (0, window_len - 1 - slot_frames)))
    flat_grad = padded.reshape(head_count, block_size * (window_len - 1))
    flat_grad = jnp.pad(flat_grad, ((0, 0), (block_size - 1, 1)))
    return flat_grad.reshape(head_count, block_size, window_len)


def block_raw(block_content, block_position, slot_keys, table, block_start, length):
    block_size = block_content.shape[0]
    slot_frames = slot_keys.shape[0]
    window = lax.dynamic_slice_in_dim(
        table, slot_frames - block_size - block_start, block_size + slot_frames - 1, 0
    )
    content = jnp.einsum(
        "bhe,khe->hbk", block_content, slot_keys, preferred_element_type=jnp.float32
    )
    wide = jnp.einsum("bhe,whe->hbw", block_position, window, preferred_element_type=jnp.float32)
    raw = content + skew(wide, slot_frames)
    live_keys = lax.broadcasted_iota(jnp.int32, (1, 1, slot_frames), 2) < length
    scores = jnp.where(live_keys, raw * block_content.shape[2] ** (-0.5), -jnp.inf)
    return (scores, window)


def ffn_forward(residual, norm_gain, norm_shift, weight_up, weight_down):
    normed, scaled, inv_std = norm_forward(residual, norm_gain, norm_shift)
    gathered = widen(normed)
    slot_count, slot_frames, model_width = gathered.shape
    flat_act = gathered.reshape(slot_count * slot_frames, model_width)
    pre_act = jnp.dot(flat_act, weight_up, preferred_element_type=jnp.float32)
    hidden = (pre_act * jax.nn.sigmoid(pre_act)).astype(jnp.bfloat16)
    partial_out = jnp.dot(hidden, weight_down, preferred_element_type=jnp.float32).reshape(
        slot_count, slot_frames, model_width
    )
    return (narrow(partial_out), (scaled, inv_std, flat_act, pre_act, hidden))


def ffn_backward(grad_after, saved, norm_gain, weight_up, weight_down):
    scaled, inv_std, flat_act, pre_act, hidden = saved
    grad_round = widen_grad(grad_after)
    slot_count, slot_frames, model_width = grad_round.shape
    grad_flat = grad_round.reshape(slot_count * slot_frames, model_width)
    grad_down = contract_rows(hidden, grad_flat)
    grad_hidden = times_transposed(grad_flat, weight_down)
    gate_sig = jax.nn.sigmoid(pre_act)
    grad_pre = (grad_hidden * gate_sig * (1.0 + pre_act * (1.0 - gate_sig))).astype(jnp.bfloat16)
    grad_up = contract_rows(flat_act, grad_pre)
    grad_act = times_transposed(grad_pre, weight_up).reshape(slot_count, slot_frames, model_width)
    grad_resid, grad_gain, grad_shift = norm_backward(
        narrow_grad(grad_act), scaled, inv_std, norm_gain
    )
    return (grad_resid, grad_gain, grad_shift, grad_up, grad_down)


def attn_forward(
    residual,
    norm_gain,
    norm_shift,
    attention_in,
    position_proj,
    position_bias,
    attention_out,
    lengths,
):
    normed, scaled, inv_std = norm_forward(residual, norm_gain, norm_shift)
    gathered = widen(normed)
    slot_count, slot_frames, model_width = gathered.shape
    flat_act = gathered.reshape(slot_count * slot_frames, model_width)
    head_count, head_size = (position_bias.shape[1], position_bias.shape[2])
    local_width = head_count * head_size
    projected = jnp.einsum(
        "fd,sdc->sfc", flat_act, attention_in, preferred_element_type=jnp.float32
    )
    biases = position_bias.astype(jnp.float32).reshape(2, 1, local_width)
    block_size = min(512, slot_frames)
    per_slot = slot_frames // block_size
    block_count = slot_count * per_slot
    shape_blocks = (block_count, block_size, head_count, head_size)
    shape_slots = (slot_count, slot_frames, head_count, head_size)
    query_content = (projected[0] + biases[0]).astype(jnp.bfloat16).reshape(shape_blocks)
    query_position = (projected[0] + biases[1]).astype(jnp.bfloat16).reshape(shape_blocks)
    key_all = projected[1].astype(jnp.bfloat16).reshape(shape_slots)
    value_all = projected[2].astype(jnp.bfloat16).reshape(shape_slots)
    table_in = relative_table(slot_frames, model_width).astype(jnp.bfloat16)
    table = (
        jnp.dot(table_in, position_proj, preferred_element_type=jnp.float32)
        .astype(jnp.bfloat16)
        .reshape(2 * slot_frames - 1, head_count, head_size)
    )

    def forward_block(block_index):
        slot_index = block_index // per_slot
        block_start = block_index % per_slot * block_size
        block_content = lax.dynamic_index_in_dim(query_content, block_index, 0, keepdims=False)
        block_position = lax.dynamic_index_in_dim(query_position, block_index, 0, keepdims=False)
        slot_keys = lax.dynamic_index_in_dim(key_all, slot_index, 0, keepdims=False)
        slot_values = lax.dynamic_index_in_dim(value_all, slot_index, 0, keepdims=False)
        length = lax.dynamic_index_in_dim(lengths, slot_index, 0, keepdims=False)
        scores, window = block_raw(
            block_content, block_position, slot_keys, table, block_start, length
        )
        row_top = jnp.max(scores, axis=-1, keepdims=True)
        log_total = row_top + jnp.log(jnp.sum(jnp.exp(scores - row_top), axis=-1, keepdims=True))
        probs_soft = jnp.exp(scores - log_total).astype(jnp.bfloat16)
        context = jnp.einsum(
            "hbk,khe->bhe", probs_soft, slot_values, preferred_element_type=jnp.float32
        )
        return (context, log_total)

    context_all, log_totals = lax.map(forward_block, jnp.arange(block_count, dtype=jnp.int32))
    context_round = context_all.reshape(slot_count * slot_frames, local_width).astype(jnp.bfloat16)
    partial_out = jnp.dot(context_round, attention_out, preferred_element_type=jnp.float32).reshape(
        slot_count, slot_frames, model_width
    )
    saved = (
        scaled,
        inv_std,
        flat_act,
        query_content,
        query_position,
        key_all,
        value_all,
        table_in,
        table,
        context_round,
        log_totals,
    )
    return (narrow(partial_out), saved)


def attn_backward(grad_after, saved, norm_gain, attention_in, attention_out, lengths):
    (
        scaled,
        inv_std,
        flat_act,
        query_content,
        query_position,
        key_all,
        value_all,
        table_in,
        table,
        context_round,
        log_totals,
    ) = saved
    grad_round = widen_grad(grad_after)
    slot_count, slot_frames, model_width = grad_round.shape
    frames = slot_count * slot_frames
    grad_flat = grad_round.reshape(frames, model_width)
    grad_back_proj = contract_rows(context_round, grad_flat)
    block_count, block_size, head_count, head_size = query_content.shape
    local_width = head_count * head_size
    per_slot = slot_frames // block_size
    score_scale = head_size ** (-0.5)
    grad_context = (
        times_transposed(grad_flat, attention_out).astype(jnp.bfloat16).reshape(query_content.shape)
    )
    zero_keys = jnp.zeros(key_all.shape, jnp.float32)
    zero_table = jnp.zeros(table.shape, jnp.float32)

    def backward_block(accum, block_index):
        grad_keys, grad_values, grad_table = accum
        slot_index = block_index // per_slot
        block_start = block_index % per_slot * block_size
        block_content = lax.dynamic_index_in_dim(query_content, block_index, 0, keepdims=False)
        block_position = lax.dynamic_index_in_dim(query_position, block_index, 0, keepdims=False)
        block_grad = lax.dynamic_index_in_dim(grad_context, block_index, 0, keepdims=False)
        block_log = lax.dynamic_index_in_dim(log_totals, block_index, 0, keepdims=False)
        slot_keys = lax.dynamic_index_in_dim(key_all, slot_index, 0, keepdims=False)
        slot_values = lax.dynamic_index_in_dim(value_all, slot_index, 0, keepdims=False)
        length = lax.dynamic_index_in_dim(lengths, slot_index, 0, keepdims=False)
        scores, window = block_raw(
            block_content, block_position, slot_keys, table, block_start, length
        )
        probs_soft = jnp.exp(scores - block_log)
        grad_probs = jnp.einsum(
            "bhe,khe->hbk", block_grad, slot_values, preferred_element_type=jnp.float32
        )
        delta_row = jnp.sum(probs_soft * grad_probs, axis=-1, keepdims=True)
        grad_raw = (probs_soft * (grad_probs - delta_row) * score_scale).astype(jnp.bfloat16)
        grad_content = jnp.einsum(
            "hbk,khe->bhe", grad_raw, slot_keys, preferred_element_type=jnp.float32
        )
        grad_wide = unskew(grad_raw, window.shape[0])
        grad_position = jnp.einsum(
            "hbw,whe->bhe", grad_wide, window, preferred_element_type=jnp.float32
        )
        key_part = jnp.einsum(
            "hbk,bhe->khe", grad_raw, block_content, preferred_element_type=jnp.float32
        )
        value_part = jnp.einsum(
            "hbk,bhe->khe",
            probs_soft.astype(jnp.bfloat16),
            block_grad,
            preferred_element_type=jnp.float32,
        )
        window_part = jnp.einsum(
            "hbw,bhe->whe", grad_wide, block_position, preferred_element_type=jnp.float32
        )
        grad_keys = lax.dynamic_update_index_in_dim(
            grad_keys,
            lax.dynamic_index_in_dim(grad_keys, slot_index, 0, keepdims=False) + key_part,
            slot_index,
            0,
        )
        grad_values = lax.dynamic_update_index_in_dim(
            grad_values,
            lax.dynamic_index_in_dim(grad_values, slot_index, 0, keepdims=False) + value_part,
            slot_index,
            0,
        )
        window_start = slot_frames - block_size - block_start
        grad_table = lax.dynamic_update_slice_in_dim(
            grad_table,
            lax.dynamic_slice_in_dim(grad_table, window_start, window.shape[0], 0) + window_part,
            window_start,
            0,
        )
        return ((grad_keys, grad_values, grad_table), (grad_content, grad_position))

    accum, query_grads = lax.scan(
        backward_block, (zero_keys, zero_keys, zero_table), jnp.arange(block_count, dtype=jnp.int32)
    )
    grad_content_all = query_grads[0].reshape(frames, local_width)
    grad_position_all = query_grads[1].reshape(frames, local_width)
    grad_bias = jnp.stack(
        [jnp.sum(grad_content_all, axis=0), jnp.sum(grad_position_all, axis=0)]
    ).reshape(2, head_count, head_size)
    grad_query = (grad_content_all + grad_position_all).astype(jnp.bfloat16)
    grad_proj = jnp.stack(
        [
            grad_query,
            accum[0].reshape(frames, local_width).astype(jnp.bfloat16),
            accum[1].reshape(frames, local_width).astype(jnp.bfloat16),
        ]
    )
    grad_in_proj = jnp.einsum(
        "fd,sfc->sdc", flat_act, grad_proj, preferred_element_type=jnp.float32
    )
    grad_act = jnp.einsum(
        "sfc,sdc->fd", grad_proj, attention_in, preferred_element_type=jnp.float32
    ).reshape(slot_count, slot_frames, model_width)
    grad_table_proj = contract_rows(
        table_in, accum[2].reshape(2 * slot_frames - 1, local_width).astype(jnp.bfloat16)
    )
    grad_resid, grad_gain, grad_shift = norm_backward(
        narrow_grad(grad_act), scaled, inv_std, norm_gain
    )
    return (
        grad_resid,
        grad_gain,
        grad_shift,
        grad_in_proj,
        grad_table_proj,
        grad_bias,
        grad_back_proj,
    )


def conv_forward(
    residual,
    norm_gain,
    norm_shift,
    pointwise_in,
    depthwise,
    batch_gain,
    batch_shift,
    pointwise_out,
    lengths,
    live_full,
):
    normed, scaled, inv_std = norm_forward(residual, norm_gain, norm_shift)
    gathered = widen(normed)
    slot_count, slot_frames, model_width = gathered.shape
    flat_act = gathered.reshape(slot_count * slot_frames, model_width)
    both_halves = jnp.einsum(
        "fd,dsc->sfc", flat_act, pointwise_in, preferred_element_type=jnp.float32
    )
    gate_sig = jax.nn.sigmoid(both_halves[1])
    gated = both_halves[0] * gate_sig * live_full
    channels = gated.shape[1]
    kernel = depthwise.astype(jnp.float32)
    tap_count = kernel.shape[0]
    half_taps = tap_count // 2
    padded = jnp.pad(
        gated.reshape(slot_count, slot_frames, channels), ((0, 0), (half_taps, half_taps), (0, 0))
    )
    mixed_conv = padded[:, 0:slot_frames, :] * kernel[0]
    for tap_index in range(1, tap_count):
        mixed_conv = (
            mixed_conv + padded[:, tap_index : tap_index + slot_frames, :] * kernel[tap_index]
        )
    mixed_conv = mixed_conv.reshape(slot_count * slot_frames, channels)
    totals = lax.psum(
        (
            jnp.sum(mixed_conv * live_full, axis=0),
            jnp.sum(mixed_conv * mixed_conv * live_full, axis=0),
            jnp.sum(lengths).astype(jnp.float32),
        ),
        "batch",
    )
    frame_count = totals[2]
    batch_mean = totals[0] / frame_count
    batch_inv = lax.rsqrt(totals[1] / frame_count - batch_mean * batch_mean + eps_batch)
    centered = (mixed_conv - batch_mean) * batch_inv
    normed_batch = centered * batch_gain.astype(jnp.float32) + batch_shift.astype(jnp.float32)
    batch_sig = jax.nn.sigmoid(normed_batch)
    swished = (normed_batch * batch_sig).astype(jnp.bfloat16)
    partial_out = jnp.dot(swished, pointwise_out, preferred_element_type=jnp.float32).reshape(
        slot_count, slot_frames, model_width
    )
    saved = (
        scaled,
        inv_std,
        flat_act,
        both_halves,
        gate_sig,
        padded,
        centered,
        batch_inv,
        frame_count,
        normed_batch,
        batch_sig,
        swished,
    )
    return (narrow(partial_out), saved)


def conv_backward(
    grad_after, saved, norm_gain, pointwise_in, depthwise, batch_gain, pointwise_out, live_full
):
    (
        scaled,
        inv_std,
        flat_act,
        both_halves,
        gate_sig,
        padded,
        centered,
        batch_inv,
        frame_count,
        normed_batch,
        batch_sig,
        swished,
    ) = saved
    grad_round = widen_grad(grad_after)
    slot_count, slot_frames, model_width = grad_round.shape
    grad_flat = grad_round.reshape(slot_count * slot_frames, model_width)
    grad_point_out = contract_rows(swished, grad_flat)
    grad_swished = times_transposed(grad_flat, pointwise_out)
    grad_normed = grad_swished * batch_sig * (1.0 + normed_batch * (1.0 - batch_sig))
    sums = lax.psum(
        (jnp.sum(grad_normed, axis=0), jnp.sum(grad_normed * centered, axis=0)), "batch"
    )
    gamma = batch_gain.astype(jnp.float32)
    grad_mixed = batch_inv * (
        grad_normed * gamma
        - live_full * (gamma * sums[0] + centered * gamma * sums[1]) / frame_count
    )
    channels = grad_mixed.shape[1]
    kernel = depthwise.astype(jnp.float32)
    tap_count = kernel.shape[0]
    half_taps = tap_count // 2
    grad_mixed3 = grad_mixed.reshape(slot_count, slot_frames, channels)
    grad_kernel = jnp.stack(
        [
            jnp.sum(grad_mixed3 * padded[:, tap_index : tap_index + slot_frames, :], axis=(0, 1))
            for tap_index in range(tap_count)
        ]
    )
    spread = jnp.pad(grad_mixed3, ((0, 0), (half_taps, half_taps), (0, 0)))
    grad_gated = spread[:, 2 * half_taps : 2 * half_taps + slot_frames, :] * kernel[0]
    for tap_index in range(1, tap_count):
        begin = 2 * half_taps - tap_index
        grad_gated = grad_gated + spread[:, begin : begin + slot_frames, :] * kernel[tap_index]
    grad_gated = grad_gated.reshape(slot_count * slot_frames, channels) * live_full
    grad_halves = jnp.stack(
        [grad_gated * gate_sig, grad_gated * both_halves[0] * gate_sig * (1.0 - gate_sig)]
    ).astype(jnp.bfloat16)
    grad_point_in = jnp.einsum(
        "fd,sfc->dsc", flat_act, grad_halves, preferred_element_type=jnp.float32
    )
    grad_act = jnp.einsum(
        "sfc,dsc->fd", grad_halves, pointwise_in, preferred_element_type=jnp.float32
    ).reshape(slot_count, slot_frames, model_width)
    grad_resid, grad_gain, grad_shift = norm_backward(
        narrow_grad(grad_act), scaled, inv_std, norm_gain
    )
    return (grad_resid, grad_gain, grad_shift, grad_point_in, grad_point_out, grad_kernel, sums)


def per_device(
    features,
    lengths,
    norm_gains,
    norm_shifts,
    first_up,
    first_down,
    attention_in,
    position_proj,
    position_bias,
    attention_out,
    pointwise_in,
    depthwise,
    batch_gain,
    batch_shift,
    pointwise_out,
    second_up,
    second_down,
    cotangent,
):
    slot_count, half_frames, model_width = features.shape
    slot_frames = half_frames * lax.axis_size("tensor")
    positions = (
        lax.broadcasted_iota(jnp.int32, (slot_count, half_frames), 1)
        + lax.axis_index("tensor") * half_frames
    )
    live_half = (positions < lengths[:, None]).astype(jnp.float32)[:, :, None]
    full_positions = lax.broadcasted_iota(jnp.int32, (slot_count, slot_frames), 1)
    live_full = (
        (full_positions < lengths[:, None]).astype(jnp.float32).reshape(slot_count * slot_frames, 1)
    )
    gain_rows = norm_gains.astype(jnp.float32)
    shift_rows = norm_shifts.astype(jnp.float32)
    stream_zero = features.astype(jnp.float32)
    branch_one, saved_one = ffn_forward(
        stream_zero, gain_rows[0], shift_rows[0], first_up, first_down
    )
    stream_one = stream_zero + 0.5 * branch_one
    branch_two, saved_two = attn_forward(
        stream_one,
        gain_rows[1],
        shift_rows[1],
        attention_in,
        position_proj,
        position_bias,
        attention_out,
        lengths,
    )
    stream_two = stream_one + branch_two
    branch_three, saved_three = conv_forward(
        stream_two,
        gain_rows[2],
        shift_rows[2],
        pointwise_in,
        depthwise,
        batch_gain,
        batch_shift,
        pointwise_out,
        lengths,
        live_full,
    )
    stream_three = stream_two + branch_three
    branch_four, saved_four = ffn_forward(
        stream_three, gain_rows[3], shift_rows[3], second_up, second_down
    )
    stream_four = stream_three + 0.5 * branch_four
    final_norm, scaled_final, inv_final = norm_forward(stream_four, gain_rows[4], shift_rows[4])
    output = (final_norm * live_half).astype(jnp.bfloat16)
    grad_final = cotangent.astype(jnp.float32) * live_half
    grad_stream, gain_five, shift_five = norm_backward(
        grad_final, scaled_final, inv_final, gain_rows[4]
    )
    grad_branch, gain_four, shift_four, up_two, down_two = ffn_backward(
        0.5 * grad_stream, saved_four, gain_rows[3], second_up, second_down
    )
    grad_stream = grad_stream + grad_branch
    grad_branch, gain_three, shift_three, point_in_grad, point_out_grad, kernel_grad, batch_sums = (
        conv_backward(
            grad_stream,
            saved_three,
            gain_rows[2],
            pointwise_in,
            depthwise,
            batch_gain,
            pointwise_out,
            live_full,
        )
    )
    grad_stream = grad_stream + grad_branch
    grad_branch, gain_two, shift_two, heads_grad, table_grad, bias_grad, back_grad = attn_backward(
        grad_stream, saved_two, gain_rows[1], attention_in, attention_out, lengths
    )
    grad_stream = grad_stream + grad_branch
    grad_branch, gain_one, shift_one, up_one, down_one = ffn_backward(
        0.5 * grad_stream, saved_one, gain_rows[0], first_up, first_down
    )
    (
        up_one,
        down_one,
        heads_grad,
        table_grad,
        back_grad,
        point_in_grad,
        point_out_grad,
        up_two,
        down_two,
    ) = (
        lax.psum_scatter(up_one, "batch", scatter_dimension=0, tiled=True),
        lax.psum_scatter(down_one, "batch", scatter_dimension=1, tiled=True),
        lax.psum_scatter(heads_grad, "batch", scatter_dimension=1, tiled=True),
        lax.psum_scatter(table_grad, "batch", scatter_dimension=0, tiled=True),
        lax.psum_scatter(back_grad, "batch", scatter_dimension=1, tiled=True),
        lax.psum_scatter(point_in_grad, "batch", scatter_dimension=0, tiled=True),
        lax.psum_scatter(point_out_grad, "batch", scatter_dimension=1, tiled=True),
        lax.psum_scatter(up_two, "batch", scatter_dimension=0, tiled=True),
        lax.psum_scatter(down_two, "batch", scatter_dimension=1, tiled=True),
    )
    grad_stream = grad_stream + grad_branch
    gain_grads = jnp.stack([gain_one, gain_two, gain_three, gain_four, gain_five])
    shift_grads = jnp.stack([shift_one, shift_two, shift_three, shift_four, shift_five])
    gain_grads, shift_grads = lax.psum((gain_grads, shift_grads), ("batch", "tensor"))
    bias_grad, kernel_grad = lax.psum((bias_grad, kernel_grad), "batch")
    return (
        output,
        grad_stream,
        gain_grads,
        shift_grads,
        up_one,
        down_one,
        heads_grad,
        table_grad,
        bias_grad,
        back_grad,
        point_in_grad,
        kernel_grad,
        batch_sums[1],
        batch_sums[0],
        point_out_grad,
        up_two,
        down_two,
    )


def solution(mesh):
    in_specs = (
        P("batch", "tensor", None),
        P("batch"),
        P(),
        P(),
        P(None, "tensor"),
        P("tensor", None),
        P(None, None, "tensor"),
        P(None, "tensor"),
        P(None, "tensor", None),
        P("tensor", None),
        P(None, None, "tensor"),
        P(None, "tensor"),
        P("tensor"),
        P("tensor"),
        P("tensor", None),
        P(None, "tensor"),
        P("tensor", None),
        P("batch", "tensor", None),
    )
    out_specs = (
        P("batch", "tensor", None),
        P("batch", "tensor", None),
        P(),
        P(),
        P("batch", "tensor"),
        P("tensor", "batch"),
        P(None, "batch", "tensor"),
        P("batch", "tensor"),
        P(None, "tensor", None),
        P("tensor", "batch"),
        P("batch", None, "tensor"),
        P(None, "tensor"),
        P("tensor"),
        P("tensor"),
        P("tensor", "batch"),
        P("batch", "tensor"),
        P("tensor", "batch"),
    )
    return jax.shard_map(
        per_device, mesh=mesh, in_specs=in_specs, out_specs=out_specs, check_vma=False
    )
```

profile of v0, /device:TPU:0, one launch (start us, length us, event | category | flops | bytes accessed | tf_op | source)
XLA Modules:
  0.0 2585.9 jit_solution(7235221445657931016)
XLA Ops:
  59.4 121.7 %multiply_sine_fusion = (bf16[2047,512,1]{0,2,1:T(2,128)(2,1)}, bf16[2047,512,1]{0,2,1:T(2,128)(2,1)}) fusion(f32[2047]{0:T(1024)S(1)} %subtract_convert_fusion, f32[512]{0:T(512)S(1)} %multiply_exponential_fusion), kind=kLoop, calls=%fused_computation.78 | loop fusion | flops 3144192 | bytes 4202492 | tf_op jit(solution)/shard_map/sin | solution.py:66
  238.8 208.9 %while.36 = (s32[]{:T(128)}, bf16[2,512,4,128]{3,1,2,0:T(8,128)(2,1)}, f32[2,4,512,1]{2,1,3,0:T(4,128)S(1)}, s32[1]{0:T(128)}, s32[2]{0:T(128)S(1)}, /*index=5*/...) while((s32[]{:T(128)}, ...), condition=%wide.region_8.9_spmd.clone, body=%wide.region_5.8_spmd.sunk.clone | while | flops 1895300096 | bytes 190245280 | solution.py:189
  266.3 18.9 reshape.782
  285.2 14.9 reshape.783
  313.5 14.0 reshape.784
  363.0 18.9 reshape.782
  381.9 14.9 reshape.783
  410.2 14.0 reshape.784
  491.4 42.9 %all-reduce.8 = (f32[512]{0:T(512)S(1)}, f32[]{:T(128)}, f32[512]{0:T(512)S(1)}) all-reduce(f32[512]{0:T(512)S(1)} %get-tuple-element.485, f32[]{:T(128)S(6)} %convert_element_type.340, f32[512]{0:T(512)S(1)} %get-tuple-element.484), channel_id=1, replica_groups=mesh['batch'=16,'tensor'=2] {'batch'}, use_global_device_ids=true, to_apply=%region_16.17 | all-reduce | flops 1025 | bytes 8200 | tf_op jit(solution)/shard_map/psum | solution.py:372
  666.2 42.0 %all-reduce.7 = (f32[512]{0:T(512)S(1)}, f32[512]{0:T(512)S(1)}) all-reduce(f32[512]{0:T(512)S(1)} %get-tuple-element.487, f32[512]{0:T(512)S(1)} %get-tuple-element.486), channel_id=1, replica_groups=mesh['batch'=16,'tensor'=2] {'batch'}, use_global_device_ids=true, to_apply=%region_31.32 | all-reduce | flops 1024 | bytes 8192 | tf_op jit(solution)/shard_map/psum | solution.py:430
  761.3 413.0 %while.37 = (s32[]{:T(128)}, f32[1,1024,4,128]{1,3,2,0:T(8,128)}, f32[1,1024,4,128]{1,3,2,0:T(8,128)}, f32[2047,4,128]{0,2,1:T(8,128)}, f32[2,512,4,128]{3,1,2,0...) while((s32[]{:T(128)}, f32[1,1024,4,128]{1,3,2,0:T(8,128)}, ...), condition=%wide.region_37.38_spmd.clone, body=%wide.region_35.37_spmd.sunk.clone | while | flops 5658381824 | bytes 389863968 | solution.py:299
  775.9 18.8 reshape.786
  794.8 14.9 reshape.787
  823.2 14.1 reshape.788
  922.7 13.9 reshape.793
  948.3 15.0 dynamic_update_slice.53
  977.9 18.8 reshape.786
  996.8 14.9 reshape.787
  1011.7 13.7 slice.284
  1025.4 14.1 reshape.788
  1124.7 13.9 reshape.793
  1150.4 15.5 dynamic_update_slice.53
  1332.9 81.5 %all-reduce.6 = (f32[2,4,128]{2,1,0:T(4,128)}, f32[5,512]{1,0:T(8,128)}) all-reduce(f32[2,4,128]{2,1,0:T(4,128)S(1)} %pad_maximum_fusion.6, f32[5,512]{1,0:T(8,128)S(1)} %stack.103), channel_id=1, replica_groups=mesh['batch'=16,'tensor'=2] {'batch'}, use_global_device_ids=true, to_apply=%region_62.63 | all-reduce | flops 3584 | bytes 28672 | tf_op jit(solution)/shard_map/psum | solution.py:591
  1416.3 177.1 %all-reduce.11.cloned.1.call-done = f32[3,1024,512]{2,0,1:T(4,128)} async-done(((f32[3,1024,512]{2,0,1:T(4,128)}), f32[3,1024,512]{2,0,1:T(4,128)}) %all-reduce.11.cloned.1.call-update) | async-done | bytes 6291472
  1607.0 42.5 %all-reduce.5 = (f32[5,1024]{1,0:T(8,128)}, f32[5,1024]{1,0:T(8,128)}) all-reduce(f32[5,1024]{1,0:T(8,128)S(1)} %stack.88, f32[5,1024]{1,0:T(8,128)S(1)} %stack.94), channel_id=1, replica_groups=mesh['batch'=16,'tensor'=2] {'batch','tensor'}, use_global_device_ids=true, to_apply=%region_49.50 | all-reduce | flops 10240 | bytes 81920 | tf_op jit(solution)/shard_map/psum | solution.py:590
  1653.8 36.4 %reduce-scatter.43.cloned.1.call-done = f32[512,64]{0,1:T(8,128)} async-done(((f32[512,1024]{0,1:T(8,128)}), f32[512,64]{0,1:T(8,128)}) %reduce-scatter.43.cloned.1.call-update) | async-done | bytes 131088 | tf_op jit(solution)/shard_map/reduce_scatter | solution.py:583
  1690.2 81.1 %reduce-scatter.39.cloned.1.call-done = f32[512,64]{0,1:T(8,128)} async-done(((f32[512,1024]{0,1:T(8,128)}), f32[512,64]{0,1:T(8,128)}) %reduce-scatter.39.cloned.1.call-update) | async-done | bytes 131088 | tf_op jit(solution)/shard_map/reduce_scatter | solution.py:581
  1771.3 81.1 %reduce-scatter.37.cloned.1.call-done = f32[64,512]{1,0:T(8,128)} async-done(((f32[1024,512]{1,0:T(8,128)}), f32[64,512]{1,0:T(8,128)}) %reduce-scatter.37.cloned.1.call-update) | async-done | bytes 131088 | tf_op jit(solution)/shard_map/reduce_scatter | solution.py:580
  1852.4 177.4 %reduce-scatter.47.cloned.1.call-done = f32[2048,64]{0,1:T(8,128)} async-done(((f32[2048,1024]{0,1:T(8,128)}), f32[2048,64]{0,1:T(8,128)}) %reduce-scatter.47.cloned.1.call-update) | async-done | bytes 524304 | tf_op jit(solution)/shard_map/reduce_scatter | solution.py:585
  2029.8 183.2 %reduce-scatter.45.cloned.1.call-done = f32[64,2048]{1,0:T(8,128)} async-done(((f32[1024,2048]{1,0:T(8,128)}), f32[64,2048]{1,0:T(8,128)}) %reduce-scatter.45.cloned.1.call-update) | async-done | bytes 524304 | tf_op jit(solution)/shard_map/reduce_scatter | solution.py:584
  2213.0 183.1 %reduce-scatter.35.cloned.1.call-done = f32[2048,64]{0,1:T(8,128)} async-done(((f32[2048,1024]{0,1:T(8,128)}), f32[2048,64]{0,1:T(8,128)}) %reduce-scatter.35.cloned.1.call-update) | async-done | bytes 524304 | tf_op jit(solution)/shard_map/reduce_scatter | solution.py:578
  2396.0 183.2 %reduce-scatter.33.cloned.1.call-done = f32[64,2048]{1,0:T(8,128)} async-done(((f32[1024,2048]{1,0:T(8,128)}), f32[64,2048]{1,0:T(8,128)}) %reduce-scatter.33.cloned.1.call-update) | async-done | bytes 524304 | tf_op jit(solution)/shard_map/reduce_scatter | solution.py:577
  (445 shorter events, 835.4 us)
Async XLA Ops:
  7.2 203.9 %copy-start = (bf16[3,1024,512]{2,1,0:T(8,128)(2,1)S(1)}, bf16[3,1024,512]{2,1,0:T(8,128)(2,1)}, u32[]{:S(2)}) copy-start(bf16[3,1024,512]{2,1,0:T(8,128)(2,1)} %param.28) | copy-start | bytes 9437188
  7.2 19.5 all-gather.9.cloned.1.call-start
  13.3 40.7 %reduce-scatter.17.cloned.1.call-start = ((), (), s32[]{:S(2)}) async-start(), calls=%async_computation.17 | async-start | bytes 3145728 | tf_op jit(solution)/shard_map/reduce_scatter | solution.py:46
  42.9 168.2 %all-gather.11.cloned.1.call-start = ((), (), s32[]{:S(2)}) async-start(), calls=%async_computation.18 | async-start | bytes 3145728 | tf_op jit(solution)/shard_map/all_gather | solution.py:42
  58.9 405.8 %reduce-scatter.19.cloned.1.call-start = ((), (), s32[]{:S(2)}) async-start(), calls=%async_computation.19 | async-start | bytes 3145728 | tf_op jit(solution)/shard_map/reduce_scatter | solution.py:46
  453.5 28.3 %all-gather.13.cloned.1.call-start = ((), (), s32[]{:S(2)}) async-start(), calls=%async_computation.20 | async-start | bytes 3145728 | tf_op jit(solution)/shard_map/all_gather | solution.py:42
  469.8 75.7 %reduce-scatter.21.cloned.1.call-start = ((), (), s32[]{:S(2)}) async-start(), calls=%async_computation.21 | async-start | bytes 3145728 | tf_op jit(solution)/shard_map/reduce_scatter | solution.py:46
  470.6 237.6 %copy-start.68 = (f32[512]{0:T(512)}, f32[512]{0:T(512)S(1)}, u32[]{:S(2)}) copy-start(f32[512]{0:T(512)S(1)} %convert_element_type.341) | copy-start | bytes 6148
  539.7 22.7 all-gather.15.cloned.1.call-start
  550.4 39.4 %reduce-scatter.23.cloned.1.call-start = ((), (), s32[]{:S(2)}) async-start(), calls=%async_computation.23 | async-start | bytes 3145728 | tf_op jit(solution)/shard_map/reduce_scatter | solution.py:46
  578.7 30.6 %all-gather.17.cloned.1.call-start = ((), (), s32[]{:S(2)}) async-start(), calls=%async_computation.24 | async-start | bytes 3145728 | tf_op jit(solution)/shard_map/all_gather | solution.py:52
  597.3 42.7 %reduce-scatter.25.cloned.1.call-start = ((), (), s32[]{:S(2)}) async-start(), calls=%async_computation.25 | async-start | bytes 3145728 | tf_op jit(solution)/shard_map/reduce_scatter | solution.py:56
  628.9 31.3 %all-gather.19.cloned.1.call-start = ((), (), s32[]{:S(2)}) async-start(), calls=%async_computation.26 | async-start | bytes 3145728 | tf_op jit(solution)/shard_map/all_gather | solution.py:52
  648.2 81.5 %reduce-scatter.27.cloned.1.call-start = ((), (), s32[]{:S(2)}) async-start(), calls=%async_computation.27 | async-start | bytes 3145728 | tf_op jit(solution)/shard_map/reduce_scatter | solution.py:56
  724.0 25.4 all-gather.21.cloned.1.call-start
  737.4 475.5 %reduce-scatter.29.cloned.1.call-start = ((), (), s32[]{:S(2)}) async-start(), calls=%async_computation.29 | async-start | bytes 3145728 | tf_op jit(solution)/shard_map/reduce_scatter | solution.py:56
  1201.8 44.3 %all-gather.23.cloned.1.call-start = ((), (), s32[]{:S(2)}) async-start(), calls=%async_computation.30 | async-start | bytes 3145728 | tf_op jit(solution)/shard_map/all_gather | solution.py:52
  1220.5 193.9 %reduce-scatter.41.cloned.1.call-start = ((), (), s32[]{:S(2)}) async-start(), calls=%async_computation.36 | async-start | bytes 4456448 | tf_op jit(solution)/shard_map/reduce_scatter | solution.py:582
  1227.2 366.2 %all-reduce.11.cloned.1.call-start = ((), (), s32[]{:S(2)}) async-start(), calls=%async_computation.40 | async-start | bytes 16777216
  1245.8 358.4 %reduce-scatter.31.cloned.1.call-start = ((), (), s32[]{:S(2)}) async-start(), calls=%async_computation.31 | async-start | bytes 3145728 | tf_op jit(solution)/shard_map/reduce_scatter | solution.py:56
  1265.4 424.8 %reduce-scatter.43.cloned.1.call-start = ((), (), s32[]{:S(2)}) async-start(), calls=%async_computation.37 | async-start | bytes 2228224 | tf_op jit(solution)/shard_map/reduce_scatter | solution.py:583
  1271.1 500.2 %reduce-scatter.39.cloned.1.call-start = ((), (), s32[]{:S(2)}) async-start(), calls=%async_computation.35 | async-start | bytes 2228224 | tf_op jit(solution)/shard_map/reduce_scatter | solution.py:581
  1275.7 576.6 %reduce-scatter.37.cloned.1.call-start = ((), (), s32[]{:S(2)}) async-start(), calls=%async_computation.34 | async-start | bytes 2228224 | tf_op jit(solution)/shard_map/reduce_scatter | solution.py:580
  1283.4 746.3 %reduce-scatter.47.cloned.1.call-start = ((), (), s32[]{:S(2)}) async-start(), calls=%async_computation.39 | async-start | bytes 8912896 | tf_op jit(solution)/shard_map/reduce_scatter | solution.py:585
  1295.5 917.5 %reduce-scatter.45.cloned.1.call-start = ((), (), s32[]{:S(2)}) async-start(), calls=%async_computation.38 | async-start | bytes 8912896 | tf_op jit(solution)/shard_map/reduce_scatter | solution.py:584
  1306.3 1089.8 %reduce-scatter.35.cloned.1.call-start = ((), (), s32[]{:S(2)}) async-start(), calls=%async_computation.33 | async-start | bytes 8912896 | tf_op jit(solution)/shard_map/reduce_scatter | solution.py:578
  1318.4 1260.8 %reduce-scatter.33.cloned.1.call-start = ((), (), s32[]{:S(2)}) async-start(), calls=%async_computation.32 | async-start | bytes 8912896 | tf_op jit(solution)/shard_map/reduce_scatter | solution.py:577
  1331.1 273.2 %copy-start.38 = (f32[1,1024]{1,0:T(1,128)S(1)}, f32[1,1024]{1,0:T(1,128)}, u32[]{:S(2)}) copy-start(f32[1,1024]{1,0:T(1,128)} %copy-done.37) | copy-start | bytes 12292
  1331.1 273.2 %copy-start.43 = (f32[512]{0:T(512)S(1)}, f32[512]{0:T(512)}, u32[]{:S(2)}) copy-start(f32[512]{0:T(512)} %copy-done.42) | copy-start | bytes 6148
  1331.1 273.2 %copy-start.47 = (f32[512]{0:T(512)S(1)}, f32[512]{0:T(512)}, u32[]{:S(2)}) copy-start(f32[512]{0:T(512)} %copy-done.46) | copy-start | bytes 6148
  1416.3 190.7 %copy-start.55 = (f32[1024]{0:T(1024)S(1)}, f32[1024]{0:T(1024)}, u32[]{:S(2)}) copy-start(f32[1024]{0:T(1024)} %get-tuple-element.494) | copy-start | bytes 12292
  1416.3 190.7 %copy-start.57 = (f32[1024]{0:T(1024)S(1)}, f32[1024]{0:T(1024)}, u32[]{:S(2)}) copy-start(f32[1024]{0:T(1024)} %get-tuple-element.495) | copy-start | bytes 12292
  (91 other events, 1775.6 us)
Sparse Core Ops, SparseCore 0:
  13.4 13.2 all-gather.8
  43.0 10.9 reduce-scatter.16
  59.0 11.8 all-gather.10
  453.7 10.9 reduce-scatter.18
  470.0 11.8 all-gather.12
  539.9 5.6 reduce-scatter.20
  550.5 11.8 all-gather.14
  578.8 10.9 reduce-scatter.22
  597.4 11.8 all-gather.16
  629.0 10.9 reduce-scatter.24
  648.3 11.8 all-gather.18
  724.1 5.6 reduce-scatter.26
  737.5 11.8 all-gather.20
  1201.9 10.9 reduce-scatter.28
  1220.6 11.8 all-gather.22
  1234.6 96.3 reduce-scatter.40
  1336.9 256.4 all-reduce.10
  1595.5 8.7 reduce-scatter.30
  1607.1 83.0 reduce-scatter.42
  1692.9 78.3 reduce-scatter.38
  1774.1 78.1 reduce-scatter.36
  1855.2 174.5 reduce-scatter.46
  2032.7 180.2 reduce-scatter.44
  2215.7 180.2 reduce-scatter.34
  2398.9 180.2 reduce-scatter.32
where the time goes:
time: 2600 us; the launch traced here: 2590 us
  waiting for transfers between devices  1250 us (48%)
  local copies, waits for them, and re-layouts  537 us (21%)
  matrix products  308 us (12%)
  other arithmetic  225 us (9%)
  blocking collectives  209 us (8%)
  loops' own time  37.5 us (1%)
    reduce_scatter x1, waiting for transfers between devices, per_device(): lax.psum_scatter(up_one, 'batch', scatter_dimension=0, tiled=True)  183 us
    reduce_scatter x1, waiting for transfers between devices, per_device(): lax.psum_scatter(up_two, 'batch', scatter_dimension=0, tiled=True)  183 us
    reduce_scatter x1, waiting for transfers between devices, per_device(): lax.psum_scatter(down_one, 'batch', scatter_dimension=1, tiled=True)  183 us
    while x48, local copies, waits for them, and re-layouts  180 us
    unnamed x26, waiting for transfers between devices  177 us
    reduce_scatter x1, waiting for transfers between devices, per_device(): lax.psum_scatter(down_two, 'batch', scatter_dimension=1, tiled=True)  177 us
    sin x1, other arithmetic, relative_table(): jnp.sin(angles)  122 us
    psum x1, blocking collectives, per_device(): bias_grad, kernel_grad = lax.psum((bias_grad, kernel_grad), 'batch')  81.5 us
  transfers between devices with their start and end apart: 25, of which 22 were waited for; matrix products, arithmetic and copies ran while one was open for 10% of the time, Pallas kernels for 0%

commit v1 on v0

--- a/solution.py
+++ b/solution.py
@@ -1,8 +1,12 @@
+import functools
 import math
 
 import jax
 import jax.numpy as jnp
+import numpy as np
 from jax import lax
+from jax.experimental import pallas as pl
+from jax.experimental.pallas import tpu as pltpu
 from jax.sharding import PartitionSpec as P
 
 eps_norm = 1e-05
@@ -58,47 +62,116 @@
     ).astype(jnp.float32)
 
 
+def scatter_batch(grad, dimension):
+    return lax.psum_scatter(
+        grad.astype(jnp.bfloat16), "batch", scatter_dimension=dimension, tiled=True
+    ).astype(jnp.float32)
+
+
 def relative_table(slot_frames, model_width):
-    offsets = (slot_frames - 1 - jnp.arange(2 * slot_frames - 1)).astype(jnp.float32)
-    column = jnp.arange(model_width // 2).astype(jnp.float32)
-    freqs = jnp.exp(column * (-2.0 * math.log(10000.0) / model_width))
-    angles = offsets[:, None] * freqs[None, :]
-    return jnp.stack([jnp.sin(angles), jnp.cos(angles)], axis=-1).reshape(
-        2 * slot_frames - 1, model_width
-    )
-
-
-def skew(wide, slot_frames):
-    head_count, block_size, window_len = wide.shape
-    flat_wide = wide.reshape(head_count, block_size * window_len)
-    flat_wide = lax.slice_in_dim(
-        flat_wide, block_size - 1, block_size - 1 + block_size * (window_len - 1), axis=1
-    )
-    return flat_wide.reshape(head_count, block_size, window_len - 1)[:, :, :slot_frames]
-
-
-def unskew(grad_raw, window_len):
-    head_count, block_size, slot_frames = grad_raw.shape
-    padded = jnp.pad(grad_raw, ((0, 0), (0, 0), (0, window_len - 1 - slot_frames)))
-    flat_grad = padded.reshape(head_count, block_size * (window_len - 1))
-    flat_grad = jnp.pad(flat_grad, ((0, 0), (block_size - 1, 1)))
-    return flat_grad.reshape(head_count, block_size, window_len)
-
-
-def block_raw(block_content, block_position, slot_keys, table, block_start, length):
-    block_size = block_content.shape[0]
-    slot_frames = slot_keys.shape[0]
-    window = lax.dynamic_slice_in_dim(
-        table, slot_frames - block_size - block_start, block_size + slot_frames - 1, 0
-    )
-    content = jnp.einsum(
-        "bhe,khe->hbk", block_content, slot_keys, preferred_element_type=jnp.float32
-    )
-    wide = jnp.einsum("bhe,whe->hbw", block_position, window, preferred_element_type=jnp.float32)
-    raw = content + skew(wide, slot_frames)
-    live_keys = lax.broadcasted_iota(jnp.int32, (1, 1, slot_frames), 2) < length
-    scores = jnp.where(live_keys, raw * block_content.shape[2] ** (-0.5), -jnp.inf)
-    return (scores, window)
+    step = min(32, slot_frames)
+    column = np.arange(model_width)
+    freqs = np.exp((column // 2) * (-2.0 * math.log(10000.0) / model_width))
+    coarse = (slot_frames - 1 - step * np.arange(2 * slot_frames // step))[:, None] * freqs + (column % 2) * (
+        np.pi / 2
+    )
+    fine = np.arange(step)[:, None] * freqs
+    parts = [jnp.asarray(part, jnp.float32) for part in (np.sin(coarse), np.cos(coarse), np.cos(fine), np.sin(fine))]
+    table = parts[0][:, None, :] * parts[2][None] - parts[1][:, None, :] * parts[3][None]
+    return table.reshape(2 * slot_frames, model_width).astype(jnp.bfloat16)
+
+
+def dot_nn(a, b):
+    return lax.dot_general(a, b, (((1,), (0,)), ((), ())), preferred_element_type=jnp.float32)
+def dot_nt(a, b):
+    return lax.dot_general(a, b, (((1,), (1,)), ((), ())), preferred_element_type=jnp.float32)
+def dot_tn(a, b):
+    return lax.dot_general(a, b, (((0,), (0,)), ((), ())), preferred_element_type=jnp.float32)
+
+def flip_rows(x):
+    order = 7 - lax.broadcasted_iota(jnp.int32, (8, x.shape[1]), 0)
+    return jnp.concatenate(
+        [jnp.take_along_axis(x[at : at + 8], order, axis=0) for at in range(x.shape[0] - 8, -8, -8)], axis=0)
+
+def attend_kernel(frames, block, lengths, content, position, keys, values, table, context, probs):
+    wide_len = frames + block
+    start = pl.multiple_of(frames - block - pl.program_id(1) * block, block)
+    window = table[pl.ds(start, wide_len), :]
+    wide = dot_nt(position[...], window)
+    skewed = pltpu.roll(wide, frames + 1, 1, stride=1, stride_axis=0)[:, :frames]
+    raw = (dot_nt(content[...], keys[...]) + skewed) * (content.shape[1] ** -0.5)
+    live = lax.broadcasted_iota(jnp.int32, (1, frames), 1) < lengths[0]
+    scores = jnp.where(live, raw, -jnp.inf)
+    weight = jnp.exp(scores - jnp.max(scores, axis=1, keepdims=True))
+    soft = (weight / jnp.sum(weight, axis=1, keepdims=True)).astype(jnp.bfloat16)
+    probs[0] = soft
+    context[...] = dot_nn(soft, values[...]).astype(jnp.bfloat16)
+
+def attend(lengths, content, position, keys, values, table, head, block):
+    frames, width = content.shape
+    heads = width // head
+    rows = pl.BlockSpec((block, head), lambda h, i, *_: (i, h))
+    whole = pl.BlockSpec((frames, head), lambda h, i, *_: (0, h))
+    return pl.pallas_call(
+        functools.partial(attend_kernel, frames, block),
+        out_shape=(jax.ShapeDtypeStruct((frames, width), jnp.bfloat16), jax.ShapeDtypeStruct((heads, frames, frames), jnp.bfloat16)),
+        grid_spec=pltpu.PrefetchScalarGridSpec(
+            num_scalar_prefetch=1, grid=(heads, frames // block),
+            in_specs=[rows, rows, whole, whole, pl.BlockSpec((2 * frames, head), lambda h, i, *_: (0, h))],
+            out_specs=[rows, pl.BlockSpec((1, block, frames), lambda h, i, *_: (h, i, 0))]),
+        name="attend",
+    )(lengths, content, position, keys, values, table)
+
+def attend_back_kernel(frames, block, probs, grad_context, content, position, keys, values, table, grad_query, grad_keys, grad_values, grad_table, grad_bias, key_sum, value_sum, table_sum):
+    wide_len = frames + block
+    step = pl.program_id(1)
+    start = pl.multiple_of(frames - block - step * block, block)
+    @pl.when(step == 0)
+    def _():
+        key_sum[...] = jnp.zeros_like(key_sum)
+        value_sum[...] = jnp.zeros_like(value_sum)
+        table_sum[...] = jnp.zeros_like(table_sum)
+        grad_bias[...] = jnp.zeros_like(grad_bias)
+    soft = probs[0]
+    grad_out = grad_context[...]
+    grad_probs = dot_nt(grad_out, values[...])
+    wide_soft = soft.astype(jnp.float32)
+    delta = jnp.sum(wide_soft * grad_probs, axis=1, keepdims=True)
+    grad_raw = wide_soft * (grad_probs - delta) * (content.shape[1] ** -0.5)
+    padded = jnp.concatenate([flip_rows(grad_raw), jnp.zeros((block, block), jnp.float32)], axis=1)
+    grad_wide = pltpu.roll(padded, 0, 1, stride=1, stride_axis=0).astype(jnp.bfloat16)
+    grad_raw = grad_raw.astype(jnp.bfloat16)
+    from_content = dot_nn(grad_raw, keys[...])
+    from_position = dot_nn(grad_wide, table[pl.ds(start, wide_len), :])
+    from_position = flip_rows(from_position)
+    grad_query[...] = (from_content + from_position).astype(jnp.bfloat16)
+    grad_bias[0:1, :] += jnp.sum(from_content, axis=0, keepdims=True)
+    grad_bias[1:2, :] += jnp.sum(from_position, axis=0, keepdims=True)
+    key_sum[...] += dot_tn(content[...], grad_raw)
+    value_sum[...] += dot_tn(grad_out, soft)
+    table_sum[:, pl.ds(start, wide_len)] += dot_tn(flip_rows(position[...].astype(jnp.float32)).astype(jnp.bfloat16), grad_wide)
+    @pl.when(step == pl.num_programs(1) - 1)
+    def _():
+        grad_keys[...] = key_sum[...].T.astype(jnp.bfloat16)
+        grad_values[...] = value_sum[...].T.astype(jnp.bfloat16)
+        grad_table[...] = table_sum[...].T.astype(jnp.bfloat16)
+
+def attend_back(probs, grad_context, content, position, keys, values, table, head, block):
+    frames, width = content.shape
+    heads = width // head
+    rows = pl.BlockSpec((block, head), lambda h, i: (i, h))
+    whole = pl.BlockSpec((frames, head), lambda h, i: (0, h))
+    both = pl.BlockSpec((2 * frames, head), lambda h, i: (0, h))
+    out = functools.partial(jax.ShapeDtypeStruct, dtype=jnp.bfloat16)
+    return pl.pallas_call(
+        functools.partial(attend_back_kernel, frames, block),
+        out_shape=(out((frames, width)), out((frames, width)), out((frames, width)), out((2 * frames, width)), jax.ShapeDtypeStruct((8, width), jnp.float32)),
+        grid=(heads, frames // block),
+        in_specs=[pl.BlockSpec((1, block, frames), lambda h, i: (h, i, 0)), rows, rows, rows, whole, whole, both],
+        out_specs=[rows, whole, whole, both, pl.BlockSpec((8, head), lambda h, i: (0, h))],
+        scratch_shapes=[pltpu.VMEM((head, frames), jnp.float32), pltpu.VMEM((head, frames), jnp.float32), pltpu.VMEM((head, 2 * frames), jnp.float32)],
+        name="attend_back",
+    )(probs, grad_context, content, position, keys, values, table)
 
 
 def ffn_forward(residual, norm_gain, norm_shift, weight_up, weight_down):
@@ -151,44 +224,16 @@
         "fd,sdc->sfc", flat_act, attention_in, preferred_element_type=jnp.float32
     )
     biases = position_bias.astype(jnp.float32).reshape(2, 1, local_width)
-    block_size = min(512, slot_frames)
-    per_slot = slot_frames // block_size
-    block_count = slot_count * per_slot
-    shape_blocks = (block_count, block_size, head_count, head_size)
-    shape_slots = (slot_count, slot_frames, head_count, head_size)
-    query_content = (projected[0] + biases[0]).astype(jnp.bfloat16).reshape(shape_blocks)
-    query_position = (projected[0] + biases[1]).astype(jnp.bfloat16).reshape(shape_blocks)
-    key_all = projected[1].astype(jnp.bfloat16).reshape(shape_slots)
-    value_all = projected[2].astype(jnp.bfloat16).reshape(shape_slots)
-    table_in = relative_table(slot_frames, model_width).astype(jnp.bfloat16)
-    table = (
-        jnp.dot(table_in, position_proj, preferred_element_type=jnp.float32)
-        .astype(jnp.bfloat16)
-        .reshape(2 * slot_frames - 1, head_count, head_size)
-    )
-
-    def forward_block(block_index):
-        slot_index = block_index // per_slot
-        block_start = block_index % per_slot * block_size
-        block_content = lax.dynamic_index_in_dim(query_content, block_index, 0, keepdims=False)
-        block_position = lax.dynamic_index_in_dim(query_position, block_index, 0, keepdims=False)
-        slot_keys = lax.dynamic_index_in_dim(key_all, slot_index, 0, keepdims=False)
-        slot_values = lax.dynamic_index_in_dim(value_all, slot_index, 0, keepdims=False)
-        length = lax.dynamic_index_in_dim(lengths, slot_index, 0, keepdims=False)
-        scores, window = block_raw(
-            block_content, block_position, slot_keys, table, block_start, length
-        )
-        row_top = jnp.max(scores, axis=-1, keepdims=True)
-        log_total = row_top + jnp.log(jnp.sum(jnp.exp(scores - row_top), axis=-1, keepdims=True))
-        probs_soft = jnp.exp(scores - log_total).astype(jnp.bfloat16)
-        context = jnp.einsum(
-            "hbk,khe->bhe", probs_soft, slot_values, preferred_element_type=jnp.float32
-        )
-        return (context, log_total)
-
-    context_all, log_totals = lax.map(forward_block, jnp.arange(block_count, dtype=jnp.int32))
-    context_round = context_all.reshape(slot_count * slot_frames, local_width).astype(jnp.bfloat16)
-    partial_out = jnp.dot(context_round, attention_out, preferred_element_type=jnp.float32).reshape(
+    query_content = (projected[0] + biases[0]).astype(jnp.bfloat16)
+    query_position = (projected[0] + biases[1]).astype(jnp.bfloat16)
+    key_all = projected[1].astype(jnp.bfloat16)
+    value_all = projected[2].astype(jnp.bfloat16)
+    table_in = relative_table(slot_frames, model_width)
+    table = jnp.dot(table_in, position_proj, preferred_element_type=jnp.float32).astype(jnp.bfloat16)
+    context, probs = attend(
+        lengths, query_content, query_position, key_all, value_all, table, head_size, min(256, slot_frames)
+    )
+    partial_out = jnp.dot(context, attention_out, preferred_element_type=jnp.float32).reshape(
         slot_count, slot_frames, model_width
     )
     saved = (
@@ -201,13 +246,13 @@
         value_all,
         table_in,
         table,
-        context_round,
-        log_totals,
+        context,
+        probs,
     )
     return (narrow(partial_out), saved)
 
 
-def attn_backward(grad_after, saved, norm_gain, attention_in, attention_out, lengths):
+def attn_backward(grad_after, saved, norm_gain, attention_in, attention_out, head_count, head_size):
     (
         scaled,
         inv_std,
@@ -218,109 +263,33 @@
         value_all,
         table_in,
         table,
-        context_round,
-        log_totals,
+        context,
+        probs,
     ) = saved
     grad_round = widen_grad(grad_after)
     slot_count, slot_frames, model_width = grad_round.shape
     frames = slot_count * slot_frames
     grad_flat = grad_round.reshape(frames, model_width)
-    grad_back_proj = contract_rows(context_round, grad_flat)
-    block_count, block_size, head_count, head_size = query_content.shape
-    local_width = head_count * head_size
-    per_slot = slot_frames // block_size
-    score_scale = head_size ** (-0.5)
-    grad_context = (
-        times_transposed(grad_flat, attention_out).astype(jnp.bfloat16).reshape(query_content.shape)
-    )
-    zero_keys = jnp.zeros(key_all.shape, jnp.float32)
-    zero_table = jnp.zeros(table.shape, jnp.float32)
-
-    def backward_block(accum, block_index):
-        grad_keys, grad_values, grad_table = accum
-        slot_index = block_index // per_slot
-        block_start = block_index % per_slot * block_size
-        block_content = lax.dynamic_index_in_dim(query_content, block_index, 0, keepdims=False)
-        block_position = lax.dynamic_index_in_dim(query_position, block_index, 0, keepdims=False)
-        block_grad = lax.dynamic_index_in_dim(grad_context, block_index, 0, keepdims=False)
-        block_log = lax.dynamic_index_in_dim(log_totals, block_index, 0, keepdims=False)
-        slot_keys = lax.dynamic_index_in_dim(key_all, slot_index, 0, keepdims=False)
-        slot_values = lax.dynamic_index_in_dim(value_all, slot_index, 0, keepdims=False)
-        length = lax.dynamic_index_in_dim(lengths, slot_index, 0, keepdims=False)
-        scores, window = block_raw(
-            block_content, block_position, slot_keys, table, block_start, length
-        )
-        probs_soft = jnp.exp(scores - block_log)
-        grad_probs = jnp.einsum(
-            "bhe,khe->hbk", block_grad, slot_values, preferred_element_type=jnp.float32
-        )
-        delta_row = jnp.sum(probs_soft * grad_probs, axis=-1, keepdims=True)
-        grad_raw = (probs_soft * (grad_probs - delta_row) * score_scale).astype(jnp.bfloat16)
-        grad_content = jnp.einsum(
-            "hbk,khe->bhe", grad_raw, slot_keys, preferred_element_type=jnp.float32
-        )
-        grad_wide = unskew(grad_raw, window.shape[0])
-        grad_position = jnp.einsum(
-            "hbw,whe->bhe", grad_wide, window, preferred_element_type=jnp.float32
-        )
-        key_part = jnp.einsum(
-            "hbk,bhe->khe", grad_raw, block_content, preferred_element_type=jnp.float32
-        )
-        value_part = jnp.einsum(
-            "hbk,bhe->khe",
-            probs_soft.astype(jnp.bfloat16),
-            block_grad,
-            preferred_element_type=jnp.float32,
-        )
-        window_part = jnp.einsum(
-            "hbw,bhe->whe", grad_wide, block_position, preferred_element_type=jnp.float32
-        )
-        grad_keys = lax.dynamic_update_index_in_dim(
-            grad_keys,
-            lax.dynamic_index_in_dim(grad_keys, slot_index, 0, keepdims=False) + key_part,
-            slot_index,
-            0,
-        )
-        grad_values = lax.dynamic_update_index_in_dim(
-            grad_values,
-            lax.dynamic_index_in_dim(grad_values, slot_index, 0, keepdims=False) + value_part,
-            slot_index,
-            0,
-        )
-        window_start = slot_frames - block_size - block_start
-        grad_table = lax.dynamic_update_slice_in_dim(
-            grad_table,
-            lax.dynamic_slice_in_dim(grad_table, window_start, window.shape[0], 0) + window_part,
-            window_start,
-            0,
-        )
-        return ((grad_keys, grad_values, grad_table), (grad_content, grad_position))
-
-    accum, query_grads = lax.scan(
-        backward_block, (zero_keys, zero_keys, zero_table), jnp.arange(block_count, dtype=jnp.int32)
-    )
-    grad_content_all = query_grads[0].reshape(frames, local_width)
-    grad_position_all = query_grads[1].reshape(frames, local_width)
-    grad_bias = jnp.stack(
-        [jnp.sum(grad_content_all, axis=0), jnp.sum(grad_position_all, axis=0)]
-    ).reshape(2, head_count, head_size)
-    grad_query = (grad_content_all + grad_position_all).astype(jnp.bfloat16)
-    grad_proj = jnp.stack(
-        [
-            grad_query,
-            accum[0].reshape(frames, local_width).astype(jnp.bfloat16),
-            accum[1].reshape(frames, local_width).astype(jnp.bfloat16),
-        ]
-    )
-    grad_in_proj = jnp.einsum(
-        "fd,sfc->sdc", flat_act, grad_proj, preferred_element_type=jnp.float32
-    )
-    grad_act = jnp.einsum(
-        "sfc,sdc->fd", grad_proj, attention_in, preferred_element_type=jnp.float32
-    ).reshape(slot_count, slot_frames, model_width)
-    grad_table_proj = contract_rows(
-        table_in, accum[2].reshape(2 * slot_frames - 1, local_width).astype(jnp.bfloat16)
-    )
+    grad_back_proj = contract_rows(context, grad_flat)
+    grad_context = times_transposed(grad_flat, attention_out).astype(jnp.bfloat16)
+    grad_query, grad_keys, grad_values, grad_table, grad_bias = attend_back(
+        probs,
+        grad_context,
+        query_content,
+        query_position,
+        key_all,
+        value_all,
+        table,
+        head_size,
+        min(256, slot_frames),
+    )
+    grad_bias = grad_bias[:2].reshape(2, head_count, head_size)
+    grad_proj = (grad_query, grad_keys, grad_values)
+    grad_in_proj = jnp.stack([contract_rows(flat_act, part) for part in grad_proj])
+    grad_act = sum(times_transposed(part, attention_in[at]) for at, part in enumerate(grad_proj)).reshape(
+        slot_count, slot_frames, model_width
+    )
+    grad_table_proj = contract_rows(table_in, grad_table)
     grad_resid, grad_gain, grad_shift = norm_backward(
         narrow_grad(grad_act), scaled, inv_std, norm_gain
     )
@@ -557,7 +526,13 @@
     )
     grad_stream = grad_stream + grad_branch
     grad_branch, gain_two, shift_two, heads_grad, table_grad, bias_grad, back_grad = attn_backward(
-        grad_stream, saved_two, gain_rows[1], attention_in, attention_out, lengths
+        grad_stream,
+        saved_two,
+        gain_rows[1],
+        attention_in,
+        attention_out,
+        position_bias.shape[1],
+        position_bias.shape[2],
     )
     grad_stream = grad_stream + grad_branch
     grad_branch, gain_one, shift_one, up_one, down_one = ffn_backward(
@@ -574,15 +549,15 @@
         up_two,
         down_two,
     ) = (
-        lax.psum_scatter(up_one, "batch", scatter_dimension=0, tiled=True),
-        lax.psum_scatter(down_one, "batch", scatter_dimension=1, tiled=True),
-        lax.psum_scatter(heads_grad, "batch", scatter_dimension=1, tiled=True),
-        lax.psum_scatter(table_grad, "batch", scatter_dimension=0, tiled=True),
-        lax.psum_scatter(back_grad, "batch", scatter_dimension=1, tiled=True),
-        lax.psum_scatter(point_in_grad, "batch", scatter_dimension=0, tiled=True),
-        lax.psum_scatter(point_out_grad, "batch", scatter_dimension=1, tiled=True),
-        lax.psum_scatter(up_two, "batch", scatter_dimension=0, tiled=True),
-        lax.psum_scatter(down_two, "batch", scatter_dimension=1, tiled=True),
+        scatter_batch(up_one, 0),
+        scatter_batch(down_one, 1),
+        scatter_batch(heads_grad, 1),
+        scatter_batch(table_grad, 0),
+        scatter_batch(back_grad, 1),
+        scatter_batch(point_in_grad, 0),
+        scatter_batch(point_out_grad, 1),
+        scatter_batch(up_two, 0),
+        scatter_batch(down_two, 1),
     )
     grad_stream = grad_stream + grad_branch
     gain_grads = jnp.stack([gain_one, gain_two, gain_three, gain_four, gain_five])

time: 2600 us -> 1280 us (0.49)
  waiting for transfers between devices: 1250 us -> 725 us
  local copies, waits for them, and re-layouts: 537 us -> 28.5 us
  other arithmetic: 225 us -> 81.9 us
  matrix products: 308 us -> 171 us
  Pallas kernels: 0 us -> 45.6 us
  loops' own time: 37.5 us -> 0 us
    reduce_scatter x8 -> x9, waiting for transfers between devices: 925 us -> 576 us  [scatter_batch(): lax.psum_scatter(grad.astype(jnp.bfloat16), 'batch', scatter_dimension=di...]
    while x52 -> x0, local copies, waits for them, and re-layouts: 191 us -> none
    unnamed x26 -> x25, waiting for transfers between devices: 177 us -> 0.41 us
    reshape x13 -> x1, local copies, waits for them, and re-layouts: 159 us -> 0.02 us  [attn_backward(): grad_bias = grad_bias[:2].reshape(2, head_count, head_size)]
    sin x1 -> x0, other arithmetic: 122 us -> none  [relative_table(): jnp.sin(angles)]
    dot_general x23 -> x1, matrix products: 124 us -> 4.15 us  [attn_forward(): jnp.dot(context, attention_out, preferred_element_type=jnp.float32)]
    slice x6 -> x1, local copies, waits for them, and re-layouts: 58.6 us -> 0.72 us  [attn_backward(): grad_bias = grad_bias[:2].reshape(2, head_count, head_size)]
    pallas_call x0 -> x2, Pallas kernels: none -> 45.6 us  [the longest x1 25.2 us: attend_back(): pl.pallas_call(functools.partial(attend_back_kernel, frames, block), out_...]
  transfers between devices with their start and end apart: 25 -> 25, of which waited for: 22 -> 24; matrix products, arithmetic and copies ran while one was open for 10% -> 8% of each run, Pallas kernels for 0% -> 0%
where the time goes in v1:
time: 1280 us; the launch traced here: 1270 us
  waiting for transfers between devices  725 us (57%)
  blocking collectives  203 us (16%)
  matrix products  171 us (13%)
  other arithmetic  81.9 us (6%)
  Pallas kernels  45.6 us (4%)
  local copies, waits for them, and re-layouts  28.5 us (2%)
  between operations  16.1 us (1%)
    reduce_scatter x9, waiting for transfers between devices, scatter_batch(): lax.psum_scatter(grad.astype(jnp.bfloat16), 'batch', scatter_dimension=di...  576 us
    psum x1, blocking collectives, per_device(): bias_grad, kernel_grad = lax.psum((bias_grad, kernel_grad), 'batch')  72.6 us
    dot_general x10, matrix products, contract_rows(): lax.dot_general(left, right, (((0,), (0,)), ((), ())), preferred_element_...  53.8 us
    dot_general x9, matrix products, times_transposed(): lax.dot_general(left, right, (((1,), (1,)), ((), ())), preferred_element_...  51.6 us
    psum x1, blocking collectives, per_device(): lax.psum((gain_grads, shift_grads), ('batch', 'tensor'))  45.1 us
    psum x1, blocking collectives, conv_forward(): lax.psum((jnp.sum(mixed_conv * live_full, axis=0), jnp.sum(mixed_conv * m...  42.9 us
    psum x1, blocking collectives, conv_backward(): lax.psum((jnp.sum(grad_normed, axis=0), jnp.sum(grad_normed * centered, a...  42 us
    reduce_scatter x4, waiting for transfers between devices, narrow(): lax.psum_scatter(partial_out.astype(jnp.bfloat16), 'tensor', scatter_dime...  38.6 us
  transfers between devices with their start and end apart: 25, of which 24 were waited for; matrix products, arithmetic and copies ran while one was open for 8% of the time, Pallas kernels for 0%

profile of v1, /device:TPU:0, one launch (start us, length us, event | category | flops | bytes accessed | tf_op | source)
XLA Modules:
  0.0 1273.8 jit_solution(15387933556841223177)
XLA Ops:
  12.7 13.4 %all-gather.9.cloned.1.call-done = bf16[1,1024,1024]{2,1,0:T(8,128)(2,1)} async-done(((bf16[1,512,1024]{2,1,0:T(8,128)(2,1)}), bf16[1,1024,1024]{2,1,0:T(8,128)(2,1)}) %all-gather.9.cloned.1.call-update) | async-done | bytes 2097168 | tf_op jit(solution)/shard_map/all_gather | solution.py:46
  26.1 11.3 multiply_convert_fusion.3
  45.1 11.0 reduce-scatter.18.cloned.1.call-done
  82.6 20.4 %attend.1 = (bf16[1024,512]{1,0:T(8,128)(2,1)}, bf16[4,1024,1024]{2,1,0:T(8,128)(2,1)}) custom-call(s32[1]{0:T(128)} %copy.51.lengths, bf16[1024,512]{1,0:T(8,128)(2,1)} %get-tuple-element.101.content, bf16[1024,512]{1,0:T(8,128)(2,1)} %get-tuple-element.100.position, bf16[1024,512]{1,0:T(8,128)(2,1)} %get-tuple-element.104.keys, ...), custom_call_target="tpu_custom_call" | custom-call | tf_op jit(solution)/shard_map/attend/pallas_call | solution.py:115
  107.2 11.0 reduce-scatter.20.cloned.1.call-done
  123.6 11.5 all-gather.13.cloned.1.call-done
  143.9 42.9 %all-reduce.5 = (f32[512]{0:T(512)S(1)}, f32[]{:T(128)}, f32[512]{0:T(512)S(1)}) all-reduce(f32[512]{0:T(512)S(1)} %get-tuple-element.63, f32[]{:T(128)S(6)} %convert_element_type.269, f32[512]{0:T(512)S(1)} %get-tuple-element.62), channel_id=1, replica_groups=mesh['batch'=16,'tensor'=2] {'batch'}, use_global_device_ids=true, to_apply=%region_12.13 | all-reduce | flops 1025 | bytes 8200 | tf_op jit(solution)/shard_map/psum | solution.py:341
  202.8 12.0 all-gather.15.cloned.1.call-done
  214.7 11.3 multiply_convert_fusion.2
  234.0 10.8 reduce-scatter.24.cloned.1.call-done
  252.4 12.0 all-gather.17.cloned.1.call-done
  264.4 11.4 multiply_convert_fusion.1
  283.9 10.8 reduce-scatter.26.cloned.1.call-done
  302.3 11.9 all-gather.19.cloned.1.call-done
  320.3 42.0 %all-reduce.4 = (f32[512]{0:T(512)S(1)}, f32[512]{0:T(512)S(1)}) all-reduce(f32[512]{0:T(512)S(1)} %get-tuple-element.65, f32[512]{0:T(512)S(1)} %get-tuple-element.64), channel_id=1, replica_groups=mesh['batch'=16,'tensor'=2] {'batch'}, use_global_device_ids=true, to_apply=%region_27.28 | all-reduce | flops 1024 | bytes 8192 | tf_op jit(solution)/shard_map/psum | solution.py:399
  387.7 11.5 all-gather.21.cloned.1.call-done
  403.4 25.2 %attend_back.1 = (bf16[1024,512]{1,0:T(8,128)(2,1)}, bf16[1024,512]{1,0:T(8,128)(2,1)}, bf16[1024,512]{1,0:T(8,128)(2,1)}, bf16[2048,512]{1,0:T(8,128)(2,1)}, f32[8,512]{1,0:T(8,128)}) custom-call(bf16[4,1024,1024]{2,1,0:T(8,128)(2,1)} %get-tuple-element.25.probs, bf16[1024,512]{1,0:T(8,128)(2,1)} %fusion.106.grad_context, ...), custom_call_target="tpu_custom_call" | custom-call | tf_op jit(solution)/shard_map/attend_back/pallas_call | solution.py:166
  435.7 11.0 reduce-scatter.30.cloned.1.call-done
  452.4 9.4 convolution_convert_fusion
  503.1 11.5 multiply_convert_fusion
  533.9 8.3 convolution_convert_fusion.3
  542.3 20.5 %reduce-scatter.50.cloned.1.call-done = bf16[2048,64]{0,1:T(8,128)(2,1)} async-done(((bf16[2048,1024]{0,1:T(8,128)(2,1)}), bf16[2048,64]{0,1:T(8,128)(2,1)}) %reduce-scatter.50.cloned.1.call-update) | async-done | bytes 262160 | tf_op jit(solution)/shard_map/reduce_scatter | solution.py:66
  564.5 95.1 %reduce-scatter.48.cloned.1.call-done = bf16[64,2048]{1,0:T(8,128)(2,1)} async-done(((bf16[1024,2048]{1,0:T(8,128)(2,1)}), bf16[64,2048]{1,0:T(8,128)(2,1)}) %reduce-scatter.48.cloned.1.call-update) | async-done | bytes 262160 | tf_op jit(solution)/shard_map/reduce_scatter | solution.py:66
  661.4 78.7 %reduce-scatter.46.cloned.1.call-done = bf16[512,64]{0,1:T(8,128)(2,1)} async-done(((bf16[512,1024]{0,1:T(8,128)(2,1)}), bf16[512,64]{0,1:T(8,128)(2,1)}) %reduce-scatter.46.cloned.1.call-update) | async-done | bytes 65552 | tf_op jit(solution)/shard_map/reduce_scatter | solution.py:66
  741.6 78.7 %reduce-scatter.44.cloned.1.call-done = bf16[64,2,512]{2,0,1:T(8,128)(2,1)} async-done(((bf16[1024,2,512]{2,0,1:T(8,128)(2,1)}), bf16[64,2,512]{2,0,1:T(8,128)(2,1)}) %reduce-scatter.44.cloned.1.call-update) | async-done | bytes 131088 | tf_op jit(solution)/shard_map/reduce_scatter | solution.py:66
  822.8 72.6 %all-reduce.3 = (f32[2,4,128]{2,1,0:T(4,128)}, f32[5,512]{1,0:T(8,128)}) all-reduce(f32[2,4,128]{2,1,0:T(4,128)S(1)} %reshape.459, f32[5,512]{1,0:T(8,128)S(1)} %stack.98), channel_id=1, replica_groups=mesh['batch'=16,'tensor'=2] {'batch'}, use_global_device_ids=true, to_apply=%region_53.54 | all-reduce | flops 3584 | bytes 28672 | tf_op jit(solution)/shard_map/psum | solution.py:566
  899.4 75.7 %reduce-scatter.40.cloned.1.call-done = bf16[64,512]{1,0:T(8,128)(2,1)} async-done(((bf16[1024,512]{1,0:T(8,128)(2,1)}), bf16[64,512]{1,0:T(8,128)(2,1)}) %reduce-scatter.40.cloned.1.call-update) | async-done | bytes 65552 | tf_op jit(solution)/shard_map/reduce_scatter | solution.py:66
  976.6 81.6 %reduce-scatter.38.cloned.1.call-done = bf16[3,64,512]{2,1,0:T(8,128)(2,1)} async-done(((bf16[3,1024,512]{2,1,0:T(8,128)(2,1)}), bf16[3,64,512]{2,1,0:T(8,128)(2,1)}) %reduce-scatter.38.cloned.1.call-update) | async-done | bytes 196624 | tf_op jit(solution)/shard_map/reduce_scatter | solution.py:66
  1059.9 8.6 reduce-scatter.32.cloned.1.call-done
  1070.8 45.1 %all-reduce.2 = (f32[5,1024]{1,0:T(8,128)}, f32[5,1024]{1,0:T(8,128)}) all-reduce(f32[5,1024]{1,0:T(8,128)S(1)} %stack.82, f32[5,1024]{1,0:T(8,128)S(1)} %stack.88), channel_id=1, replica_groups=mesh['batch'=16,'tensor'=2] {'batch','tensor'}, use_global_device_ids=true, to_apply=%region_42.43 | all-reduce | flops 10240 | bytes 81920 | tf_op jit(solution)/shard_map/psum | solution.py:565
  1119.9 48.0 %reduce-scatter.36.cloned.1.call-done = bf16[2048,64]{0,1:T(8,128)(2,1)} async-done(((bf16[2048,1024]{0,1:T(8,128)(2,1)}), bf16[2048,64]{0,1:T(8,128)(2,1)}) %reduce-scatter.36.cloned.1.call-update) | async-done | bytes 262160 | tf_op jit(solution)/shard_map/reduce_scatter | solution.py:66
  1169.7 95.3 %reduce-scatter.34.cloned.1.call-done = bf16[64,2048]{1,0:T(8,128)(2,1)} async-done(((bf16[1024,2048]{1,0:T(8,128)(2,1)}), bf16[64,2048]{1,0:T(8,128)(2,1)}) %reduce-scatter.34.cloned.1.call-update) | async-done | bytes 262160 | tf_op jit(solution)/shard_map/reduce_scatter | solution.py:66
  (302 shorter events, 237.2 us)
Async XLA Ops:
  7.2 127.8 %copy-start = (bf16[1024,2,512]{2,1,0:T(2,128)(2,1)S(1)}, bf16[1024,2,512]{2,1,0:T(2,128)(2,1)}, u32[]{:S(2)}) copy-start(bf16[1024,2,512]{2,1,0:T(2,128)(2,1)} %param.32) | copy-start | bytes 6291460
  7.2 18.9 %all-gather.9.cloned.1.call-start = ((), (), s32[]{:S(2)}) async-start(), calls=%async_computation.17 | async-start | bytes 3145728 | tf_op jit(solution)/shard_map/all_gather | solution.py:46
  12.7 43.5 %reduce-scatter.18.cloned.1.call-start = ((), (), s32[]{:S(2)}) async-start(), calls=%async_computation.18 | async-start | bytes 3145728 | tf_op jit(solution)/shard_map/reduce_scatter | solution.py:50
  45.1 28.3 %all-gather.11.cloned.1.call-start = ((), (), s32[]{:S(2)}) async-start(), calls=%async_computation.19 | async-start | bytes 3145728 | tf_op jit(solution)/shard_map/all_gather | solution.py:46
  61.4 56.8 %reduce-scatter.20.cloned.1.call-start = ((), (), s32[]{:S(2)}) async-start(), calls=%async_computation.20 | async-start | bytes 3145728 | tf_op jit(solution)/shard_map/reduce_scatter | solution.py:50
  107.2 27.9 %all-gather.13.cloned.1.call-start = ((), (), s32[]{:S(2)}) async-start(), calls=%async_computation.21 | async-start | bytes 3145728 | tf_op jit(solution)/shard_map/all_gather | solution.py:46
  123.0 74.9 %reduce-scatter.22.cloned.1.call-start = ((), (), s32[]{:S(2)}) async-start(), calls=%async_computation.22 | async-start | bytes 3145728 | tf_op jit(solution)/shard_map/reduce_scatter | solution.py:50
  192.1 22.6 %all-gather.15.cloned.1.call-start = ((), (), s32[]{:S(2)}) async-start(), calls=%async_computation.23 | async-start | bytes 3145728 | tf_op jit(solution)/shard_map/all_gather | solution.py:46
  202.7 42.1 %reduce-scatter.24.cloned.1.call-start = ((), (), s32[]{:S(2)}) async-start(), calls=%async_computation.24 | async-start | bytes 3145728 | tf_op jit(solution)/shard_map/reduce_scatter | solution.py:50
  233.8 30.6 %all-gather.17.cloned.1.call-start = ((), (), s32[]{:S(2)}) async-start(), calls=%async_computation.25 | async-start | bytes 3145728 | tf_op jit(solution)/shard_map/all_gather | solution.py:56
  252.4 42.3 %reduce-scatter.26.cloned.1.call-start = ((), (), s32[]{:S(2)}) async-start(), calls=%async_computation.26 | async-start | bytes 3145728 | tf_op jit(solution)/shard_map/reduce_scatter | solution.py:60
  283.6 30.7 %all-gather.19.cloned.1.call-start = ((), (), s32[]{:S(2)}) async-start(), calls=%async_computation.27 | async-start | bytes 3145728 | tf_op jit(solution)/shard_map/all_gather | solution.py:56
  302.3 80.1 %reduce-scatter.28.cloned.1.call-start = ((), (), s32[]{:S(2)}) async-start(), calls=%async_computation.28 | async-start | bytes 3145728 | tf_op jit(solution)/shard_map/reduce_scatter | solution.py:60
  376.6 22.6 %all-gather.21.cloned.1.call-start = ((), (), s32[]{:S(2)}) async-start(), calls=%async_computation.29 | async-start | bytes 3145728 | tf_op jit(solution)/shard_map/all_gather | solution.py:56
  387.2 59.5 %reduce-scatter.30.cloned.1.call-start = ((), (), s32[]{:S(2)}) async-start(), calls=%async_computation.30 | async-start | bytes 3145728 | tf_op jit(solution)/shard_map/reduce_scatter | solution.py:60
  435.6 67.4 %all-gather.23.cloned.1.call-start = ((), (), s32[]{:S(2)}) async-start(), calls=%async_computation.31 | async-start | bytes 3145728 | tf_op jit(solution)/shard_map/all_gather | solution.py:56
  452.2 110.6 %reduce-scatter.50.cloned.1.call-start = ((), (), s32[]{:S(2)}) async-start(), calls=%async_computation.41 | async-start | bytes 4456448 | tf_op jit(solution)/shard_map/reduce_scatter | solution.py:66
  461.8 197.9 %reduce-scatter.48.cloned.1.call-start = ((), (), s32[]{:S(2)}) async-start(), calls=%async_computation.40 | async-start | bytes 4456448 | tf_op jit(solution)/shard_map/reduce_scatter | solution.py:66
  471.9 268.2 %reduce-scatter.46.cloned.1.call-start = ((), (), s32[]{:S(2)}) async-start(), calls=%async_computation.39 | async-start | bytes 1114112 | tf_op jit(solution)/shard_map/reduce_scatter | solution.py:66
  477.6 342.7 %reduce-scatter.44.cloned.1.call-start = ((), (), s32[]{:S(2)}) async-start(), calls=%async_computation.38 | async-start | bytes 2228224 | tf_op jit(solution)/shard_map/reduce_scatter | solution.py:66
  483.5 414.3 %reduce-scatter.42.cloned.1.call-start = ((), (), s32[]{:S(2)}) async-start(), calls=%async_computation.37 | async-start | bytes 1114112 | tf_op jit(solution)/shard_map/reduce_scatter | solution.py:66
  488.6 486.5 %reduce-scatter.40.cloned.1.call-start = ((), (), s32[]{:S(2)}) async-start(), calls=%async_computation.36 | async-start | bytes 1114112 | tf_op jit(solution)/shard_map/reduce_scatter | solution.py:66
  495.2 562.9 %reduce-scatter.38.cloned.1.call-start = ((), (), s32[]{:S(2)}) async-start(), calls=%async_computation.35 | async-start | bytes 3342336 | tf_op jit(solution)/shard_map/reduce_scatter | solution.py:66
  503.0 565.4 %reduce-scatter.32.cloned.1.call-start = ((), (), s32[]{:S(2)}) async-start(), calls=%async_computation.32 | async-start | bytes 3145728 | tf_op jit(solution)/shard_map/reduce_scatter | solution.py:60
  522.4 645.6 %reduce-scatter.36.cloned.1.call-start = ((), (), s32[]{:S(2)}) async-start(), calls=%async_computation.34 | async-start | bytes 4456448 | tf_op jit(solution)/shard_map/reduce_scatter | solution.py:66
  532.3 732.8 %reduce-scatter.34.cloned.1.call-start = ((), (), s32[]{:S(2)}) async-start(), calls=%async_computation.33 | async-start | bytes 4456448 | tf_op jit(solution)/shard_map/reduce_scatter | solution.py:66
  542.3 526.2 %copy-start.33 = (f32[1,1024]{1,0:T(1,128)S(1)}, f32[1,1024]{1,0:T(1,128)}, u32[]{:S(2)}) copy-start(f32[1,1024]{1,0:T(1,128)} %copy-done.32) | copy-start | bytes 12292
  542.3 526.2 %copy-start.37 = (f32[512]{0:T(512)S(1)}, f32[512]{0:T(512)}, u32[]{:S(2)}) copy-start(f32[512]{0:T(512)} %copy-done.36) | copy-start | bytes 6148
  542.3 526.1 %copy-start.41 = (f32[512]{0:T(512)S(1)}, f32[512]{0:T(512)}, u32[]{:S(2)}) copy-start(f32[512]{0:T(512)} %copy-done.40) | copy-start | bytes 6148
  564.5 506.1 %copy-start.48 = (f32[1024]{0:T(1024)S(1)}, f32[1024]{0:T(1024)}, u32[]{:S(2)}) copy-start(f32[1024]{0:T(1024)} %get-tuple-element.48) | copy-start | bytes 12292
  661.4 409.3 %copy-start.47 = (f32[1024]{0:T(1024)S(1)}, f32[1024]{0:T(1024)}, u32[]{:S(2)}) copy-start(f32[1024]{0:T(1024)} %get-tuple-element.71) | copy-start | bytes 12292
  1115.8 151.0 %copy-start.1 = (bf16[1024,2,512]{2,1,0:T(2,128)(2,1)S(1)}, bf16[1024,2,512]{2,1,0:T(2,128)(2,1)}, u32[]{:S(2)}) copy-start(bf16[1024,2,512]{2,1,0:T(2,128)(2,1)} %param.32) | copy-start | bytes 6291460
  (66 other events, 301.1 us)
Sparse Core Ops, SparseCore 0:
  12.8 13.2 all-gather.8
  45.2 10.9 reduce-scatter.17
  61.5 11.8 all-gather.10
  107.3 10.8 reduce-scatter.19
  123.2 11.8 all-gather.12
  192.2 5.6 reduce-scatter.21
  202.8 11.8 all-gather.14
  233.9 10.8 reduce-scatter.23
  252.5 11.8 all-gather.16
  283.7 10.8 reduce-scatter.25
  302.4 11.8 all-gather.18
  376.8 5.6 reduce-scatter.27
  387.4 11.8 all-gather.20
  435.8 10.9 reduce-scatter.29
  452.3 11.8 all-gather.22
  466.3 96.4 reduce-scatter.49
  564.9 94.7 reduce-scatter.47
  661.8 78.2 reduce-scatter.45
  742.4 77.8 reduce-scatter.43
  822.4 75.3 reduce-scatter.41
  900.1 74.9 reduce-scatter.39
  977.4 80.7 reduce-scatter.37
  1060.4 7.9 reduce-scatter.31
  1070.6 97.3 reduce-scatter.35
  1170.2 94.7 reduce-scatter.33

commit v2 on v1

--- a/solution.py
+++ b/solution.py
@@ -39,33 +39,79 @@
         - jnp.mean(grad_scaled, axis=-1, keepdims=True)
         - scaled * jnp.mean(grad_scaled * scaled, axis=-1, keepdims=True)
     )
-    return (grad_in, jnp.sum(grad_out * scaled, axis=(0, 1)), jnp.sum(grad_out, axis=(0, 1)))
-
-
-def widen(normed):
-    return lax.all_gather(normed.astype(jnp.bfloat16), "tensor", axis=1, tiled=True)
-
-
-def narrow(partial_out):
-    return lax.psum_scatter(
-        partial_out.astype(jnp.bfloat16), "tensor", scatter_dimension=1, tiled=True
-    ).astype(jnp.float32)
-
-
-def widen_grad(grad_half):
-    return lax.all_gather(grad_half.astype(jnp.bfloat16), "tensor", axis=1, tiled=True)
-
-
-def narrow_grad(partial_grad):
-    return lax.psum_scatter(
-        partial_grad.astype(jnp.bfloat16), "tensor", scatter_dimension=1, tiled=True
-    ).astype(jnp.float32)
-
-
-def scatter_batch(grad, dimension):
-    return lax.psum_scatter(
-        grad.astype(jnp.bfloat16), "batch", scatter_dimension=dimension, tiled=True
-    ).astype(jnp.float32)
+    return (grad_in, jnp.sum(grad_out * scaled, axis=0), jnp.sum(grad_out, axis=0))
+
+
+def swap(half):
+    return lax.ppermute(half, "tensor", [(0, 1), (1, 0)])
+
+
+def in_order(own, peer):
+    first = lax.axis_index("tensor") == 0
+    return jnp.concatenate([jnp.where(first, own, peer), jnp.where(first, peer, own)], axis=0)
+
+
+def split_own(whole):
+    half = whole.shape[0] // 2
+    side = lax.axis_index("tensor")
+    return (
+        lax.dynamic_slice_in_dim(whole, side * half, half, 0),
+        lax.dynamic_slice_in_dim(whole, (1 - side) * half, half, 0),
+    )
+
+
+def narrow(own, peer):
+    return own + swap(peer.astype(jnp.bfloat16)).astype(jnp.float32)
+
+
+def exchange(values, axis):
+    size = lax.axis_size(axis)
+    reach = 1
+    while reach < size:
+        radix = 4 if size % (reach * 4) == 0 else 2
+        got = [
+            lax.ppermute(values, axis, [(at, at ^ (reach * other)) for at in range(size)])
+            for other in range(1, radix)
+        ]
+        values = sum(got, values)
+        reach *= radix
+    return values
+
+
+def pick(term, bit, axis):
+    return lax.dynamic_index_in_dim(term, bit, axis, keepdims=False)
+
+
+def total(terms):
+    return sum((term.astype(jnp.float32) for term in terms[1:]), terms[0].astype(jnp.float32))
+
+
+def halve(grad, order):
+    size = lax.axis_size("batch")
+    index = lax.axis_index("batch")
+    rows, columns = grad.shape
+    left = list(range(size.bit_length() - 1))[::-1]
+    terms = [grad.reshape((2,) * len(left) + (rows // size, columns))]
+    for bit in order:
+        axis = left.index(bit)
+        mine = (index // 2**bit) % 2
+        outgoing = total([pick(term, 1 - mine, axis) for term in terms]).astype(jnp.bfloat16)
+        got = lax.ppermute(outgoing, "batch", [(at, at ^ 2**bit) for at in range(size)])
+        terms = [pick(term, mine, axis) for term in terms] + [got]
+        left.remove(bit)
+    return total(terms)
+
+
+def scatter_batch(grad, kind):
+    bits = list(range(lax.axis_size("batch").bit_length() - 1))
+    orders = {"x": bits, "y": [1, 0] + bits[2:], "z": bits[2:] + bits[:2]}
+    return halve(grad.astype(jnp.bfloat16), orders[kind])
+
+
+def scatter_mixed(grad, kind):
+    cut = grad.shape[1] * 3 // 4
+    grad = grad.astype(jnp.bfloat16)
+    return jnp.concatenate([scatter_batch(grad[:, :cut], kind), scatter_batch(grad[:, cut:], "z")], axis=1)
 
 
 def relative_table(slot_frames, model_width):
@@ -176,32 +222,37 @@
 
 def ffn_forward(residual, norm_gain, norm_shift, weight_up, weight_down):
     normed, scaled, inv_std = norm_forward(residual, norm_gain, norm_shift)
-    gathered = widen(normed)
-    slot_count, slot_frames, model_width = gathered.shape
-    flat_act = gathered.reshape(slot_count * slot_frames, model_width)
-    pre_act = jnp.dot(flat_act, weight_up, preferred_element_type=jnp.float32)
-    hidden = (pre_act * jax.nn.sigmoid(pre_act)).astype(jnp.bfloat16)
-    partial_out = jnp.dot(hidden, weight_down, preferred_element_type=jnp.float32).reshape(
-        slot_count, slot_frames, model_width
-    )
-    return (narrow(partial_out), (scaled, inv_std, flat_act, pre_act, hidden))
+    act_own = normed.astype(jnp.bfloat16)
+    act_peer = swap(act_own)
+
+    def hidden_of(act):
+        pre_act = jnp.dot(act, weight_up, preferred_element_type=jnp.float32)
+        gate_sig = jax.nn.sigmoid(pre_act)
+        slope = gate_sig * (1.0 + pre_act * (1.0 - gate_sig))
+        return ((pre_act * gate_sig).astype(jnp.bfloat16), slope.astype(jnp.bfloat16))
+
+    hidden_own, slope_own = hidden_of(act_own)
+    hidden_peer, slope_peer = hidden_of(act_peer)
+    out_peer = jnp.dot(hidden_peer, weight_down, preferred_element_type=jnp.float32)
+    out_own = jnp.dot(hidden_own, weight_down, preferred_element_type=jnp.float32)
+    saved = (scaled, inv_std, act_own, act_peer, hidden_own, hidden_peer, slope_own, slope_peer)
+    return (narrow(out_own, out_peer), saved)
 
 
 def ffn_backward(grad_after, saved, norm_gain, weight_up, weight_down):
-    scaled, inv_std, flat_act, pre_act, hidden = saved
-    grad_round = widen_grad(grad_after)
-    slot_count, slot_frames, model_width = grad_round.shape
-    grad_flat = grad_round.reshape(slot_count * slot_frames, model_width)
-    grad_down = contract_rows(hidden, grad_flat)
-    grad_hidden = times_transposed(grad_flat, weight_down)
-    gate_sig = jax.nn.sigmoid(pre_act)
-    grad_pre = (grad_hidden * gate_sig * (1.0 + pre_act * (1.0 - gate_sig))).astype(jnp.bfloat16)
-    grad_up = contract_rows(flat_act, grad_pre)
-    grad_act = times_transposed(grad_pre, weight_up).reshape(slot_count, slot_frames, model_width)
+    scaled, inv_std, act_own, act_peer, hidden_own, hidden_peer, slope_own, slope_peer = saved
+    grad_own = grad_after.astype(jnp.bfloat16)
+    grad_peer = swap(grad_own)
+    pre_own = (times_transposed(grad_own, weight_down) * slope_own.astype(jnp.float32)).astype(jnp.bfloat16)
+    pre_peer = (times_transposed(grad_peer, weight_down) * slope_peer.astype(jnp.float32)).astype(jnp.bfloat16)
+    back_peer = times_transposed(pre_peer, weight_up)
+    back_own = times_transposed(pre_own, weight_up)
+    grad_down = contract_rows(grad_own, hidden_own) + contract_rows(grad_peer, hidden_peer)
+    grad_up = contract_rows(act_own, pre_own) + contract_rows(act_peer, pre_peer)
     grad_resid, grad_gain, grad_shift = norm_backward(
-        narrow_grad(grad_act), scaled, inv_std, norm_gain
-    )
-    return (grad_resid, grad_gain, grad_shift, grad_up, grad_down)
+        narrow(back_own, back_peer), scaled, inv_std, norm_gain
+    )
+    return (grad_resid, grad_gain, grad_shift, scatter_mixed(grad_up, "x"), scatter_mixed(grad_down, "y").T)
 
 
 def attn_forward(
@@ -215,14 +266,14 @@
     lengths,
 ):
     normed, scaled, inv_std = norm_forward(residual, norm_gain, norm_shift)
-    gathered = widen(normed)
-    slot_count, slot_frames, model_width = gathered.shape
-    flat_act = gathered.reshape(slot_count * slot_frames, model_width)
+    own = normed.astype(jnp.bfloat16)
+    flat_act = in_order(own, swap(own))
+    slot_frames, model_width = flat_act.shape
     head_count, head_size = (position_bias.shape[1], position_bias.shape[2])
     local_width = head_count * head_size
-    projected = jnp.einsum(
-        "fd,sdc->sfc", flat_act, attention_in, preferred_element_type=jnp.float32
-    )
+    projected = [
+        jnp.dot(flat_act, attention_in[at], preferred_element_type=jnp.float32) for at in range(3)
+    ]
     biases = position_bias.astype(jnp.float32).reshape(2, 1, local_width)
     query_content = (projected[0] + biases[0]).astype(jnp.bfloat16)
     query_position = (projected[0] + biases[1]).astype(jnp.bfloat16)
@@ -233,9 +284,9 @@
     context, probs = attend(
         lengths, query_content, query_position, key_all, value_all, table, head_size, min(256, slot_frames)
     )
-    partial_out = jnp.dot(context, attention_out, preferred_element_type=jnp.float32).reshape(
-        slot_count, slot_frames, model_width
-    )
+    context_own, context_peer = split_own(context)
+    out_peer = jnp.dot(context_peer, attention_out, preferred_element_type=jnp.float32)
+    out_own = jnp.dot(context_own, attention_out, preferred_element_type=jnp.float32)
     saved = (
         scaled,
         inv_std,
@@ -249,7 +300,7 @@
         context,
         probs,
     )
-    return (narrow(partial_out), saved)
+    return (narrow(out_own, out_peer), saved)
 
 
 def attn_backward(grad_after, saved, norm_gain, attention_in, attention_out, head_count, head_size):
@@ -266,11 +317,10 @@
         context,
         probs,
     ) = saved
-    grad_round = widen_grad(grad_after)
-    slot_count, slot_frames, model_width = grad_round.shape
-    frames = slot_count * slot_frames
-    grad_flat = grad_round.reshape(frames, model_width)
-    grad_back_proj = contract_rows(context, grad_flat)
+    grad_own = grad_after.astype(jnp.bfloat16)
+    grad_flat = in_order(grad_own, swap(grad_own))
+    slot_frames = grad_flat.shape[0]
+    grad_back_proj = contract_rows(grad_flat, context)
     grad_context = times_transposed(grad_flat, attention_out).astype(jnp.bfloat16)
     grad_query, grad_keys, grad_values, grad_table, grad_bias = attend_back(
         probs,
@@ -285,22 +335,26 @@
     )
     grad_bias = grad_bias[:2].reshape(2, head_count, head_size)
     grad_proj = (grad_query, grad_keys, grad_values)
-    grad_in_proj = jnp.stack([contract_rows(flat_act, part) for part in grad_proj])
-    grad_act = sum(times_transposed(part, attention_in[at]) for at, part in enumerate(grad_proj)).reshape(
-        slot_count, slot_frames, model_width
-    )
+    halves = [split_own(part) for part in grad_proj]
+    back_own, back_peer = (
+        sum(times_transposed(half[side], attention_in[at]) for at, half in enumerate(halves))
+        for side in (0, 1)
+    )
+    grad_in_proj = jnp.concatenate([contract_rows(flat_act, part) for part in grad_proj], axis=1)
+    grad_in_proj = scatter_batch(grad_in_proj, "y")
+    grad_in_proj = jnp.stack(jnp.split(grad_in_proj, 3, axis=1))
     grad_table_proj = contract_rows(table_in, grad_table)
     grad_resid, grad_gain, grad_shift = norm_backward(
-        narrow_grad(grad_act), scaled, inv_std, norm_gain
+        narrow(back_own, back_peer), scaled, inv_std, norm_gain
     )
     return (
         grad_resid,
         grad_gain,
         grad_shift,
         grad_in_proj,
-        grad_table_proj,
+        scatter_batch(grad_table_proj, "z"),
         grad_bias,
-        grad_back_proj,
+        scatter_batch(grad_back_proj, "z").T,
     )
 
 
@@ -313,49 +367,39 @@
     batch_gain,
     batch_shift,
     pointwise_out,
-    lengths,
+    frame_count,
     live_full,
 ):
     normed, scaled, inv_std = norm_forward(residual, norm_gain, norm_shift)
-    gathered = widen(normed)
-    slot_count, slot_frames, model_width = gathered.shape
-    flat_act = gathered.reshape(slot_count * slot_frames, model_width)
-    both_halves = jnp.einsum(
-        "fd,dsc->sfc", flat_act, pointwise_in, preferred_element_type=jnp.float32
-    )
+    own = normed.astype(jnp.bfloat16)
+    flat_act = in_order(own, swap(own))
+    slot_frames = flat_act.shape[0]
+    both_halves = [
+        jnp.dot(flat_act, pointwise_in[:, at], preferred_element_type=jnp.float32) for at in range(2)
+    ]
     gate_sig = jax.nn.sigmoid(both_halves[1])
     gated = both_halves[0] * gate_sig * live_full
     channels = gated.shape[1]
     kernel = depthwise.astype(jnp.float32)
     tap_count = kernel.shape[0]
     half_taps = tap_count // 2
-    padded = jnp.pad(
-        gated.reshape(slot_count, slot_frames, channels), ((0, 0), (half_taps, half_taps), (0, 0))
-    )
-    mixed_conv = padded[:, 0:slot_frames, :] * kernel[0]
+    padded = jnp.pad(gated, ((half_taps, half_taps), (0, 0)))
+    mixed_conv = padded[0:slot_frames] * kernel[0]
     for tap_index in range(1, tap_count):
-        mixed_conv = (
-            mixed_conv + padded[:, tap_index : tap_index + slot_frames, :] * kernel[tap_index]
-        )
-    mixed_conv = mixed_conv.reshape(slot_count * slot_frames, channels)
-    totals = lax.psum(
-        (
-            jnp.sum(mixed_conv * live_full, axis=0),
-            jnp.sum(mixed_conv * mixed_conv * live_full, axis=0),
-            jnp.sum(lengths).astype(jnp.float32),
-        ),
+        mixed_conv = mixed_conv + padded[tap_index : tap_index + slot_frames] * kernel[tap_index]
+    totals = exchange(
+        jnp.stack([jnp.sum(mixed_conv * live_full, axis=0), jnp.sum(mixed_conv * mixed_conv * live_full, axis=0)]),
         "batch",
     )
-    frame_count = totals[2]
     batch_mean = totals[0] / frame_count
     batch_inv = lax.rsqrt(totals[1] / frame_count - batch_mean * batch_mean + eps_batch)
     centered = (mixed_conv - batch_mean) * batch_inv
     normed_batch = centered * batch_gain.astype(jnp.float32) + batch_shift.astype(jnp.float32)
     batch_sig = jax.nn.sigmoid(normed_batch)
     swished = (normed_batch * batch_sig).astype(jnp.bfloat16)
-    partial_out = jnp.dot(swished, pointwise_out, preferred_element_type=jnp.float32).reshape(
-        slot_count, slot_frames, model_width
-    )
+    swished_own, swished_peer = split_own(swished)
+    out_peer = jnp.dot(swished_peer, pointwise_out, preferred_element_type=jnp.float32)
+    out_own = jnp.dot(swished_own, pointwise_out, preferred_element_type=jnp.float32)
     saved = (
         scaled,
         inv_std,
@@ -370,7 +414,7 @@
         batch_sig,
         swished,
     )
-    return (narrow(partial_out), saved)
+    return (narrow(out_own, out_peer), saved)
 
 
 def conv_backward(
@@ -390,14 +434,14 @@
         batch_sig,
         swished,
     ) = saved
-    grad_round = widen_grad(grad_after)
-    slot_count, slot_frames, model_width = grad_round.shape
-    grad_flat = grad_round.reshape(slot_count * slot_frames, model_width)
-    grad_point_out = contract_rows(swished, grad_flat)
+    grad_own = grad_after.astype(jnp.bfloat16)
+    grad_flat = in_order(grad_own, swap(grad_own))
+    slot_frames = grad_flat.shape[0]
+    grad_point_out = scatter_batch(contract_rows(grad_flat, swished), "x").T
     grad_swished = times_transposed(grad_flat, pointwise_out)
     grad_normed = grad_swished * batch_sig * (1.0 + normed_batch * (1.0 - batch_sig))
-    sums = lax.psum(
-        (jnp.sum(grad_normed, axis=0), jnp.sum(grad_normed * centered, axis=0)), "batch"
+    sums = exchange(
+        jnp.stack([jnp.sum(grad_normed, axis=0), jnp.sum(grad_normed * centered, axis=0)]), "batch"
     )
     gamma = batch_gain.astype(jnp.float32)
     grad_mixed = batch_inv * (
@@ -408,30 +452,32 @@
     kernel = depthwise.astype(jnp.float32)
     tap_count = kernel.shape[0]
     half_taps = tap_count // 2
-    grad_mixed3 = grad_mixed.reshape(slot_count, slot_frames, channels)
     grad_kernel = jnp.stack(
         [
-            jnp.sum(grad_mixed3 * padded[:, tap_index : tap_index + slot_frames, :], axis=(0, 1))
+            jnp.sum(grad_mixed * padded[tap_index : tap_index + slot_frames], axis=0)
             for tap_index in range(tap_count)
         ]
     )
-    spread = jnp.pad(grad_mixed3, ((0, 0), (half_taps, half_taps), (0, 0)))
-    grad_gated = spread[:, 2 * half_taps : 2 * half_taps + slot_frames, :] * kernel[0]
+    spread = jnp.pad(grad_mixed, ((half_taps, half_taps), (0, 0)))
+    grad_gated = spread[2 * half_taps : 2 * half_taps + slot_frames] * kernel[0]
     for tap_index in range(1, tap_count):
         begin = 2 * half_taps - tap_index
-        grad_gated = grad_gated + spread[:, begin : begin + slot_frames, :] * kernel[tap_index]
-    grad_gated = grad_gated.reshape(slot_count * slot_frames, channels) * live_full
-    grad_halves = jnp.stack(
-        [grad_gated * gate_sig, grad_gated * both_halves[0] * gate_sig * (1.0 - gate_sig)]
-    ).astype(jnp.bfloat16)
-    grad_point_in = jnp.einsum(
-        "fd,sfc->dsc", flat_act, grad_halves, preferred_element_type=jnp.float32
-    )
-    grad_act = jnp.einsum(
-        "sfc,dsc->fd", grad_halves, pointwise_in, preferred_element_type=jnp.float32
-    ).reshape(slot_count, slot_frames, model_width)
+        grad_gated = grad_gated + spread[begin : begin + slot_frames] * kernel[tap_index]
+    grad_gated = grad_gated * live_full
+    grad_halves = [
+        (grad_gated * gate_sig).astype(jnp.bfloat16),
+        (grad_gated * both_halves[0] * gate_sig * (1.0 - gate_sig)).astype(jnp.bfloat16),
+    ]
+    grad_point_in = jnp.concatenate([contract_rows(flat_act, part) for part in grad_halves], axis=1)
+    grad_point_in = scatter_batch(grad_point_in, "x")
+    grad_point_in = grad_point_in.reshape(grad_point_in.shape[0], 2, channels)
+    halves = [split_own(part) for part in grad_halves]
+    back_own, back_peer = (
+        sum(times_transposed(half[side], pointwise_in[:, at]) for at, half in enumerate(halves))
+        for side in (0, 1)
+    )
     grad_resid, grad_gain, grad_shift = norm_backward(
-        narrow_grad(grad_act), scaled, inv_std, norm_gain
+        narrow(back_own, back_peer), scaled, inv_std, norm_gain
     )
     return (grad_resid, grad_gain, grad_shift, grad_point_in, grad_point_out, grad_kernel, sums)
 
@@ -458,18 +504,14 @@
 ):
     slot_count, half_frames, model_width = features.shape
     slot_frames = half_frames * lax.axis_size("tensor")
-    positions = (
-        lax.broadcasted_iota(jnp.int32, (slot_count, half_frames), 1)
-        + lax.axis_index("tensor") * half_frames
-    )
-    live_half = (positions < lengths[:, None]).astype(jnp.float32)[:, :, None]
-    full_positions = lax.broadcasted_iota(jnp.int32, (slot_count, slot_frames), 1)
-    live_full = (
-        (full_positions < lengths[:, None]).astype(jnp.float32).reshape(slot_count * slot_frames, 1)
-    )
+    positions = lax.broadcasted_iota(jnp.int32, (half_frames, 1), 0) + lax.axis_index("tensor") * half_frames
+    live_half = (positions < lengths[0]).astype(jnp.float32)
+    full_positions = lax.broadcasted_iota(jnp.int32, (slot_frames, 1), 0)
+    live_full = (full_positions < lengths[0]).astype(jnp.float32)
+    frame_count = exchange(jnp.broadcast_to(lengths.astype(jnp.float32), (8, 128)), "batch")[0, 0]
     gain_rows = norm_gains.astype(jnp.float32)
     shift_rows = norm_shifts.astype(jnp.float32)
-    stream_zero = features.astype(jnp.float32)
+    stream_zero = features[0].astype(jnp.float32)
     branch_one, saved_one = ffn_forward(
         stream_zero, gain_rows[0], shift_rows[0], first_up, first_down
     )
@@ -494,7 +536,7 @@
         batch_gain,
         batch_shift,
         pointwise_out,
-        lengths,
+        frame_count,
         live_full,
     )
     stream_three = stream_two + branch_three
@@ -504,7 +546,7 @@
     stream_four = stream_three + 0.5 * branch_four
     final_norm, scaled_final, inv_final = norm_forward(stream_four, gain_rows[4], shift_rows[4])
     output = (final_norm * live_half).astype(jnp.bfloat16)
-    grad_final = cotangent.astype(jnp.float32) * live_half
+    grad_final = cotangent[0].astype(jnp.float32) * live_half
     grad_stream, gain_five, shift_five = norm_backward(
         grad_final, scaled_final, inv_final, gain_rows[4]
     )
@@ -538,35 +580,21 @@
     grad_branch, gain_one, shift_one, up_one, down_one = ffn_backward(
         0.5 * grad_stream, saved_one, gain_rows[0], first_up, first_down
     )
-    (
-        up_one,
-        down_one,
-        heads_grad,
-        table_grad,
-        back_grad,
-        point_in_grad,
-        point_out_grad,
-        up_two,
-        down_two,
-    ) = (
-        scatter_batch(up_one, 0),
-        scatter_batch(down_one, 1),
-        scatter_batch(heads_grad, 1),
-        scatter_batch(table_grad, 0),
-        scatter_batch(back_grad, 1),
-        scatter_batch(point_in_grad, 0),
-        scatter_batch(point_out_grad, 1),
-        scatter_batch(up_two, 0),
-        scatter_batch(down_two, 1),
-    )
     grad_stream = grad_stream + grad_branch
-    gain_grads = jnp.stack([gain_one, gain_two, gain_three, gain_four, gain_five])
-    shift_grads = jnp.stack([shift_one, shift_two, shift_three, shift_four, shift_five])
-    gain_grads, shift_grads = lax.psum((gain_grads, shift_grads), ("batch", "tensor"))
-    bias_grad, kernel_grad = lax.psum((bias_grad, kernel_grad), "batch")
+    early = exchange(
+        exchange(jnp.stack([gain_two, gain_three, gain_four, gain_five, shift_two, shift_three, shift_four, shift_five]), "batch"),
+        "tensor",
+    )
+    late = exchange(exchange(jnp.stack([gain_one, shift_one]), "batch"), "tensor")
+    gain_grads = jnp.concatenate([late[:1], early[:4]])
+    shift_grads = jnp.concatenate([late[1:], early[4:]])
+    channels = kernel_grad.shape[1]
+    head_grads = exchange(jnp.concatenate([kernel_grad, bias_grad.reshape(2, channels)]), "batch")
+    kernel_grad = head_grads[:-2]
+    bias_grad = head_grads[-2:].reshape(bias_grad.shape)
     return (
-        output,
-        grad_stream,
+        output[None],
+        grad_stream[None],
         gain_grads,
         shift_grads,
         up_one,

time: 1280 us -> 664 us (0.52)
  waiting for transfers between devices: 725 us -> 243 us
  blocking collectives: 203 us -> 0 us
  starting transfers between devices: 3.08 us -> 108 us
  other arithmetic: 81.9 us -> 58.8 us
    reduce_scatter x17 -> x0, waiting for transfers between devices: 651 us -> none  [the longest x9 576 us: scatter_batch(): lax.psum_scatter(grad.astype(jnp.bfloat16), 'batch', scatter_dimension=di...]
    ppermute x0 -> x106, waiting for transfers between devices: none -> 243 us  [the longest x52 215 us: halve(): lax.ppermute(outgoing, 'batch', [(at, at ^ 2 ** bit) for at in range(size)])]
    psum x4 -> x0, blocking collectives: 203 us -> none  [the longest x1 72.6 us: per_device(): bias_grad, kernel_grad = lax.psum((bias_grad, kernel_grad), 'batch')]
    ppermute x0 -> x106, starting transfers between devices: none -> 108 us  [the longest x52 59 us: halve(): lax.ppermute(outgoing, 'batch', [(at, at ^ 2 ** bit) for at in range(size)])]
    all_gather x8 -> x0, waiting for transfers between devices: 73.7 us -> none  [the longest x4 38.2 us: widen(): lax.all_gather(normed.astype(jnp.bfloat16), 'tensor', axis=1, tiled=True)]
    dot_general x10 -> x17, matrix products: 62.1 us -> 45.4 us  [the longest x4 14.6 us: hidden_of(): pre_act = jnp.dot(act, weight_up, preferred_element_type=jnp.float32)]
    reduce_sum x7 -> x2, other arithmetic: 20.6 us -> 5.02 us  [the longest x1 3.23 us: conv_backward(): jnp.sum(grad_mixed * padded[tap_index:tap_index + slot_frames], axis=0)]
    convert_element_type x19 -> x52, other arithmetic: 33.3 us -> 25.2 us  [the longest x39 10 us: halve(): total([pick(term, 1 - mine, axis) for term in terms]).astype(jnp.bfloat16)]
  transfers between devices with their start and end apart: 25 -> 106, of which waited for: 24 -> 44; matrix products, arithmetic and copies ran while one was open for 8% -> 25% of each run, Pallas kernels for 0% -> 0%
where the time goes in v2:
time: 664 us; the launch traced here: 654 us
  waiting for transfers between devices  243 us (37%)
  matrix products  163 us (25%)
  starting transfers between devices  108 us (16%)
  other arithmetic  58.8 us (9%)
  Pallas kernels  46.3 us (7%)
  local copies, waits for them, and re-layouts  31.2 us (5%)
    ppermute x52, waiting for transfers between devices, halve(): lax.ppermute(outgoing, 'batch', [(at, at ^ 2 ** bit) for at in range(size)])  215 us
    ppermute x52, starting transfers between devices, halve(): lax.ppermute(outgoing, 'batch', [(at, at ^ 2 ** bit) for at in range(size)])  59 us
    dot_general x16, matrix products, contract_rows(): lax.dot_general(left, right, (((0,), (0,)), ((), ())), preferred_element_...  57.9 us
    dot_general x20, matrix products, times_transposed(): lax.dot_general(left, right, (((1,), (1,)), ((), ())), preferred_element_...  55.6 us
    ppermute x38, starting transfers between devices, exchange(): lax.ppermute(values, axis, [(at, at ^ reach * other) for at in range(size)])  46.1 us
    pallas_call x1, Pallas kernels, attend_back(): pl.pallas_call(functools.partial(attend_back_kernel, frames, block), out_...  25.8 us
    ppermute x38, waiting for transfers between devices, exchange(): lax.ppermute(values, axis, [(at, at ^ reach * other) for at in range(size)])  21.2 us
    pallas_call x1, Pallas kernels, attend(): pl.pallas_call(functools.partial(attend_kernel, frames, block), out_shape...  20.5 us
  transfers between devices with their start and end apart: 106, of which 44 were waited for; matrix products, arithmetic and copies ran while one was open for 25% of the time, Pallas kernels for 0%

profile of v2, /device:TPU:0, one launch (start us, length us, event | category | flops | bytes accessed | tf_op | source)
XLA Modules:
  0.0 654.4 jit_solution(9920655879318259592)
XLA Ops:
  45.2 20.5 %attend.1 = (bf16[1024,512]{1,0:T(8,128)(2,1)}, bf16[4,1024,1024]{2,1,0:T(8,128)(2,1)}) custom-call(s32[1]{0:T(128)} %copy.155.lengths, bf16[1024,512]{1,0:T(8,128)(2,1)} %get-tuple-element.82.content, bf16[1024,512]{1,0:T(8,128)(2,1)} %get-tuple-element.81.position, bf16[1024,512]{1,0:T(8,128)(2,1)} %convolution_convert_fusion.10.keys, ...), custom_call_target="tpu_custom_call" | custom-call | tf_op jit(solution)/shard_map/attend/pallas_call | solution.py:161
  140.7 5.8 fusion.161
  155.5 7.1 %add_convert_fusion = bf16[1024,2048]{1,0:T(8,128)(2,1)S(1)} fusion(f32[1024,2048]{1,0:T(8,128)} %fusion.161, bf16[512,1024]{1,0:T(8,128)(2,1)S(1)} %collective-permute-done.20, f32[512,2048]{1,0:T(8,128)} %copy-done.120), kind=kOutput, calls=%fused_computation | convolution fusion | flops 2156920832 | bytes 17825792 | tf_op jit(solution)/shard_map/dot_general | solution.py:17
  174.1 12.2 %collective-permute-done.102 = bf16[2,2,2,64,512]{4,3,2,1,0:T(8,128)(2,1)S(1)} collective-permute-done((bf16[2,2,2,64,512]{4,3,2,1,0:T(8,128)(2,1)S(1)}, bf16[2,2,2,64,512]{4,3,2,1,0:T(8,128)(2,1)S(1)}, u32[]{:S(2)}, u32[]{:S(2)}) %collective-permute-start.102) | collective-permute-done | bytes 524320 | tf_op jit(solution)/shard_map/ppermute | solution.py:99
  189.8 10.1 %collective-permute-done.103 = bf16[2,2,64,512]{3,2,1,0:T(8,128)(2,1)S(1)} collective-permute-done((bf16[2,2,64,512]{3,2,1,0:T(8,128)(2,1)S(1)}, bf16[2,2,64,512]{3,2,1,0:T(8,128)(2,1)S(1)}, u32[]{:S(2)}, u32[]{:S(2)}) %collective-permute-start.103) | collective-permute-done | bytes 262176 | tf_op jit(solution)/shard_map/ppermute | solution.py:99
  201.5 11.2 %collective-permute-done.96 = bf16[2,64,512]{2,1,0:T(8,128)(2,1)S(1)} collective-permute-done((bf16[2,64,512]{2,1,0:T(8,128)(2,1)S(1)}, bf16[2,64,512]{2,1,0:T(8,128)(2,1)S(1)}, u32[]{:S(2)}, u32[]{:S(2)}) %collective-permute-start.96) | collective-permute-done | bytes 131104 | tf_op jit(solution)/shard_map/ppermute | solution.py:99
  214.4 5.8 multiply_reduce_fusion.5
  237.4 11.2 %collective-permute-done.25 = f32[2,512]{1,0:T(2,128)S(1)} collective-permute-done((f32[2,512]{1,0:T(2,128)S(1)}, f32[2,512]{1,0:T(2,128)S(1)}, u32[]{:S(2)}, u32[]{:S(2)}) %collective-permute-start.25) | collective-permute-done | bytes 4128 | tf_op jit(solution)/shard_map/ppermute | solution.py:73
  273.6 8.0 %collective-permute-done.92 = bf16[2,64,1536]{2,1,0:T(8,128)(2,1)S(1)} collective-permute-done((bf16[2,64,1536]{2,1,0:T(8,128)(2,1)S(1)}, bf16[2,64,1536]{2,1,0:T(8,128)(2,1)S(1)}, u32[]{:S(2)}, u32[]{:S(2)}) %collective-permute-start.92) | collective-permute-done | bytes 393248 | tf_op jit(solution)/shard_map/ppermute | solution.py:99
  283.0 10.8 %collective-permute-done.100 = bf16[2,64,1536]{2,1,0:T(8,128)(2,1)S(1)} collective-permute-done((bf16[2,64,1536]{2,1,0:T(8,128)(2,1)S(1)}, bf16[2,64,1536]{2,1,0:T(8,128)(2,1)S(1)}, u32[]{:S(2)}, u32[]{:S(2)}) %collective-permute-start.100) | collective-permute-done | bytes 393248 | tf_op jit(solution)/shard_map/ppermute | solution.py:99
  296.4 8.1 %collective-permute-done.101 = bf16[64,1536]{1,0:T(8,128)(2,1)S(1)} collective-permute-done((bf16[64,1536]{1,0:T(8,128)(2,1)S(1)}, bf16[64,1536]{1,0:T(8,128)(2,1)S(1)}, u32[]{:S(2)}, u32[]{:S(2)}) %collective-permute-start.101) | collective-permute-done | bytes 196640 | tf_op jit(solution)/shard_map/ppermute | solution.py:99
  310.8 10.1 %collective-permute-done.83 = bf16[2,2,64,1024]{3,2,0,1:T(8,128)(2,1)S(1)} collective-permute-done((bf16[2,2,64,1024]{3,2,0,1:T(8,128)(2,1)S(1)}, bf16[2,2,64,1024]{3,2,0,1:T(8,128)(2,1)S(1)}, u32[]{:S(2)}, u32[]{:S(2)}) %collective-permute-start.83) | collective-permute-done | bytes 524320 | tf_op jit(solution)/shard_map/ppermute | solution.py:99
  324.8 5.1 collective-permute-done.84
  331.0 5.9 collective-permute-done.85
  341.8 25.8 %attend_back.1 = (bf16[1024,512]{1,0:T(8,128)(2,1)}, bf16[1024,512]{1,0:T(8,128)(2,1)}, bf16[1024,512]{1,0:T(8,128)(2,1)}, bf16[2048,512]{1,0:T(8,128)(2,1)}, f32[8,512]{1,0:T(8,128)}) custom-call(bf16[4,1024,1024]{2,1,0:T(8,128)(2,1)} %get-tuple-element.25.probs, bf16[1024,512]{1,0:T(8,128)(2,1)} %convolution_convert_fusion.8.grad_context, ...), custom_call_target="tpu_custom_call" | custom-call | tf_op jit(solution)/shard_map/attend_back/pallas_call | solution.py:212
  403.4 5.7 collective-permute-done.68
  409.2 8.4 %collective-permute-done.78 = bf16[2,2,2,64,512]{4,3,2,1,0:T(8,128)(2,1)S(1)} collective-permute-done((bf16[2,2,2,64,512]{4,3,2,1,0:T(8,128)(2,1)S(1)}, bf16[2,2,2,64,512]{4,3,2,1,0:T(8,128)(2,1)S(1)}, u32[]{:S(2)}, u32[]{:S(2)}) %collective-permute-start.78) | collective-permute-done | bytes 524320 | tf_op jit(solution)/shard_map/ppermute | solution.py:99
  422.6 13.2 %collective-permute-done.69 = bf16[2,2,64,512]{3,2,1,0:T(8,128)(2,1)S(1)} collective-permute-done((bf16[2,2,64,512]{3,2,1,0:T(8,128)(2,1)S(1)}, bf16[2,2,64,512]{3,2,1,0:T(8,128)(2,1)S(1)}, u32[]{:S(2)}, u32[]{:S(2)}) %collective-permute-start.69) | collective-permute-done | bytes 262176 | tf_op jit(solution)/shard_map/ppermute | solution.py:99
  436.5 5.3 collective-permute-done.79
  458.3 5.4 multiply_reduce_fusion.7
  479.6 5.8 fusion.159
  485.6 6.0 fusion.181
  496.5 5.9 add_convert_fusion.2
  502.5 5.9 add_convert_fusion.3
  517.8 9.0 %collective-permute-done.52 = bf16[2,2,2,64,512]{4,3,2,1,0:T(8,128)(2,1)S(1)} collective-permute-done((bf16[2,2,2,64,512]{4,3,2,1,0:T(8,128)(2,1)S(1)}, bf16[2,2,2,64,512]{4,3,2,1,0:T(8,128)(2,1)S(1)}, u32[]{:S(2)}, u32[]{:S(2)}) %collective-permute-start.52) | collective-permute-done | bytes 524320 | tf_op jit(solution)/shard_map/ppermute | solution.py:99
  527.7 10.3 %collective-permute-done.60 = bf16[2,2,2,64,512]{4,3,2,1,0:T(8,128)(2,1)S(1)} collective-permute-done((bf16[2,2,2,64,512]{4,3,2,1,0:T(8,128)(2,1)S(1)}, bf16[2,2,2,64,512]{4,3,2,1,0:T(8,128)(2,1)S(1)}, u32[]{:S(2)}, u32[]{:S(2)}) %collective-permute-start.60) | collective-permute-done | bytes 524320 | tf_op jit(solution)/shard_map/ppermute | solution.py:99
  540.0 11.4 %collective-permute-done.66 = bf16[2,64,1536]{2,1,0:T(8,128)(2,1)S(1)} collective-permute-done((bf16[2,64,1536]{2,1,0:T(8,128)(2,1)S(1)}, bf16[2,64,1536]{2,1,0:T(8,128)(2,1)S(1)}, u32[]{:S(2)}, u32[]{:S(2)}) %collective-permute-start.66) | collective-permute-done | bytes 393248 | tf_op jit(solution)/shard_map/ppermute | solution.py:99
  555.5 13.8 %collective-permute-done.61 = bf16[2,2,64,512]{3,2,1,0:T(8,128)(2,1)S(1)} collective-permute-done((bf16[2,2,64,512]{3,2,1,0:T(8,128)(2,1)S(1)}, bf16[2,2,64,512]{3,2,1,0:T(8,128)(2,1)S(1)}, u32[]{:S(2)}, u32[]{:S(2)}) %collective-permute-start.61) | collective-permute-done | bytes 262176 | tf_op jit(solution)/shard_map/ppermute | solution.py:99
  604.0 15.4 %collective-permute-done.49 = bf16[2,2,64,1536]{3,2,1,0:T(8,128)(2,1)S(1)} collective-permute-done((bf16[2,2,64,1536]{3,2,1,0:T(8,128)(2,1)S(1)}, bf16[2,2,64,1536]{3,2,1,0:T(8,128)(2,1)S(1)}, u32[]{:S(2)}, u32[]{:S(2)}) %collective-permute-start.49) | collective-permute-done | bytes 786464 | tf_op jit(solution)/shard_map/ppermute | solution.py:99
  623.3 8.3 %collective-permute-done.50 = bf16[2,64,1536]{2,1,0:T(8,128)(2,1)S(1)} collective-permute-done((bf16[2,64,1536]{2,1,0:T(8,128)(2,1)S(1)}, bf16[2,64,1536]{2,1,0:T(8,128)(2,1)S(1)}, u32[]{:S(2)}, u32[]{:S(2)}) %collective-permute-start.50) | collective-permute-done | bytes 393248 | tf_op jit(solution)/shard_map/ppermute | solution.py:99
  633.8 9.1 %collective-permute-done.58 = bf16[2,64,1536]{2,1,0:T(8,128)(2,1)S(1)} collective-permute-done((bf16[2,64,1536]{2,1,0:T(8,128)(2,1)S(1)}, bf16[2,64,1536]{2,1,0:T(8,128)(2,1)S(1)}, u32[]{:S(2)}, u32[]{:S(2)}) %collective-permute-start.58) | collective-permute-done | bytes 393248 | tf_op jit(solution)/shard_map/ppermute | solution.py:99
  644.1 8.8 %collective-permute-done.59 = bf16[64,1536]{1,0:T(8,128)(2,1)S(1)} collective-permute-done((bf16[64,1536]{1,0:T(8,128)(2,1)S(1)}, bf16[64,1536]{1,0:T(8,128)(2,1)S(1)}, u32[]{:S(2)}, u32[]{:S(2)}) %collective-permute-start.59) | collective-permute-done | bytes 196640 | tf_op jit(solution)/shard_map/ppermute | solution.py:99
  (653 shorter events, 344.7 us)
Async XLA Ops:
  67.9 23.6 %collective-permute-start.13 = (f32[8,128]{1,0:T(8,128)S(1)}, f32[8,128]{1,0:T(8,128)S(1)}, u32[]{:S(2)}, u32[]{:S(2)}) collective-permute-start(f32[8,128]{1,0:T(8,128)S(1)} %broadcast_in_dim.6), channel_id=1, source_target_pairs={{0,6},{2,4},{4,2},{6,0},{8,14},{10,12},{12,10},{14,8},{16,22},{18,... | collective-permute-start | bytes 12296 | tf_op jit(solution)/shard_map/ppermute | solution.py:73
  162.9 23.5 %collective-permute-start.102 = (bf16[2,2,2,64,512]{4,3,2,1,0:T(8,128)(2,1)S(1)}, bf16[2,2,2,64,512]{4,3,2,1,0:T(8,128)(2,1)S(1)}, u32[]{:S(2)}, u32[]{:S(2)}) collective-permute-start(bf16[2,2,2,64,512]{4,3,2,1,0:T(8,128)(2,1)S(1)} %dynamic-slice_bitcast_fusion.5), channel_id=1, source_target_pairs={{0,8},{2,10},{4,12},{6,14},{8,0},{10,2},{12,4},{14,6},{16,24},{18,... | collective-permute-start | bytes 1572872 | tf_op jit(solution)/shard_map/ppermute | solution.py:99
  170.1 44.3 %collective-permute-start.21 = (bf16[512,1024]{1,0:T(8,128)(2,1)S(1)}, bf16[512,1024]{1,0:T(8,128)(2,1)S(1)}, u32[]{:S(2)}, u32[]{:S(2)}) collective-permute-start(bf16[512,1024]{1,0:T(8,128)(2,1)S(1)} %convolution_convert_fusion.15), channel_id=1, source_target_pairs={{0,1},{1,0},{2,3},{3,2},{4,5},{5,4},{6,7},{7,6},{8,9},{9,8},{10,11... | collective-permute-start | bytes 3145736 | tf_op jit(solution)/shard_map/ppermute | solution.py:46
  172.6 55.1 %collective-permute-start.90 = (bf16[2,2,2,64,1536]{4,3,2,1,0:T(8,128)(2,1)S(1)}, bf16[2,2,2,64,1536]{4,3,2,1,0:T(8,128)(2,1)S(1)}, u32[]{:S(2)}, u32[]{:S(2)}) collective-permute-start(bf16[2,2,2,64,1536]{4,3,2,1,0:T(8,128)(2,1)S(1)} %dynamic-slice_bitcast_fusion.1), channel_id=1, source_target_pairs={{0,2},{2,0},{4,6},{6,4},{8,10},{10,8},{12,14},{14,12},{16,18},{18,... | collective-permute-start | bytes 4718600 | tf_op jit(solution)/shard_map/ppermute | solution.py:99
  186.6 26.1 %collective-permute-start.96 = (bf16[2,64,512]{2,1,0:T(8,128)(2,1)S(1)}, bf16[2,64,512]{2,1,0:T(8,128)(2,1)S(1)}, u32[]{:S(2)}, u32[]{:S(2)}) collective-permute-start(bf16[2,64,512]{2,1,0:T(8,128)(2,1)S(1)} %fusion.110), channel_id=1, source_target_pairs={{0,2},{2,0},{4,6},{6,4},{8,10},{10,8},{12,14},{14,12},{16,18},{18,... | collective-permute-start | bytes 393224 | tf_op jit(solution)/shard_map/ppermute | solution.py:99
  188.2 40.3 %collective-permute-start.98 = (bf16[2,2,2,64,1536]{4,3,2,1,0:T(8,128)(2,1)S(1)}, bf16[2,2,2,64,1536]{4,3,2,1,0:T(8,128)(2,1)S(1)}, u32[]{:S(2)}, u32[]{:S(2)}) collective-permute-start(bf16[2,2,2,64,1536]{4,3,2,1,0:T(8,128)(2,1)S(1)} %dynamic-slice_bitcast_fusion), channel_id=1, source_target_pairs={{0,4},{2,6},{4,0},{6,2},{8,12},{10,14},{12,8},{14,10},{16,20},{18,... | collective-permute-start | bytes 4718600 | tf_op jit(solution)/shard_map/ppermute | solution.py:99
  199.9 23.1 %collective-permute-start.104 = (bf16[2,64,512]{2,1,0:T(8,128)(2,1)S(1)}, bf16[2,64,512]{2,1,0:T(8,128)(2,1)S(1)}, u32[]{:S(2)}, u32[]{:S(2)}) collective-permute-start(bf16[2,64,512]{2,1,0:T(8,128)(2,1)S(1)} %fusion.109), channel_id=1, source_target_pairs={{0,2},{2,0},{4,6},{6,4},{8,10},{10,8},{12,14},{14,12},{16,18},{18,... | collective-permute-start | bytes 393224 | tf_op jit(solution)/shard_map/ppermute | solution.py:99
  227.9 41.5 %collective-permute-start.91 = (bf16[2,2,64,1536]{3,2,1,0:T(8,128)(2,1)S(1)}, bf16[2,2,64,1536]{3,2,1,0:T(8,128)(2,1)S(1)}, u32[]{:S(2)}, u32[]{:S(2)}) collective-permute-start(bf16[2,2,64,1536]{3,2,1,0:T(8,128)(2,1)S(1)} %fusion.30), channel_id=1, source_target_pairs={{0,4},{2,6},{4,0},{6,2},{8,12},{10,14},{12,8},{14,10},{16,20},{18,... | collective-permute-start | bytes 2359304 | tf_op jit(solution)/shard_map/ppermute | solution.py:99
  228.7 42.0 %collective-permute-start.99 = (bf16[2,2,64,1536]{3,2,1,0:T(8,128)(2,1)S(1)}, bf16[2,2,64,1536]{3,2,1,0:T(8,128)(2,1)S(1)}, u32[]{:S(2)}, u32[]{:S(2)}) collective-permute-start(bf16[2,2,64,1536]{3,2,1,0:T(8,128)(2,1)S(1)} %fusion.29), channel_id=1, source_target_pairs={{0,2},{2,0},{4,6},{6,4},{8,10},{10,8},{12,14},{14,12},{16,18},{18,... | collective-permute-start | bytes 2359304 | tf_op jit(solution)/shard_map/ppermute | solution.py:99
  267.3 37.4 %collective-permute-start.29 = (bf16[512,1024]{1,0:T(8,128)(2,1)S(1)}, bf16[512,1024]{1,0:T(8,128)(2,1)S(1)}, u32[]{:S(2)}, u32[]{:S(2)}) collective-permute-start(bf16[512,1024]{1,0:T(8,128)(2,1)S(1)} %add_convert_fusion.5), channel_id=1, source_target_pairs={{0,1},{1,0},{2,3},{3,2},{4,5},{5,4},{6,7},{7,6},{8,9},{9,8},{10,11... | collective-permute-start | bytes 3145736 | tf_op jit(solution)/shard_map/ppermute | solution.py:46
  270.9 22.9 %collective-permute-start.100 = (bf16[2,64,1536]{2,1,0:T(8,128)(2,1)S(1)}, bf16[2,64,1536]{2,1,0:T(8,128)(2,1)S(1)}, u32[]{:S(2)}, u32[]{:S(2)}) collective-permute-start(bf16[2,64,1536]{2,1,0:T(8,128)(2,1)S(1)} %fusion.61), channel_id=1, source_target_pairs={{0,8},{2,10},{4,12},{6,14},{8,0},{10,2},{12,4},{14,6},{16,24},{18,... | collective-permute-start | bytes 1179656 | tf_op jit(solution)/shard_map/ppermute | solution.py:99
  272.0 34.8 %collective-permute-start.82 = (bf16[2,2,2,64,1024]{4,3,2,1,0:T(8,128)(2,1)S(1)}, bf16[2,2,2,64,1024]{4,3,2,1,0:T(8,128)(2,1)S(1)}, u32[]{:S(2)}, u32[]{:S(2)}) collective-permute-start(bf16[2,2,2,64,1024]{4,3,2,1,0:T(8,128)(2,1)S(1)} %fusion.36), channel_id=1, source_target_pairs={{0,2},{2,0},{4,6},{6,4},{8,10},{10,8},{12,14},{14,12},{16,18},{18,... | collective-permute-start | bytes 3145736 | tf_op jit(solution)/shard_map/ppermute | solution.py:99
  273.0 21.0 %collective-permute-start.87 = (bf16[2,2,64,512]{3,2,1,0:T(8,128)(2,1)S(1)}, bf16[2,2,64,512]{3,2,1,0:T(8,128)(2,1)S(1)}, u32[]{:S(2)}, u32[]{:S(2)}) collective-permute-start(bf16[2,2,64,512]{3,2,1,0:T(8,128)(2,1)S(1)} %fusion.70), channel_id=1, source_target_pairs={{0,4},{2,6},{4,0},{6,2},{8,12},{10,14},{12,8},{14,10},{16,20},{18,... | collective-permute-start | bytes 786440 | tf_op jit(solution)/shard_map/ppermute | solution.py:99
  294.0 27.9 %collective-permute-start.88 = (bf16[2,64,512]{2,1,0:T(8,128)(2,1)S(1)}, bf16[2,64,512]{2,1,0:T(8,128)(2,1)S(1)}, u32[]{:S(2)}, u32[]{:S(2)}) collective-permute-start(bf16[2,64,512]{2,1,0:T(8,128)(2,1)S(1)} %fusion.111), channel_id=1, source_target_pairs={{0,8},{2,10},{4,12},{6,14},{8,0},{10,2},{12,4},{14,6},{16,24},{18,... | collective-permute-start | bytes 393224 | tf_op jit(solution)/shard_map/ppermute | solution.py:99
  310.0 28.0 %collective-permute-start.30 = (bf16[512,1024]{1,0:T(8,128)(2,1)}, bf16[512,1024]{1,0:T(8,128)(2,1)S(1)}, u32[]{:S(2)}, u32[]{:S(2)}) collective-permute-start(bf16[512,1024]{1,0:T(8,128)(2,1)} %get-tuple-element.63), channel_id=1, source_target_pairs={{0,1},{1,0},{2,3},{3,2},{4,5},{5,4},{6,7},{7,6},{8,9},{9,8},{10,11... | collective-permute-start | bytes 3145736 | tf_op jit(solution)/shard_map/ppermute | solution.py:46
  382.5 35.2 %collective-permute-start.74 = (f32[7,512]{1,0:T(8,128)S(1)}, f32[7,512]{1,0:T(8,128)S(1)}, u32[]{:S(2)}, u32[]{:S(2)}) collective-permute-start(f32[7,512]{1,0:T(8,128)S(1)} %concatenate.65), channel_id=1, source_target_pairs={{0,6},{2,4},{4,2},{6,0},{8,14},{10,12},{12,10},{14,8},{16,22},{18,... | collective-permute-start | bytes 43016 | tf_op jit(solution)/shard_map/ppermute | solution.py:73
  383.4 35.0 %collective-permute-start.73 = (f32[7,512]{1,0:T(8,128)S(1)}, f32[7,512]{1,0:T(8,128)S(1)}, u32[]{:S(2)}, u32[]{:S(2)}) collective-permute-start(f32[7,512]{1,0:T(8,128)S(1)} %concatenate.65), channel_id=1, source_target_pairs={{0,4},{2,6},{4,0},{6,2},{8,12},{10,14},{12,8},{14,10},{16,20},{18,... | collective-permute-start | bytes 43016 | tf_op jit(solution)/shard_map/ppermute | solution.py:73
  384.8 36.4 %collective-permute-start.72 = (f32[7,512]{1,0:T(8,128)S(1)}, f32[7,512]{1,0:T(8,128)S(1)}, u32[]{:S(2)}, u32[]{:S(2)}) collective-permute-start(f32[7,512]{1,0:T(8,128)S(1)} %concatenate.65), channel_id=1, source_target_pairs={{0,2},{2,0},{4,6},{6,4},{8,10},{10,8},{12,14},{14,12},{16,18},{18,... | collective-permute-start | bytes 43016 | tf_op jit(solution)/shard_map/ppermute | solution.py:73
  394.4 23.2 %collective-permute-start.78 = (bf16[2,2,2,64,512]{4,3,2,1,0:T(8,128)(2,1)S(1)}, bf16[2,2,2,64,512]{4,3,2,1,0:T(8,128)(2,1)S(1)}, u32[]{:S(2)}, u32[]{:S(2)}) collective-permute-start(bf16[2,2,2,64,512]{4,3,2,1,0:T(8,128)(2,1)S(1)} %dynamic-slice_bitcast_fusion.8), channel_id=1, source_target_pairs={{0,8},{2,10},{4,12},{6,14},{8,0},{10,2},{12,4},{14,6},{16,24},{18,... | collective-permute-start | bytes 1572872 | tf_op jit(solution)/shard_map/ppermute | solution.py:99
  409.1 49.1 %collective-permute-start.31 = (bf16[512,1024]{1,0:T(8,128)(2,1)}, bf16[512,1024]{1,0:T(8,128)(2,1)S(1)}, u32[]{:S(2)}, u32[]{:S(2)}) collective-permute-start(bf16[512,1024]{1,0:T(8,128)(2,1)} %add_convert_fusion.4), channel_id=1, source_target_pairs={{0,1},{1,0},{2,3},{3,2},{4,5},{5,4},{6,7},{7,6},{8,9},{9,8},{10,11... | collective-permute-start | bytes 3145736 | tf_op jit(solution)/shard_map/ppermute | solution.py:46
  417.7 73.9 %collective-permute-start.64 = (bf16[2,2,2,64,1536]{4,3,2,1,0:T(8,128)(2,1)}, bf16[2,2,2,64,1536]{4,3,2,1,0:T(8,128)(2,1)}, u32[]{:S(2)}, u32[]{:S(2)}) collective-permute-start(bf16[2,2,2,64,1536]{4,3,2,1,0:T(8,128)(2,1)} %dynamic-slice_bitcast_fusion.2), channel_id=1, source_target_pairs={{0,4},{2,6},{4,0},{6,2},{8,12},{10,14},{12,8},{14,10},{16,20},{18,... | collective-permute-start | bytes 4718600 | tf_op jit(solution)/shard_map/ppermute | solution.py:99
  418.4 23.3 %collective-permute-start.79 = (bf16[2,2,64,512]{3,2,1,0:T(8,128)(2,1)S(1)}, bf16[2,2,64,512]{3,2,1,0:T(8,128)(2,1)S(1)}, u32[]{:S(2)}, u32[]{:S(2)}) collective-permute-start(bf16[2,2,64,512]{3,2,1,0:T(8,128)(2,1)S(1)} %fusion.72), channel_id=1, source_target_pairs={{0,16},{2,18},{4,20},{6,22},{8,24},{10,26},{12,28},{14,30},{16,0},... | collective-permute-start | bytes 786440 | tf_op jit(solution)/shard_map/ppermute | solution.py:99
  421.3 21.2 %collective-permute-start.77 = (f32[7,512]{1,0:T(8,128)S(1)}, f32[7,512]{1,0:T(8,128)S(1)}, u32[]{:S(2)}, u32[]{:S(2)}) collective-permute-start(f32[7,512]{1,0:T(8,128)S(1)} %add_add_fusion.5), channel_id=1, source_target_pairs={{0,24},{2,26},{4,28},{6,30},{8,16},{10,18},{12,20},{14,22},{16,8},... | collective-permute-start | bytes 43016 | tf_op jit(solution)/shard_map/ppermute | solution.py:73
  470.5 23.0 %collective-permute-start.32 = (bf16[512,1024]{1,0:T(8,128)(2,1)S(1)}, bf16[512,1024]{1,0:T(8,128)(2,1)S(1)}, u32[]{:S(2)}, u32[]{:S(2)}) collective-permute-start(bf16[512,1024]{1,0:T(8,128)(2,1)S(1)} %get-tuple-element.61), channel_id=1, source_target_pairs={{0,1},{1,0},{2,3},{3,2},{4,5},{5,4},{6,7},{7,6},{8,9},{9,8},{10,11... | collective-permute-start | bytes 3145736 | tf_op jit(solution)/shard_map/ppermute | solution.py:46
  493.0 22.9 %collective-permute-start.65 = (bf16[2,2,64,1536]{3,2,0,1:T(8,128)(2,1)S(1)}, bf16[2,2,64,1536]{3,2,0,1:T(8,128)(2,1)S(1)}, u32[]{:S(2)}, u32[]{:S(2)}) collective-permute-start(bf16[2,2,64,1536]{3,2,0,1:T(8,128)(2,1)S(1)} %copy.88), channel_id=1, source_target_pairs={{0,2},{2,0},{4,6},{6,4},{8,10},{10,8},{12,14},{14,12},{16,18},{18,... | collective-permute-start | bytes 2359304 | tf_op jit(solution)/shard_map/ppermute | solution.py:99
  511.6 71.6 %collective-permute-start.33 = (bf16[512,1024]{1,0:T(8,128)(2,1)S(1)}, bf16[512,1024]{1,0:T(8,128)(2,1)S(1)}, u32[]{:S(2)}, u32[]{:S(2)}) collective-permute-start(bf16[512,1024]{1,0:T(8,128)(2,1)S(1)} %convolution_convert_fusion.14), channel_id=1, source_target_pairs={{0,1},{1,0},{2,3},{3,2},{4,5},{5,4},{6,7},{7,6},{8,9},{9,8},{10,11... | collective-permute-start | bytes 3145736 | tf_op jit(solution)/shard_map/ppermute | solution.py:46
  512.7 86.5 %collective-permute-start.48 = (bf16[2,2,2,64,1536]{4,3,2,1,0:T(8,128)(2,1)S(1)}, bf16[2,2,2,64,1536]{4,3,2,1,0:T(8,128)(2,1)S(1)}, u32[]{:S(2)}, u32[]{:S(2)}) collective-permute-start(bf16[2,2,2,64,1536]{4,3,2,1,0:T(8,128)(2,1)S(1)} %dynamic-slice_bitcast_fusion.4), channel_id=1, source_target_pairs={{0,2},{2,0},{4,6},{6,4},{8,10},{10,8},{12,14},{14,12},{16,18},{18,... | collective-permute-start | bytes 4718600 | tf_op jit(solution)/shard_map/ppermute | solution.py:99
  514.4 23.7 %collective-permute-start.60 = (bf16[2,2,2,64,512]{4,3,2,1,0:T(8,128)(2,1)S(1)}, bf16[2,2,2,64,512]{4,3,2,1,0:T(8,128)(2,1)S(1)}, u32[]{:S(2)}, u32[]{:S(2)}) collective-permute-start(bf16[2,2,2,64,512]{4,3,2,1,0:T(8,128)(2,1)S(1)} %dynamic-slice_bitcast_fusion.10), channel_id=1, source_target_pairs={{0,8},{2,10},{4,12},{6,14},{8,0},{10,2},{12,4},{14,6},{16,24},{18,... | collective-permute-start | bytes 1572872 | tf_op jit(solution)/shard_map/ppermute | solution.py:99
  517.1 34.3 %collective-permute-start.66 = (bf16[2,64,1536]{2,1,0:T(8,128)(2,1)S(1)}, bf16[2,64,1536]{2,1,0:T(8,128)(2,1)S(1)}, u32[]{:S(2)}, u32[]{:S(2)}) collective-permute-start(bf16[2,64,1536]{2,1,0:T(8,128)(2,1)S(1)} %fusion.63), channel_id=1, source_target_pairs={{0,8},{2,10},{4,12},{6,14},{8,0},{10,2},{12,4},{14,6},{16,24},{18,... | collective-permute-start | bytes 1179656 | tf_op jit(solution)/shard_map/ppermute | solution.py:99
  526.8 73.7 %collective-permute-start.56 = (bf16[2,2,2,64,1536]{4,3,2,1,0:T(8,128)(2,1)S(1)}, bf16[2,2,2,64,1536]{4,3,2,1,0:T(8,128)(2,1)S(1)}, u32[]{:S(2)}, u32[]{:S(2)}) collective-permute-start(bf16[2,2,2,64,1536]{4,3,2,1,0:T(8,128)(2,1)S(1)} %dynamic-slice_bitcast_fusion.3), channel_id=1, source_target_pairs={{0,4},{2,6},{4,0},{6,2},{8,12},{10,14},{12,8},{14,10},{16,20},{18,... | collective-permute-start | bytes 4718600 | tf_op jit(solution)/shard_map/ppermute | solution.py:99
  552.6 20.9 %collective-permute-start.67 = (bf16[64,1536]{1,0:T(8,128)(2,1)S(1)}, bf16[64,1536]{1,0:T(8,128)(2,1)S(1)}, u32[]{:S(2)}, u32[]{:S(2)}) collective-permute-start(bf16[64,1536]{1,0:T(8,128)(2,1)S(1)} %fusion.102), channel_id=1, source_target_pairs={{0,16},{2,18},{4,20},{6,22},{8,24},{10,26},{12,28},{14,30},{16,0},... | collective-permute-start | bytes 589832 | tf_op jit(solution)/shard_map/ppermute | solution.py:99
  621.2 21.7 %collective-permute-start.58 = (bf16[2,64,1536]{2,1,0:T(8,128)(2,1)S(1)}, bf16[2,64,1536]{2,1,0:T(8,128)(2,1)S(1)}, u32[]{:S(2)}, u32[]{:S(2)}) collective-permute-start(bf16[2,64,1536]{2,1,0:T(8,128)(2,1)S(1)} %fusion.64), channel_id=1, source_target_pairs={{0,8},{2,10},{4,12},{6,14},{8,0},{10,2},{12,4},{14,6},{16,24},{18,... | collective-permute-start | bytes 1179656 | tf_op jit(solution)/shard_map/ppermute | solution.py:99
  (198 other events, 1876.7 us)

commit v3 on v2

--- a/solution.py
+++ b/solution.py
@@ -64,8 +64,13 @@
     return own + swap(peer.astype(jnp.bfloat16)).astype(jnp.float32)
 
 
-def exchange(values, axis):
+def after(value, tie):
+    return lax.optimization_barrier((value, tie))[0]
+
+
+def exchange(values, axis, fillers=()):
     size = lax.axis_size(axis)
+    fillers, filled = list(fillers), []
     reach = 1
     while reach < size:
         radix = 4 if size % (reach * 4) == 0 else 2
@@ -73,45 +78,200 @@
             lax.ppermute(values, axis, [(at, at ^ (reach * other)) for at in range(size)])
             for other in range(1, radix)
         ]
+        if fillers:
+            *got, work = lax.optimization_barrier((*got, fillers.pop(0)(values)))
+            filled.append(work)
         values = sum(got, values)
         reach *= radix
-    return values
-
-
-def pick(term, bit, axis):
-    return lax.dynamic_index_in_dim(term, bit, axis, keepdims=False)
-
-
-def total(terms):
-    return sum((term.astype(jnp.float32) for term in terms[1:]), terms[0].astype(jnp.float32))
-
-
-def halve(grad, order):
+    for filler in fillers:
+        filled.append(filler(values))
+    return values, filled
+
+
+def scatter_batch(grad):
+    return lax.psum_scatter(
+        grad.astype(jnp.bfloat16), "batch", scatter_dimension=0, tiled=True
+    ).astype(jnp.float32)
+
+
+chunk_width = 512
+
+
+def reduce_plan(size, chunk_count):
+    bits = list(range(size.bit_length() - 1))
+    kinds = (bits, [1, 0] + bits[2:], bits[2:] + bits[:2])
+    few = max(1, round(chunk_count * 2 / 9))
+    orders = []
+    for at in range(chunk_count):
+        orders.append(kinds[2] if at % 4 == 3 and sum(o is kinds[2] for o in orders) < few else None)
+    plain = [at for at in range(chunk_count) if orders[at] is None]
+    for turn, at in enumerate(plain):
+        orders[at] = kinds[turn % 2]
+    free, arrivals, events = {}, [], []
+
+    def issue(chunk, stage, now):
+        bit = orders[chunk][stage]
+        link = min(bit, 2)
+        cost = 2.0 ** -(stage + 1) * (2 if bit >= 3 else 1)
+        free[link] = max(free.get(link, 0.0), now) + cost
+        arrivals.append((free[link] + 0.05, chunk, stage))
+
+    def issue_small(stage, now):
+        link = min(stage, 2) if stage < len(bits) else 3
+        free[link] = max(free.get(link, 0.0), now) + 0.03
+        arrivals.append((free[link] + 0.1, -1, stage))
+
+    issue_small(0, 0.0)
+    for chunk in range(chunk_count):
+        issue(chunk, 0, 0.0)
+    while arrivals:
+        arrivals.sort()
+        now, chunk, stage = arrivals.pop(0)
+        events.append((chunk, stage + 1))
+        if chunk < 0 and stage < len(bits):
+            issue_small(stage + 1, now)
+        elif chunk >= 0 and stage + 1 < len(bits):
+            issue(chunk, stage + 1, now)
+    return orders, events
+
+
+def reduce_kernel(size, places, pair_rows, *refs):
+    stages = size.bit_length() - 1
+    orders, events = reduce_plan(size, len(places))
+    count = max(at for at, _ in places) + 1
+    grads, small, out, small_out = refs[:count], refs[count], refs[count + 1], refs[count + 2]
+    refs = refs[count + 3 :]
+    landed = refs[:stages]
+    leaving = (None,) + tuple(refs[stages : 2 * stages - 1])
+    small_sum, small_landed, sent, arrived, small_sent, small_arrived = refs[2 * stages - 1 :]
+    rows = out.shape[0]
+    me = lax.axis_index("batch")
+    mine = [lax.rem(me // 2**bit, 2) for bit in range(stages)]
+
+    def shard(block):
+        return sum(2**bit * lax.rem(mine[bit] + (block >> bit) % 2, 2) for bit in range(stages))
+
+    barrier = pltpu.get_barrier_semaphore()
+    for bit in range(stages):
+        pl.semaphore_signal(barrier, inc=1, device_id={"batch": shard(2**bit)}, device_id_type=pl.DeviceIdType.MESH)
+    peer = {"tensor": 1 - lax.axis_index("tensor")}
+    pl.semaphore_signal(barrier, inc=1, device_id=peer, device_id_type=pl.DeviceIdType.MESH)
+    pl.semaphore_wait(barrier, stages + 1)
+
+    def blocks(chunk, stage):
+        order = orders[chunk]
+        return [
+            block
+            for block in range(size)
+            if (block >> order[stage]) % 2 and not any((block >> bit) % 2 for bit in order[:stage])
+        ]
+
+    def copy(chunk, stage, source, target):
+        return pltpu.make_async_remote_copy(
+            src_ref=source,
+            dst_ref=target,
+            send_sem=sent.at[chunk, stage],
+            recv_sem=arrived.at[chunk, stage],
+            device_id={"batch": shard(2 ** orders[chunk][stage])},
+            device_id_type=pl.DeviceIdType.MESH,
+        )
+
+    def columns(chunk):
+        return pl.ds(places[chunk][1], chunk_width)
+
+    def summed(chunk, block, stage, tile):
+        total = grads[places[chunk][0]][shard(block), tile, columns(chunk)].astype(jnp.float32)
+        for past in range(stage):
+            at = blocks(chunk, past).index(block | (1 << orders[chunk][past]))
+            total = total + landed[past][chunk, at, tile, :].astype(jnp.float32)
+        return total
+
+    def whole(chunk, stage):
+        return copy(chunk, stage, landed[stage].at[chunk], landed[stage].at[chunk])
+
+    def small_copy(stage):
+        rows = pl.ds(0, small.shape[0] if stage < stages else pair_rows)
+        return pltpu.make_async_remote_copy(
+            src_ref=(small if stage == 0 else small_sum.at[stage]).at[rows],
+            dst_ref=small_landed.at[stage, rows],
+            send_sem=small_sent.at[stage],
+            recv_sem=small_arrived.at[stage],
+            device_id={"batch": shard(2**stage)} if stage < stages else peer,
+            device_id_type=pl.DeviceIdType.MESH,
+        )
+
+    small_copy(0).start()
+    for chunk in range(len(places)):
+        for at, block in enumerate(blocks(chunk, 0)):
+            copy(
+                chunk, 0, grads[places[chunk][0]].at[shard(block), :, columns(chunk)], landed[0].at[chunk, at]
+            ).start()
+
+    step = min(16, rows)
+    for chunk, stage in events:
+        if chunk < 0:
+            small_copy(stage - 1).wait_recv()
+            held = small[...] if stage == 1 else small_sum[stage - 1]
+            if stage <= stages:
+                small_sum[stage] = held + small_landed[stage - 1]
+                small_copy(stage).start()
+            else:
+                small_out[:pair_rows, :] = held[:pair_rows] + small_landed[stages, :pair_rows, :]
+                small_out[pair_rows:, :] = held[pair_rows:]
+            continue
+        whole(chunk, stage - 1).wait_recv()
+
+        def work(tile_index, carry, chunk=chunk, stage=stage):
+            tile = pl.ds(pl.multiple_of(tile_index * step, step), step)
+            if stage < stages:
+                for at, block in enumerate(blocks(chunk, stage)):
+                    leaving[stage][chunk, at, tile, :] = summed(chunk, block, stage, tile).astype(jnp.bfloat16)
+            else:
+                out[tile, pl.ds(chunk * chunk_width, chunk_width)] = summed(chunk, 0, stage, tile)
+            return carry
+
+        lax.fori_loop(0, rows // step, work, 0)
+        if stage < stages:
+            copy(chunk, stage, leaving[stage].at[chunk], landed[stage].at[chunk]).start()
+    for stage in range(stages + 1):
+        small_copy(stage).wait_send()
+    for chunk in range(len(places)):
+        for stage in range(stages):
+            whole(chunk, stage).wait_send()
+
+
+def reduce_rows(grads, small, pair_rows):
     size = lax.axis_size("batch")
-    index = lax.axis_index("batch")
-    rows, columns = grad.shape
-    left = list(range(size.bit_length() - 1))[::-1]
-    terms = [grad.reshape((2,) * len(left) + (rows // size, columns))]
-    for bit in order:
-        axis = left.index(bit)
-        mine = (index // 2**bit) % 2
-        outgoing = total([pick(term, 1 - mine, axis) for term in terms]).astype(jnp.bfloat16)
-        got = lax.ppermute(outgoing, "batch", [(at, at ^ 2**bit) for at in range(size)])
-        terms = [pick(term, mine, axis) for term in terms] + [got]
-        left.remove(bit)
-    return total(terms)
-
-
-def scatter_batch(grad, kind):
-    bits = list(range(lax.axis_size("batch").bit_length() - 1))
-    orders = {"x": bits, "y": [1, 0] + bits[2:], "z": bits[2:] + bits[:2]}
-    return halve(grad.astype(jnp.bfloat16), orders[kind])
-
-
-def scatter_mixed(grad, kind):
-    cut = grad.shape[1] * 3 // 4
-    grad = grad.astype(jnp.bfloat16)
-    return jnp.concatenate([scatter_batch(grad[:, :cut], kind), scatter_batch(grad[:, cut:], "z")], axis=1)
+    stages = size.bit_length() - 1
+    rows = grads[0].shape[0] // size
+    places = [(at, begin) for at, grad in enumerate(grads) for begin in range(0, grad.shape[1], chunk_width)]
+    chunks = len(places)
+    total_width = chunks * chunk_width
+    halves = [pltpu.VMEM((chunks, size >> (stage + 1), rows, chunk_width), jnp.bfloat16) for stage in range(stages)]
+    vmem = pl.BlockSpec(memory_space=pltpu.VMEM)
+    return pl.pallas_call(
+        functools.partial(reduce_kernel, size, places, pair_rows),
+        out_shape=(jax.ShapeDtypeStruct((rows, total_width), jnp.float32), jax.ShapeDtypeStruct(small.shape, jnp.float32)),
+        in_specs=[vmem] * (len(grads) + 1),
+        out_specs=(vmem, vmem),
+        scratch_shapes=halves
+        + halves[1:]
+        + [pltpu.VMEM((stages + 1,) + small.shape, jnp.float32)] * 2
+        + [pltpu.SemaphoreType.DMA((chunks, stages))] * 2
+        + [pltpu.SemaphoreType.DMA((stages + 1,))] * 2,
+        compiler_params=pltpu.CompilerParams(
+            collective_id=1, has_side_effects=True, vmem_limit_bytes=60 * 1024 * 1024
+        ),
+        name="reduce_rows",
+    )(*[grad.reshape(size, rows, grad.shape[1]) for grad in grads], small)
+
+
+def finish_sums(grads, small, pair_rows):
+    if grads[0].shape[0] // lax.axis_size("batch") % 16 == 0 and not any(grad.shape[1] % chunk_width for grad in grads):
+        return reduce_rows(grads, small, pair_rows)
+    small, _ = exchange(small, "batch")
+    paired, _ = exchange(small[:pair_rows], "tensor")
+    return scatter_batch(jnp.concatenate(grads, axis=1)), jnp.concatenate([paired, small[pair_rows:]])
 
 
 def relative_table(slot_frames, model_width):
@@ -247,12 +407,23 @@
     pre_peer = (times_transposed(grad_peer, weight_down) * slope_peer.astype(jnp.float32)).astype(jnp.bfloat16)
     back_peer = times_transposed(pre_peer, weight_up)
     back_own = times_transposed(pre_own, weight_up)
-    grad_down = contract_rows(grad_own, hidden_own) + contract_rows(grad_peer, hidden_peer)
-    grad_up = contract_rows(act_own, pre_own) + contract_rows(act_peer, pre_peer)
+
+    def grad_down(tie, begin=0, end=None):
+        own, peer = hidden_own, hidden_peer
+        if tie is not None:
+            own, peer = after((own, peer), tie)
+        return (contract_rows(grad_own, own[:, begin:end]) + contract_rows(grad_peer, peer[:, begin:end])).astype(jnp.bfloat16)
+
+    def grad_up(tie, begin=0, end=None):
+        own, peer = act_own, act_peer
+        if tie is not None:
+            own, peer = after((own, peer), tie)
+        return (contract_rows(own, pre_own[:, begin:end]) + contract_rows(peer, pre_peer[:, begin:end])).astype(jnp.bfloat16)
+
     grad_resid, grad_gain, grad_shift = norm_backward(
         narrow(back_own, back_peer), scaled, inv_std, norm_gain
     )
-    return (grad_resid, grad_gain, grad_shift, scatter_mixed(grad_up, "x"), scatter_mixed(grad_down, "y").T)
+    return (grad_resid, grad_gain, grad_shift, grad_up, grad_down)
 
 
 def attn_forward(
@@ -340,9 +511,7 @@
         sum(times_transposed(half[side], attention_in[at]) for at, half in enumerate(halves))
         for side in (0, 1)
     )
-    grad_in_proj = jnp.concatenate([contract_rows(flat_act, part) for part in grad_proj], axis=1)
-    grad_in_proj = scatter_batch(grad_in_proj, "y")
-    grad_in_proj = jnp.stack(jnp.split(grad_in_proj, 3, axis=1))
+    grad_in_proj = [contract_rows(flat_act, part).astype(jnp.bfloat16) for part in grad_proj]
     grad_table_proj = contract_rows(table_in, grad_table)
     grad_resid, grad_gain, grad_shift = norm_backward(
         narrow(back_own, back_peer), scaled, inv_std, norm_gain
@@ -352,9 +521,9 @@
         grad_gain,
         grad_shift,
         grad_in_proj,
-        scatter_batch(grad_table_proj, "z"),
+        grad_table_proj,
         grad_bias,
-        scatter_batch(grad_back_proj, "z").T,
+        grad_back_proj,
     )
 
 
@@ -367,7 +536,7 @@
     batch_gain,
     batch_shift,
     pointwise_out,
-    frame_count,
+    slot_count,
     live_full,
 ):
     normed, scaled, inv_std = norm_forward(residual, norm_gain, norm_shift)
@@ -387,10 +556,17 @@
     mixed_conv = padded[0:slot_frames] * kernel[0]
     for tap_index in range(1, tap_count):
         mixed_conv = mixed_conv + padded[tap_index : tap_index + slot_frames] * kernel[tap_index]
-    totals = exchange(
-        jnp.stack([jnp.sum(mixed_conv * live_full, axis=0), jnp.sum(mixed_conv * mixed_conv * live_full, axis=0)]),
+    totals, _ = exchange(
+        jnp.stack(
+            [
+                jnp.sum(mixed_conv * live_full, axis=0),
+                jnp.sum(mixed_conv * mixed_conv * live_full, axis=0),
+                jnp.broadcast_to(slot_count, (channels,)),
+            ]
+        ),
         "batch",
     )
+    frame_count = totals[2, 0]
     batch_mean = totals[0] / frame_count
     batch_inv = lax.rsqrt(totals[1] / frame_count - batch_mean * batch_mean + eps_batch)
     centered = (mixed_conv - batch_mean) * batch_inv
@@ -418,7 +594,7 @@
 
 
 def conv_backward(
-    grad_after, saved, norm_gain, pointwise_in, depthwise, batch_gain, pointwise_out, live_full
+    grad_after, saved, norm_gain, pointwise_in, depthwise, batch_gain, pointwise_out, live_full, fillers
 ):
     (
         scaled,
@@ -437,11 +613,11 @@
     grad_own = grad_after.astype(jnp.bfloat16)
     grad_flat = in_order(grad_own, swap(grad_own))
     slot_frames = grad_flat.shape[0]
-    grad_point_out = scatter_batch(contract_rows(grad_flat, swished), "x").T
+    grad_point_out = contract_rows(grad_flat, swished)
     grad_swished = times_transposed(grad_flat, pointwise_out)
     grad_normed = grad_swished * batch_sig * (1.0 + normed_batch * (1.0 - batch_sig))
-    sums = exchange(
-        jnp.stack([jnp.sum(grad_normed, axis=0), jnp.sum(grad_normed * centered, axis=0)]), "batch"
+    sums, filled = exchange(
+        jnp.stack([jnp.sum(grad_normed, axis=0), jnp.sum(grad_normed * centered, axis=0)]), "batch", fillers
     )
     gamma = batch_gain.astype(jnp.float32)
     grad_mixed = batch_inv * (
@@ -468,9 +644,7 @@
         (grad_gated * gate_sig).astype(jnp.bfloat16),
         (grad_gated * both_halves[0] * gate_sig * (1.0 - gate_sig)).astype(jnp.bfloat16),
     ]
-    grad_point_in = jnp.concatenate([contract_rows(flat_act, part) for part in grad_halves], axis=1)
-    grad_point_in = scatter_batch(grad_point_in, "x")
-    grad_point_in = grad_point_in.reshape(grad_point_in.shape[0], 2, channels)
+    grad_point_in = [contract_rows(flat_act, part) for part in grad_halves]
     halves = [split_own(part) for part in grad_halves]
     back_own, back_peer = (
         sum(times_transposed(half[side], pointwise_in[:, at]) for at, half in enumerate(halves))
@@ -479,7 +653,7 @@
     grad_resid, grad_gain, grad_shift = norm_backward(
         narrow(back_own, back_peer), scaled, inv_std, norm_gain
     )
-    return (grad_resid, grad_gain, grad_shift, grad_point_in, grad_point_out, grad_kernel, sums)
+    return (grad_resid, grad_gain, grad_shift, grad_point_in, grad_point_out, grad_kernel, sums, filled)
 
 
 def per_device(
@@ -508,7 +682,6 @@
     live_half = (positions < lengths[0]).astype(jnp.float32)
     full_positions = lax.broadcasted_iota(jnp.int32, (slot_frames, 1), 0)
     live_full = (full_positions < lengths[0]).astype(jnp.float32)
-    frame_count = exchange(jnp.broadcast_to(lengths.astype(jnp.float32), (8, 128)), "batch")[0, 0]
     gain_rows = norm_gains.astype(jnp.float32)
     shift_rows = norm_shifts.astype(jnp.float32)
     stream_zero = features[0].astype(jnp.float32)
@@ -536,7 +709,7 @@
         batch_gain,
         batch_shift,
         pointwise_out,
-        frame_count,
+        lengths[0].astype(jnp.float32),
         live_full,
     )
     stream_three = stream_two + branch_three
@@ -554,18 +727,29 @@
         0.5 * grad_stream, saved_four, gain_rows[3], second_up, second_down
     )
     grad_stream = grad_stream + grad_branch
-    grad_branch, gain_three, shift_three, point_in_grad, point_out_grad, kernel_grad, batch_sums = (
-        conv_backward(
-            grad_stream,
-            saved_three,
-            gain_rows[2],
-            pointwise_in,
-            depthwise,
-            batch_gain,
-            pointwise_out,
-            live_full,
-        )
-    )
+    early = second_up.shape[1] // 2
+    (
+        grad_branch,
+        gain_three,
+        shift_three,
+        point_in_grad,
+        point_out_grad,
+        kernel_grad,
+        batch_sums,
+        (down_two, (up_two, up_rest)),
+    ) = conv_backward(
+        grad_stream,
+        saved_three,
+        gain_rows[2],
+        pointwise_in,
+        depthwise,
+        batch_gain,
+        pointwise_out,
+        live_full,
+        [down_two, lambda tie: (up_two(tie, 0, early), up_two(tie, early))],
+    )
+    down_two, up_two = scatter_batch(down_two).T, scatter_batch(up_two)
+    points = [part.astype(jnp.bfloat16) for part in (*point_in_grad, point_out_grad)]
     grad_stream = grad_stream + grad_branch
     grad_branch, gain_two, shift_two, heads_grad, table_grad, bias_grad, back_grad = attn_backward(
         grad_stream,
@@ -581,17 +765,43 @@
         0.5 * grad_stream, saved_one, gain_rows[0], first_up, first_down
     )
     grad_stream = grad_stream + grad_branch
-    early = exchange(
-        exchange(jnp.stack([gain_two, gain_three, gain_four, gain_five, shift_two, shift_three, shift_four, shift_five]), "batch"),
-        "tensor",
-    )
-    late = exchange(exchange(jnp.stack([gain_one, shift_one]), "batch"), "tensor")
-    gain_grads = jnp.concatenate([late[:1], early[:4]])
-    shift_grads = jnp.concatenate([late[1:], early[4:]])
-    channels = kernel_grad.shape[1]
-    head_grads = exchange(jnp.concatenate([kernel_grad, bias_grad.reshape(2, channels)]), "batch")
-    kernel_grad = head_grads[:-2]
-    bias_grad = head_grads[-2:].reshape(bias_grad.shape)
+    up_one, down_one = up_one(None), down_one(None)
+    gain_grads = jnp.stack([gain_one, gain_two, gain_three, gain_four, gain_five])
+    shift_grads = jnp.stack([shift_one, shift_two, shift_three, shift_four, shift_five])
+    norms, channels = gain_grads.shape[0], kernel_grad.shape[1]
+    packed = jnp.concatenate([kernel_grad, bias_grad.reshape(2, channels)]).reshape(-1)
+    packed = jnp.pad(packed, (0, -packed.shape[0] % (8 * model_width))).reshape(-1, model_width)
+    pair_rows = 2 * norms + -2 * norms % 8
+    norm_grads = jnp.pad(jnp.concatenate([gain_grads, shift_grads]), ((0, pair_rows - 2 * norms), (0, 0)))
+    sums, small = finish_sums(
+        [
+            *points,
+            up_rest,
+            *heads_grad,
+            table_grad.astype(jnp.bfloat16),
+            back_grad.astype(jnp.bfloat16),
+            up_one,
+            down_one,
+        ],
+        jnp.concatenate([norm_grads, packed]),
+        pair_rows,
+    )
+    gain_grads, shift_grads = small[:norms], small[norms : 2 * norms]
+    packed = small[pair_rows:].reshape(-1)
+    kernel_grad = packed[: kernel_grad.size].reshape(kernel_grad.shape)
+    bias_grad = packed[kernel_grad.size : kernel_grad.size + bias_grad.size].reshape(bias_grad.shape)
+    def take(part):
+        nonlocal sums
+        taken, sums = sums[:, : part.shape[1]], sums[:, part.shape[1] :]
+        return taken
+
+    value_point, gate_point, point_out_grad = [take(part) for part in points]
+    point_in_grad = jnp.stack([value_point, gate_point], axis=1)
+    point_out_grad = point_out_grad.T
+    up_two = jnp.concatenate([up_two, take(up_rest)], axis=1)
+    heads_grad = jnp.stack([take(part) for part in heads_grad])
+    table_grad, back_grad = take(table_grad), take(back_grad).T
+    up_one, down_one = take(up_one), take(down_one).T
     return (
         output[None],
         grad_stream[None],

time: 664 us -> 554 us (0.83)
  waiting for transfers between devices: 243 us -> 24.2 us
  Pallas kernels: 46.3 us -> 236 us
  starting transfers between devices: 108 us -> 21 us
  between operations: 4.11 us -> 16.8 us
  other arithmetic: 58.8 us -> 50.6 us
    ppermute x52 -> x0, waiting for transfers between devices: 215 us -> none  [halve(): lax.ppermute(outgoing, 'batch', [(at, at ^ 2 ** bit) for at in range(size)])]
    pallas_call x0 -> x1, Pallas kernels: none -> 190 us  [reduce_rows(): pl.pallas_call(functools.partial(reduce_kernel, size, places, pair_rows),...]
    ppermute x52 -> x0, starting transfers between devices: 59 us -> none  [halve(): lax.ppermute(outgoing, 'batch', [(at, at ^ 2 ** bit) for at in range(size)])]
    ppermute x38 -> x12, starting transfers between devices: 46.1 us -> 16.8 us  [exchange(): lax.ppermute(values, axis, [(at, at ^ reach * other) for at in range(size)])]
    ppermute x38 -> x12, waiting for transfers between devices: 21.2 us -> 7.32 us  [exchange(): lax.ppermute(values, axis, [(at, at ^ reach * other) for at in range(size)])]
    dot_general x16 -> x18, matrix products: 57.9 us -> 68.6 us  [contract_rows(): lax.dot_general(left, right, (((0,), (0,)), ((), ())), preferred_element_...]
    ppermute x16, waiting for transfers between devices: 6.64 us -> 16.8 us  [swap(): return lax.ppermute(half, 'tensor', [(0, 1), (1, 0)])]
    convert_element_type x39 -> x1, other arithmetic: 10 us -> 0.92 us  [scatter_batch(): return lax.psum_scatter(grad.astype(jnp.bfloat16), 'batch', scatter_dimen...]
  transfers between devices with their start and end apart: 106 -> 30, of which waited for: 44 -> 12; matrix products, arithmetic and copies ran while one was open for 25% -> 29% of each run, Pallas kernels for 0% -> 40%
where the time goes in v3:
time: 554 us; the launch traced here: 544 us
  Pallas kernels  236 us (43%)
  matrix products  166 us (30%)
  other arithmetic  50.6 us (9%)
  local copies, waits for them, and re-layouts  29.7 us (5%)
  waiting for transfers between devices  24.2 us (4%)
  starting transfers between devices  21 us (4%)
  between operations  16.8 us (3%)
    pallas_call x1, Pallas kernels, reduce_rows(): pl.pallas_call(functools.partial(reduce_kernel, size, places, pair_rows),...  190 us
    dot_general x18, matrix products, contract_rows(): lax.dot_general(left, right, (((0,), (0,)), ((), ())), preferred_element_...  68.6 us
    dot_general x20, matrix products, times_transposed(): lax.dot_general(left, right, (((1,), (1,)), ((), ())), preferred_element_...  48.8 us
    pallas_call x1, Pallas kernels, attend_back(): pl.pallas_call(functools.partial(attend_back_kernel, frames, block), out_...  25.5 us
    pallas_call x1, Pallas kernels, attend(): pl.pallas_call(functools.partial(attend_kernel, frames, block), out_shape...  20.5 us
    dot_general x4, matrix products, hidden_of(): pre_act = jnp.dot(act, weight_up, preferred_element_type=jnp.float32)  16.9 us
    ppermute x12, starting transfers between devices, exchange(): lax.ppermute(values, axis, [(at, at ^ reach * other) for at in range(size)])  16.8 us
    ppermute x16, waiting for transfers between devices, swap(): return lax.ppermute(half, 'tensor', [(0, 1), (1, 0)])  16.8 us
  transfers between devices with their start and end apart: 30, of which 12 were waited for; matrix products, arithmetic and copies ran while one was open for 29% of the time, Pallas kernels for 40%

profile of v3, /device:TPU:0, one launch (start us, length us, event | category | flops | bytes accessed | tf_op | source)
XLA Modules:
  0.0 543.8 jit_solution(12136479741535428778)
XLA Ops:
  15.1 4.9 fusion.120
  35.7 4.1 convolution_convert_fusion.table
  49.1 20.5 %attend.1 = (bf16[1024,512]{1,0:T(8,128)(2,1)}, bf16[4,1024,1024]{2,1,0:T(8,128)(2,1)}) custom-call(s32[1]{0:T(128)} %copy.57.lengths, bf16[1024,512]{1,0:T(8,128)(2,1)} %get-tuple-element.158.content, bf16[1024,512]{1,0:T(8,128)(2,1)} %get-tuple-element.157.position, bf16[1024,512]{1,0:T(8,128)(2,1)} %convolution_convert_fusion.10.keys, ...), custom_call_target="tpu_custom_call" | custom-call | tf_op jit(solution)/shard_map/attend/pallas_call | solution.py:321
  74.2 3.1 fusion.117
  79.7 5.6 %fusion.110 = (bf16[1024,1,512]{2,1,0:T(2,128)(2,1)S(1)}, bf16[1024,1,512]{2,1,0:T(2,128)(2,1)S(1)}) fusion(bf16[1024,2,512]{2,1,0:T(2,128)(2,1)} %param.32), kind=kLoop, calls=%fused_computation.272 | loop fusion | bytes 4194304 | tf_op jit(solution)/shard_map/slice | solution.py:547
  94.5 2.9 collective-permute-start.6
  99.0 2.9 collective-permute-done.7
  102.5 3.6 collective-permute-start.10
  120.8 4.8 multiply_convert_fusion.8
  128.2 4.8 multiply_convert_fusion.9
  142.3 5.2 multiply_convert_fusion.4
  150.4 5.2 multiply_convert_fusion.6
  155.6 3.5 multiply_reduce_fusion.5
  159.2 3.3 fusion.108
  165.5 3.5 fusion.106
  175.0 4.7 add_convert_fusion.2
  194.2 9.2 %multiply_reduce_fusion = (f32[512]{0:T(512)S(1)}, f32[512]{0:T(512)S(1)}, f32[512]{0:T(512)S(1)}, f32[512]{0:T(512)S(1)}, f32[512]{0:T(512)S(1)}, /*index=5*/f32[1024,512]{1,0:T(8,128)S(1)}) fusion(f32[1024,512]{1,0:T(8,128)} %copy-done.5, f32[]{:T(128)} %bitcast.23, f32[512]{0:T(512)S(1)} %bitcast.293, f32[1024,512]{1,0:T(8,128)} %copy-done.4, ...), kind=kLoop, calls=%fused_computation.57 | loop fusion | flops 10483200 | bytes 8413188 | tf_op jit(solution)/shard_map/reduce_sum | solution.py:633
  220.8 3.6 convolution_convert_fusion.7
  232.7 25.5 %attend_back.1 = (bf16[1024,512]{1,0:T(8,128)(2,1)}, bf16[1024,512]{1,0:T(8,128)(2,1)}, bf16[1024,512]{1,0:T(8,128)(2,1)}, bf16[2048,512]{1,0:T(8,128)(2,1)}, f32[8,512]{1,0:T(8,128)}) custom-call(bf16[4,1024,1024]{2,1,0:T(8,128)(2,1)} %get-tuple-element.50.probs, bf16[1024,512]{1,0:T(8,128)(2,1)} %convolution_convert_fusion.8.grad_context, ...), custom_call_target="tpu_custom_call" | custom-call | tf_op jit(solution)/shard_map/attend_back/pallas_call | solution.py:372
  258.2 3.6 convolution_convert_fusion.4
  272.6 4.4 convolution_convert_fusion.2
  277.0 3.4 convolution_convert_fusion.13
  280.4 3.0 multiply_reduce_fusion.7
  287.7 3.3 multiply_convert_fusion.2
  291.1 5.7 %fusion.122 = f32[1024,2048]{1,0:T(8,128)} fusion(bf16[512,1024]{1,0:T(8,128)(2,1)S(1)} %copy-done.51, bf16[512,2048]{1,0:T(8,128)(2,1)S(1)} %multiply_convert_fusion.2), kind=kOutput, calls=%fused_computation.284 | convolution fusion | flops 2147483648 | bytes 11534336 | tf_op jit(solution)/shard_map/dot_general | solution.py:17
  296.8 5.8 %fusion.104 = f32[1024,2048]{1,0:T(8,128)} fusion(bf16[512,1024]{1,0:T(8,128)(2,1)S(1)} %get-tuple-element.125, f32[512,2048]{1,0:T(8,128)S(1)} %copy-done.118), kind=kOutput, calls=%fused_computation.266 | convolution fusion | flops 2152726528 | bytes 13631488 | tf_op jit(solution)/shard_map/dot_general | solution.py:17
  302.6 3.1 multiply_convert_fusion
  305.7 3.3 convolution_convert_fusion.14
  310.2 8.7 %add_convert_fusion.1 = bf16[1024,2048]{1,0:T(8,128)(2,1)} fusion(f32[1024,2048]{1,0:T(8,128)} %fusion.122, bf16[512,1024]{1,0:T(8,128)(2,1)S(1)} %copy-done.108, bf16[512,2048]{1,0:T(8,128)(2,1)} %copy-done.113), kind=kOutput, calls=%fused_computation.1 | convolution fusion | flops 2151677952 | bytes 15728640 | tf_op jit(solution)/shard_map/dot_general | solution.py:17
  319.2 8.1 %add_convert_fusion = bf16[1024,2048]{1,0:T(8,128)(2,1)} fusion(f32[1024,2048]{1,0:T(8,128)} %fusion.104, bf16[512,1024]{1,0:T(8,128)(2,1)S(1)} %copy-done.110, f32[512,2048]{1,0:T(8,128)S(1)} %copy-done.116), kind=kOutput, calls=%fused_computation | convolution fusion | flops 2156920832 | bytes 17825792 | tf_op jit(solution)/shard_map/dot_general | solution.py:17
  327.4 4.2 fusion.15
  332.4 189.5 %reduce_rows.1 = (f32[64,9216]{1,0:T(8,128)}, f32[24,1024]{1,0:T(8,128)}) custom-call(bf16[16,64,512]{2,1,0:T(8,128)(2,1)} %bitcast.236, bf16[16,64,512]{2,1,0:T(8,128)(2,1)} %bitcast.237, bf16[16,64,512]{2,1,0:T(8,128)(2,1)} %bitcast.235, bf16[16,64,1024]{2,1,0:T(8,128)(2,1)} %bitcast.230, bf16[16,64,512]{2,1,0:T(8,128)(2,1)} %bitcast.239, ...), custom_call_target="tpu_custom_call" | custom-call | tf_op jit(solution)/shard_map/reduce_rows/pallas_call | solution.py:252
  (415 shorter events, 159.9 us)
Async XLA Ops:
  7.2 105.4 %copy-start = (bf16[512,1024]{1,0:T(8,128)(2,1)S(1)}, bf16[512,1024]{1,0:T(8,128)(2,1)}, u32[]{:S(2)}) copy-start(bf16[512,1024]{1,0:T(8,128)(2,1)} %param.36) | copy-start | bytes 3145732
  7.2 302.0 %reduce-scatter.3.cloned.1.call-start = ((), (), s32[]{:S(2)}) async-start(), calls=%async_computation.2 | async-start | bytes 2228224 | tf_op jit(solution)/shard_map/reduce_scatter | solution.py:92
  12.2 2.8 collective-permute-start
  22.5 3.7 collective-permute-start.1
  31.3 8.5 %collective-permute-start.2 = (bf16[512,1024]{1,0:T(8,128)(2,1)}, bf16[512,1024]{1,0:T(8,128)(2,1)}, u32[]{:S(2)}, u32[]{:S(2)}) collective-permute-start(bf16[512,1024]{1,0:T(8,128)(2,1)} %add_convert_fusion.11), channel_id=1, source_target_pairs={{0,1},{1,0},{2,3},{3,2},{4,5},{5,4},{6,7},{7,6},{8,9},{9,8},{10,11... | collective-permute-start | bytes 3145736 | tf_op jit(solution)/shard_map/ppermute | solution.py:46
  71.4 2.9 collective-permute-start.3
  79.4 5.9 %collective-permute-start.4 = (bf16[512,1024]{1,0:T(8,128)(2,1)}, bf16[512,1024]{1,0:T(8,128)(2,1)}, u32[]{:S(2)}, u32[]{:S(2)}) collective-permute-start(bf16[512,1024]{1,0:T(8,128)(2,1)} %add_convert_fusion.8), channel_id=1, source_target_pairs={{0,1},{1,0},{2,3},{3,2},{4,5},{5,4},{6,7},{7,6},{8,9},{9,8},{10,11... | collective-permute-start | bytes 3145736 | tf_op jit(solution)/shard_map/ppermute | solution.py:46
  94.4 71.1 %copy-start.4 = (f32[1024,512]{1,0:T(8,128)}, f32[1024,512]{1,0:T(8,128)S(1)}, u32[]{:S(2)}) copy-start(f32[1024,512]{1,0:T(8,128)S(1)} %get-tuple-element.137) | copy-start | bytes 6291460
  94.5 4.5 collective-permute-start.6
  97.4 4.5 collective-permute-start.7
  98.8 3.7 collective-permute-start.5
  102.5 5.5 %collective-permute-start.10 = (f32[3,512]{1,0:T(4,128)S(1)}, f32[3,512]{1,0:T(4,128)S(1)}, u32[]{:S(2)}, u32[]{:S(2)}) collective-permute-start(f32[3,512]{1,0:T(4,128)S(1)} %add_add_fusion.3), channel_id=1, source_target_pairs={{0,24},{2,26},{4,28},{6,30},{8,16},{10,18},{12,20},{14,22},{16,8},... | collective-permute-start | bytes 18440 | tf_op jit(solution)/shard_map/ppermute | solution.py:78
  106.2 4.5 collective-permute-start.9
  106.2 4.5 collective-permute-start.8
  113.3 2.7 collective-permute-start.11
  118.1 2.7 collective-permute-start.12
  128.0 5.0 collective-permute-start.13
  139.6 2.7 collective-permute-start.14
  149.9 5.7 %collective-permute-start.15 = (bf16[512,1024]{1,0:T(8,128)(2,1)S(1)}, bf16[512,1024]{1,0:T(8,128)(2,1)S(1)}, u32[]{:S(2)}, u32[]{:S(2)}) collective-permute-start(bf16[512,1024]{1,0:T(8,128)(2,1)S(1)} %convolution_convert_fusion.15), channel_id=1, source_target_pairs={{0,1},{1,0},{2,3},{3,2},{4,5},{5,4},{6,7},{7,6},{8,9},{9,8},{10,11... | collective-permute-start | bytes 3145736 | tf_op jit(solution)/shard_map/ppermute | solution.py:46
  162.5 2.7 collective-permute-start.16
  169.0 10.6 %collective-permute-start.19 = (f32[2,512]{1,0:T(2,128)S(1)}, f32[2,512]{1,0:T(2,128)S(1)}, u32[]{:S(2)}, u32[]{:S(2)}) collective-permute-start(f32[2,512]{1,0:T(2,128)S(1)} %pad_maximum_fusion.11), channel_id=1, source_target_pairs={{0,6},{2,4},{4,2},{6,0},{8,14},{10,12},{12,10},{14,8},{16,22},{18,... | collective-permute-start | bytes 12296 | tf_op jit(solution)/shard_map/ppermute | solution.py:78
  170.5 9.1 %collective-permute-start.18 = (f32[2,512]{1,0:T(2,128)S(1)}, f32[2,512]{1,0:T(2,128)S(1)}, u32[]{:S(2)}, u32[]{:S(2)}) collective-permute-start(f32[2,512]{1,0:T(2,128)S(1)} %pad_maximum_fusion.11), channel_id=1, source_target_pairs={{0,4},{2,6},{4,0},{6,2},{8,12},{10,14},{12,8},{14,10},{16,20},{18,... | collective-permute-start | bytes 12296 | tf_op jit(solution)/shard_map/ppermute | solution.py:78
  171.5 8.2 %collective-permute-start.17 = (f32[2,512]{1,0:T(2,128)S(1)}, f32[2,512]{1,0:T(2,128)S(1)}, u32[]{:S(2)}, u32[]{:S(2)}) collective-permute-start(f32[2,512]{1,0:T(2,128)S(1)} %pad_maximum_fusion.11), channel_id=1, source_target_pairs={{0,2},{2,0},{4,6},{6,4},{8,10},{10,8},{12,14},{14,12},{16,18},{18,... | collective-permute-start | bytes 12296 | tf_op jit(solution)/shard_map/ppermute | solution.py:78
  179.7 14.3 %collective-permute-start.22 = (f32[2,512]{1,0:T(2,128)S(1)}, f32[2,512]{1,0:T(2,128)S(1)}, u32[]{:S(2)}, u32[]{:S(2)}) collective-permute-start(f32[2,512]{1,0:T(2,128)S(1)} %add_add_fusion.5), channel_id=1, source_target_pairs={{0,24},{2,26},{4,28},{6,30},{8,16},{10,18},{12,20},{14,22},{16,8},... | collective-permute-start | bytes 12296 | tf_op jit(solution)/shard_map/ppermute | solution.py:78
  181.2 12.8 %collective-permute-start.21 = (f32[2,512]{1,0:T(2,128)S(1)}, f32[2,512]{1,0:T(2,128)S(1)}, u32[]{:S(2)}, u32[]{:S(2)}) collective-permute-start(f32[2,512]{1,0:T(2,128)S(1)} %add_add_fusion.5), channel_id=1, source_target_pairs={{0,16},{2,18},{4,20},{6,22},{8,24},{10,26},{12,28},{14,30},{16,0},... | collective-permute-start | bytes 12296 | tf_op jit(solution)/shard_map/ppermute | solution.py:78
  181.8 12.2 %collective-permute-start.20 = (f32[2,512]{1,0:T(2,128)S(1)}, f32[2,512]{1,0:T(2,128)S(1)}, u32[]{:S(2)}, u32[]{:S(2)}) collective-permute-start(f32[2,512]{1,0:T(2,128)S(1)} %add_add_fusion.5), channel_id=1, source_target_pairs={{0,8},{2,10},{4,12},{6,14},{8,0},{10,2},{12,4},{14,6},{16,24},{18,... | collective-permute-start | bytes 12296 | tf_op jit(solution)/shard_map/ppermute | solution.py:78
  194.1 340.6 %reduce-scatter.5.cloned.1.call-start = ((), (), s32[]{:S(2)}) async-start(), calls=%async_computation.3 | async-start | bytes 4456448 | tf_op jit(solution)/shard_map/reduce_scatter | solution.py:92
  210.2 2.7 collective-permute-start.23
  216.8 9.8 %collective-permute-start.24 = (bf16[512,1024]{1,0:T(8,128)(2,1)S(1)}, bf16[512,1024]{1,0:T(8,128)(2,1)}, u32[]{:S(2)}, u32[]{:S(2)}) collective-permute-start(bf16[512,1024]{1,0:T(8,128)(2,1)S(1)} %get-tuple-element.127), channel_id=1, source_target_pairs={{0,1},{1,0},{2,3},{3,2},{4,5},{5,4},{6,7},{7,6},{8,9},{9,8},{10,11... | collective-permute-start | bytes 3145736 | tf_op jit(solution)/shard_map/ppermute | solution.py:46
  269.4 11.0 %collective-permute-start.25 = (bf16[512,1024]{1,0:T(8,128)(2,1)}, bf16[512,1024]{1,0:T(8,128)(2,1)S(1)}, u32[]{:S(2)}, u32[]{:S(2)}) collective-permute-start(bf16[512,1024]{1,0:T(8,128)(2,1)} %add_convert_fusion.5), channel_id=1, source_target_pairs={{0,1},{1,0},{2,3},{3,2},{4,5},{5,4},{6,7},{7,6},{8,9},{9,8},{10,11... | collective-permute-start | bytes 3145736 | tf_op jit(solution)/shard_map/ppermute | solution.py:46
  285.6 17.0 %collective-permute-start.26 = (bf16[512,1024]{1,0:T(8,128)(2,1)S(1)}, bf16[512,1024]{1,0:T(8,128)(2,1)S(1)}, u32[]{:S(2)}, u32[]{:S(2)}) collective-permute-start(bf16[512,1024]{1,0:T(8,128)(2,1)S(1)} %get-tuple-element.125), channel_id=1, source_target_pairs={{0,1},{1,0},{2,3},{3,2},{4,5},{5,4},{6,7},{7,6},{8,9},{9,8},{10,11... | collective-permute-start | bytes 3145736 | tf_op jit(solution)/shard_map/ppermute | solution.py:46
  309.1 18.2 %collective-permute-start.27 = (bf16[512,1024]{1,0:T(8,128)(2,1)}, bf16[512,1024]{1,0:T(8,128)(2,1)S(1)}, u32[]{:S(2)}, u32[]{:S(2)}) collective-permute-start(bf16[512,1024]{1,0:T(8,128)(2,1)} %convolution_convert_fusion.14), channel_id=1, source_target_pairs={{0,1},{1,0},{2,3},{3,2},{4,5},{5,4},{6,7},{7,6},{8,9},{9,8},{10,11... | collective-permute-start | bytes 3145736 | tf_op jit(solution)/shard_map/ppermute | solution.py:46
  (117 other events, 641.3 us)
Sparse Core Ops, SparseCore 0:
  194.2 79.7 reduce-scatter.2
  276.3 113.3 reduce-scatter.4

commit v4 on v3

--- a/solution.py
+++ b/solution.py
@@ -64,13 +64,8 @@
     return own + swap(peer.astype(jnp.bfloat16)).astype(jnp.float32)
 
 
-def after(value, tie):
-    return lax.optimization_barrier((value, tie))[0]
-
-
-def exchange(values, axis, fillers=()):
+def exchange(values, axis):
     size = lax.axis_size(axis)
-    fillers, filled = list(fillers), []
     reach = 1
     while reach < size:
         radix = 4 if size % (reach * 4) == 0 else 2
@@ -78,14 +73,9 @@
             lax.ppermute(values, axis, [(at, at ^ (reach * other)) for at in range(size)])
             for other in range(1, radix)
         ]
-        if fillers:
-            *got, work = lax.optimization_barrier((*got, fillers.pop(0)(values)))
-            filled.append(work)
         values = sum(got, values)
         reach *= radix
-    for filler in fillers:
-        filled.append(filler(values))
-    return values, filled
+    return values
 
 
 def scatter_batch(grad):
@@ -95,18 +85,21 @@
 
 
 chunk_width = 512
-
-
-def reduce_plan(size, chunk_count):
+block_rows = 256
+
+
+def reduce_plan(size, ready, made):
     bits = list(range(size.bit_length() - 1))
     kinds = (bits, [1, 0] + bits[2:], bits[2:] + bits[:2])
+    chunk_count = ready + made
     few = max(1, round(chunk_count * 2 / 9))
-    orders = []
+    orders, turn = [], 0
     for at in range(chunk_count):
-        orders.append(kinds[2] if at % 4 == 3 and sum(o is kinds[2] for o in orders) < few else None)
-    plain = [at for at in range(chunk_count) if orders[at] is None]
-    for turn, at in enumerate(plain):
-        orders[at] = kinds[turn % 2]
+        if at % 4 == 3 and sum(order is kinds[2] for order in orders) < few:
+            orders.append(kinds[2])
+        else:
+            orders.append(kinds[turn % 2])
+            turn += 1
     free, arrivals, events = {}, [], []
 
     def issue(chunk, stage, now):
@@ -122,8 +115,10 @@
         arrivals.append((free[link] + 0.1, -1, stage))
 
     issue_small(0, 0.0)
-    for chunk in range(chunk_count):
+    for chunk in range(ready):
         issue(chunk, 0, 0.0)
+    for chunk in range(ready, chunk_count):
+        arrivals.append((0.1 * (chunk - ready + 1), chunk, -1))
     while arrivals:
         arrivals.sort()
         now, chunk, stage = arrivals.pop(0)
@@ -135,15 +130,16 @@
     return orders, events
 
 
-def reduce_kernel(size, places, pair_rows, *refs):
+def reduce_kernel(size, ready, pieces, pair_rows, count, *refs):
     stages = size.bit_length() - 1
-    orders, events = reduce_plan(size, len(places))
-    count = max(at for at, _ in places) + 1
-    grads, small, out, small_out = refs[:count], refs[count], refs[count + 1], refs[count + 2]
-    refs = refs[count + 3 :]
-    landed = refs[:stages]
-    leaving = (None,) + tuple(refs[stages : 2 * stages - 1])
-    small_sum, small_landed, sent, arrived, small_sent, small_arrived = refs[2 * stages - 1 :]
+    chunks = ready + len(pieces)
+    orders, events = reduce_plan(size, ready, len(pieces))
+    sources, refs = refs[:count], refs[count:]
+    given, small, out, small_out = refs[:ready], refs[ready], refs[ready + 1], refs[ready + 2]
+    refs = refs[ready + 3 :]
+    grads, left_buffer, right_buffer = refs[:3]
+    landed = refs[3 : 3 + stages]
+    small_sum, small_landed, sent, arrived, small_sent, small_arrived, left_sem, right_sem = refs[3 + stages :]
     rows = out.shape[0]
     me = lax.axis_index("batch")
     mine = [lax.rem(me // 2**bit, 2) for bit in range(stages)]
@@ -151,20 +147,47 @@
     def shard(block):
         return sum(2**bit * lax.rem(mine[bit] + (block >> bit) % 2, 2) for bit in range(stages))
 
+    def fetches(at):
+        left, right, begin, group = pieces[at]
+        copies, first = [], 0
+        for part, source in enumerate(right):
+            length = sources[source].shape[0]
+            copies.append(
+                pltpu.make_async_copy(
+                    sources[source].at[:, pl.ds(begin, chunk_width)],
+                    right_buffer.at[at % 2, pl.ds(first, length)],
+                    right_sem.at[at % 2, part],
+                )
+            )
+            first += length
+        if at == 0 or pieces[at - 1][3] != group:
+            first = 0
+            for part, source in enumerate(left):
+                length = sources[source].shape[0]
+                copies.append(
+                    pltpu.make_async_copy(
+                        sources[source], left_buffer.at[group % 2, pl.ds(first, length)], left_sem.at[group % 2, part]
+                    )
+                )
+                first += length
+        return copies
+
+    for fetch in fetches(0):
+        fetch.start()
+    peer = {"tensor": 1 - lax.axis_index("tensor")}
     barrier = pltpu.get_barrier_semaphore()
-    for bit in range(stages):
-        pl.semaphore_signal(barrier, inc=1, device_id={"batch": shard(2**bit)}, device_id_type=pl.DeviceIdType.MESH)
-    peer = {"tensor": 1 - lax.axis_index("tensor")}
-    pl.semaphore_signal(barrier, inc=1, device_id=peer, device_id_type=pl.DeviceIdType.MESH)
+    for device in [{"batch": shard(2**bit)} for bit in range(stages)] + [peer]:
+        pl.semaphore_signal(barrier, inc=1, device_id=device, device_id_type=pl.DeviceIdType.MESH)
     pl.semaphore_wait(barrier, stages + 1)
 
     def blocks(chunk, stage):
         order = orders[chunk]
-        return [
+        leaving = [
             block
             for block in range(size)
             if (block >> order[stage]) % 2 and not any((block >> bit) % 2 for bit in order[:stage])
         ]
+        return sorted(leaving, key=lambda block: [-((block >> bit) % 2) for bit in order[stage + 1 :]])
 
     def copy(chunk, stage, source, target):
         return pltpu.make_async_remote_copy(
@@ -176,11 +199,32 @@
             device_id_type=pl.DeviceIdType.MESH,
         )
 
-    def columns(chunk):
-        return pl.ds(places[chunk][1], chunk_width)
+    def grad(chunk):
+        return given[chunk] if chunk < ready else grads.at[chunk - ready]
+
+    def start(chunk):
+        for at, block in enumerate(blocks(chunk, 0)):
+            copy(chunk, 0, grad(chunk).at[shard(block)], landed[0].at[chunk, at]).start()
+
+    def make(at):
+        for fetch in fetches(at):
+            fetch.wait()
+        if at + 1 < len(pieces):
+            for fetch in fetches(at + 1):
+                fetch.start()
+        group = pieces[at][3]
+        per = block_rows // rows
+
+        def product(index, carry):
+            columns = pl.ds(pl.multiple_of(index * block_rows, block_rows), block_rows)
+            result = dot_tn(left_buffer[group % 2, :, columns], right_buffer[at % 2])
+            grads[at, pl.ds(index * per, per)] = result.astype(jnp.bfloat16).reshape(per, rows, chunk_width)
+            return carry
+
+        lax.fori_loop(0, size // per, product, 0)
 
     def summed(chunk, block, stage, tile):
-        total = grads[places[chunk][0]][shard(block), tile, columns(chunk)].astype(jnp.float32)
+        total = grad(chunk)[shard(block), tile, :].astype(jnp.float32)
         for past in range(stage):
             at = blocks(chunk, past).index(block | (1 << orders[chunk][past]))
             total = total + landed[past][chunk, at, tile, :].astype(jnp.float32)
@@ -201,11 +245,8 @@
         )
 
     small_copy(0).start()
-    for chunk in range(len(places)):
-        for at, block in enumerate(blocks(chunk, 0)):
-            copy(
-                chunk, 0, grads[places[chunk][0]].at[shard(block), :, columns(chunk)], landed[0].at[chunk, at]
-            ).start()
+    for chunk in range(ready):
+        start(chunk)
 
     step = min(16, rows)
     for chunk, stage in events:
@@ -219,58 +260,83 @@
                 small_out[:pair_rows, :] = held[:pair_rows] + small_landed[stages, :pair_rows, :]
                 small_out[pair_rows:, :] = held[pair_rows:]
             continue
+        if stage == 0:
+            make(chunk - ready)
+            start(chunk)
+            continue
         whole(chunk, stage - 1).wait_recv()
 
         def work(tile_index, carry, chunk=chunk, stage=stage):
             tile = pl.ds(pl.multiple_of(tile_index * step, step), step)
             if stage < stages:
                 for at, block in enumerate(blocks(chunk, stage)):
-                    leaving[stage][chunk, at, tile, :] = summed(chunk, block, stage, tile).astype(jnp.bfloat16)
+                    landed[stage - 1][chunk, at, tile, :] = summed(chunk, block, stage, tile).astype(jnp.bfloat16)
             else:
                 out[tile, pl.ds(chunk * chunk_width, chunk_width)] = summed(chunk, 0, stage, tile)
             return carry
 
         lax.fori_loop(0, rows // step, work, 0)
         if stage < stages:
-            copy(chunk, stage, leaving[stage].at[chunk], landed[stage].at[chunk]).start()
+            half = size >> (stage + 1)
+            copy(chunk, stage, landed[stage - 1].at[chunk, pl.ds(0, half)], landed[stage].at[chunk]).start()
     for stage in range(stages + 1):
         small_copy(stage).wait_send()
-    for chunk in range(len(places)):
+    for chunk in range(chunks):
         for stage in range(stages):
             whole(chunk, stage).wait_send()
 
 
-def reduce_rows(grads, small, pair_rows):
+def reduce_rows(products, given, small, pair_rows):
     size = lax.axis_size("batch")
     stages = size.bit_length() - 1
-    rows = grads[0].shape[0] // size
-    places = [(at, begin) for at, grad in enumerate(grads) for begin in range(0, grad.shape[1], chunk_width)]
-    chunks = len(places)
-    total_width = chunks * chunk_width
-    halves = [pltpu.VMEM((chunks, size >> (stage + 1), rows, chunk_width), jnp.bfloat16) for stage in range(stages)]
+    rows = given[0].shape[0] // size
+    sources, pieces = [], []
+    for group, (left, rights) in enumerate(products):
+        left_at = tuple(range(len(sources), len(sources) + len(left)))
+        sources.extend(left)
+        for right, first in rights:
+            right_at = tuple(range(len(sources), len(sources) + len(right)))
+            sources.extend(right)
+            pieces += [(left_at, right_at, begin, group) for begin in range(first, right[0].shape[1], chunk_width)]
+    frames = sum(part.shape[0] for part in products[0][0])
+    chunks = len(given) + len(pieces)
+    landings = [pltpu.VMEM((chunks, size >> (stage + 1), rows, chunk_width), jnp.bfloat16) for stage in range(stages)]
     vmem = pl.BlockSpec(memory_space=pltpu.VMEM)
     return pl.pallas_call(
-        functools.partial(reduce_kernel, size, places, pair_rows),
-        out_shape=(jax.ShapeDtypeStruct((rows, total_width), jnp.float32), jax.ShapeDtypeStruct(small.shape, jnp.float32)),
-        in_specs=[vmem] * (len(grads) + 1),
+        functools.partial(reduce_kernel, size, len(given), pieces, pair_rows, len(sources)),
+        out_shape=(
+            jax.ShapeDtypeStruct((rows, chunks * chunk_width), jnp.float32),
+            jax.ShapeDtypeStruct(small.shape, jnp.float32),
+        ),
+        in_specs=[pl.BlockSpec(memory_space=pl.ANY)] * len(sources) + [vmem] * (len(given) + 1),
         out_specs=(vmem, vmem),
-        scratch_shapes=halves
-        + halves[1:]
+        scratch_shapes=[
+            pltpu.VMEM((len(pieces), size, rows, chunk_width), jnp.bfloat16),
+            pltpu.VMEM((2, frames, given[0].shape[0]), jnp.bfloat16),
+            pltpu.VMEM((2, frames, chunk_width), jnp.bfloat16),
+        ]
+        + landings
         + [pltpu.VMEM((stages + 1,) + small.shape, jnp.float32)] * 2
         + [pltpu.SemaphoreType.DMA((chunks, stages))] * 2
-        + [pltpu.SemaphoreType.DMA((stages + 1,))] * 2,
+        + [pltpu.SemaphoreType.DMA((stages + 1,))] * 2
+        + [pltpu.SemaphoreType.DMA((2, 2))] * 2,
         compiler_params=pltpu.CompilerParams(
             collective_id=1, has_side_effects=True, vmem_limit_bytes=60 * 1024 * 1024
         ),
         name="reduce_rows",
-    )(*[grad.reshape(size, rows, grad.shape[1]) for grad in grads], small)
-
-
-def finish_sums(grads, small, pair_rows):
-    if grads[0].shape[0] // lax.axis_size("batch") % 16 == 0 and not any(grad.shape[1] % chunk_width for grad in grads):
-        return reduce_rows(grads, small, pair_rows)
-    small, _ = exchange(small, "batch")
-    paired, _ = exchange(small[:pair_rows], "tensor")
+    )(*sources, *[grad.reshape(size, rows, grad.shape[1]) for grad in given], small)
+
+
+def finish_sums(products, given, small, pair_rows):
+    if given[0].shape[0] // lax.axis_size("batch") % 16 == 0:
+        return reduce_rows(products, given, small, pair_rows)
+    grads = list(given)
+    for left, rights in products:
+        for right, first in rights:
+            part = sum(contract_rows(at, other[:, first:]) for at, other in zip(left, right))
+            grads.append(part.astype(jnp.bfloat16))
+    small = exchange(small, "batch")
+    paired = exchange(small[:pair_rows], "tensor")
     return scatter_batch(jnp.concatenate(grads, axis=1)), jnp.concatenate([paired, small[pair_rows:]])
 
 
@@ -408,22 +474,14 @@
     back_peer = times_transposed(pre_peer, weight_up)
     back_own = times_transposed(pre_own, weight_up)
 
-    def grad_down(tie, begin=0, end=None):
-        own, peer = hidden_own, hidden_peer
-        if tie is not None:
-            own, peer = after((own, peer), tie)
-        return (contract_rows(grad_own, own[:, begin:end]) + contract_rows(grad_peer, peer[:, begin:end])).astype(jnp.bfloat16)
-
-    def grad_up(tie, begin=0, end=None):
-        own, peer = act_own, act_peer
-        if tie is not None:
-            own, peer = after((own, peer), tie)
-        return (contract_rows(own, pre_own[:, begin:end]) + contract_rows(peer, pre_peer[:, begin:end])).astype(jnp.bfloat16)
-
     grad_resid, grad_gain, grad_shift = norm_backward(
         narrow(back_own, back_peer), scaled, inv_std, norm_gain
     )
-    return (grad_resid, grad_gain, grad_shift, grad_up, grad_down)
+    operands = (
+        ((act_own, act_peer), (pre_own, pre_peer)),
+        ((grad_own, grad_peer), (hidden_own, hidden_peer)),
+    )
+    return (grad_resid, grad_gain, grad_shift, operands)
 
 
 def attn_forward(
@@ -491,7 +549,7 @@
     grad_own = grad_after.astype(jnp.bfloat16)
     grad_flat = in_order(grad_own, swap(grad_own))
     slot_frames = grad_flat.shape[0]
-    grad_back_proj = contract_rows(grad_flat, context)
+    back_product = ((grad_flat,), [((context,), 0)])
     grad_context = times_transposed(grad_flat, attention_out).astype(jnp.bfloat16)
     grad_query, grad_keys, grad_values, grad_table, grad_bias = attend_back(
         probs,
@@ -511,7 +569,7 @@
         sum(times_transposed(half[side], attention_in[at]) for at, half in enumerate(halves))
         for side in (0, 1)
     )
-    grad_in_proj = [contract_rows(flat_act, part).astype(jnp.bfloat16) for part in grad_proj]
+    in_product = ((flat_act,), [((part,), 0) for part in grad_proj])
     grad_table_proj = contract_rows(table_in, grad_table)
     grad_resid, grad_gain, grad_shift = norm_backward(
         narrow(back_own, back_peer), scaled, inv_std, norm_gain
@@ -520,10 +578,10 @@
         grad_resid,
         grad_gain,
         grad_shift,
-        grad_in_proj,
+        in_product,
         grad_table_proj,
         grad_bias,
-        grad_back_proj,
+        back_product,
     )
 
 
@@ -556,7 +614,7 @@
     mixed_conv = padded[0:slot_frames] * kernel[0]
     for tap_index in range(1, tap_count):
         mixed_conv = mixed_conv + padded[tap_index : tap_index + slot_frames] * kernel[tap_index]
-    totals, _ = exchange(
+    totals = exchange(
         jnp.stack(
             [
                 jnp.sum(mixed_conv * live_full, axis=0),
@@ -594,7 +652,7 @@
 
 
 def conv_backward(
-    grad_after, saved, norm_gain, pointwise_in, depthwise, batch_gain, pointwise_out, live_full, fillers
+    grad_after, saved, norm_gain, pointwise_in, depthwise, batch_gain, pointwise_out, live_full
 ):
     (
         scaled,
@@ -613,11 +671,11 @@
     grad_own = grad_after.astype(jnp.bfloat16)
     grad_flat = in_order(grad_own, swap(grad_own))
     slot_frames = grad_flat.shape[0]
-    grad_point_out = contract_rows(grad_flat, swished)
+    out_product = ((grad_flat,), [((swished,), 0)])
     grad_swished = times_transposed(grad_flat, pointwise_out)
     grad_normed = grad_swished * batch_sig * (1.0 + normed_batch * (1.0 - batch_sig))
-    sums, filled = exchange(
-        jnp.stack([jnp.sum(grad_normed, axis=0), jnp.sum(grad_normed * centered, axis=0)]), "batch", fillers
+    sums = exchange(
+        jnp.stack([jnp.sum(grad_normed, axis=0), jnp.sum(grad_normed * centered, axis=0)]), "batch"
     )
     gamma = batch_gain.astype(jnp.float32)
     grad_mixed = batch_inv * (
@@ -644,7 +702,7 @@
         (grad_gated * gate_sig).astype(jnp.bfloat16),
         (grad_gated * both_halves[0] * gate_sig * (1.0 - gate_sig)).astype(jnp.bfloat16),
     ]
-    grad_point_in = [contract_rows(flat_act, part) for part in grad_halves]
+    in_product = ((flat_act,), [((part,), 0) for part in grad_halves])
     halves = [split_own(part) for part in grad_halves]
     back_own, back_peer = (
         sum(times_transposed(half[side], pointwise_in[:, at]) for at, half in enumerate(halves))
@@ -653,7 +711,7 @@
     grad_resid, grad_gain, grad_shift = norm_backward(
         narrow(back_own, back_peer), scaled, inv_std, norm_gain
     )
-    return (grad_resid, grad_gain, grad_shift, grad_point_in, grad_point_out, grad_kernel, sums, filled)
+    return (grad_resid, grad_gain, grad_shift, in_product, out_product, grad_kernel, sums)
 
 
 def per_device(
@@ -723,20 +781,18 @@
     grad_stream, gain_five, shift_five = norm_backward(
         grad_final, scaled_final, inv_final, gain_rows[4]
     )
-    grad_branch, gain_four, shift_four, up_two, down_two = ffn_backward(
+    grad_branch, gain_four, shift_four, operands_two = ffn_backward(
         0.5 * grad_stream, saved_four, gain_rows[3], second_up, second_down
     )
     grad_stream = grad_stream + grad_branch
-    early = second_up.shape[1] // 2
     (
         grad_branch,
         gain_three,
         shift_three,
-        point_in_grad,
-        point_out_grad,
+        points_product,
+        point_out_product,
         kernel_grad,
         batch_sums,
-        (down_two, (up_two, up_rest)),
     ) = conv_backward(
         grad_stream,
         saved_three,
@@ -746,12 +802,9 @@
         batch_gain,
         pointwise_out,
         live_full,
-        [down_two, lambda tie: (up_two(tie, 0, early), up_two(tie, early))],
-    )
-    down_two, up_two = scatter_batch(down_two).T, scatter_batch(up_two)
-    points = [part.astype(jnp.bfloat16) for part in (*point_in_grad, point_out_grad)]
+    )
     grad_stream = grad_stream + grad_branch
-    grad_branch, gain_two, shift_two, heads_grad, table_grad, bias_grad, back_grad = attn_backward(
+    grad_branch, gain_two, shift_two, heads_product, table_grad, bias_grad, back_product = attn_backward(
         grad_stream,
         saved_two,
         gain_rows[1],
@@ -761,11 +814,10 @@
         position_bias.shape[2],
     )
     grad_stream = grad_stream + grad_branch
-    grad_branch, gain_one, shift_one, up_one, down_one = ffn_backward(
+    grad_branch, gain_one, shift_one, operands_one = ffn_backward(
         0.5 * grad_stream, saved_one, gain_rows[0], first_up, first_down
     )
     grad_stream = grad_stream + grad_branch
-    up_one, down_one = up_one(None), down_one(None)
     gain_grads = jnp.stack([gain_one, gain_two, gain_three, gain_four, gain_five])
     shift_grads = jnp.stack([shift_one, shift_two, shift_three, shift_four, shift_five])
     norms, channels = gain_grads.shape[0], kernel_grad.shape[1]
@@ -775,14 +827,16 @@
     norm_grads = jnp.pad(jnp.concatenate([gain_grads, shift_grads]), ((0, pair_rows - 2 * norms), (0, 0)))
     sums, small = finish_sums(
         [
-            *points,
-            up_rest,
-            *heads_grad,
-            table_grad.astype(jnp.bfloat16),
-            back_grad.astype(jnp.bfloat16),
-            up_one,
-            down_one,
+            (operands_two[0][0], [(operands_two[0][1], 0)]),
+            (operands_two[1][0], [(operands_two[1][1], 0)]),
+            points_product,
+            point_out_product,
+            heads_product,
+            back_product,
+            (operands_one[0][0], [(operands_one[0][1], 0)]),
+            (operands_one[1][0], [(operands_one[1][1], 0)]),
         ],
+        [table_grad.astype(jnp.bfloat16)],
         jnp.concatenate([norm_grads, packed]),
         pair_rows,
     )
@@ -790,18 +844,19 @@
     packed = small[pair_rows:].reshape(-1)
     kernel_grad = packed[: kernel_grad.size].reshape(kernel_grad.shape)
     bias_grad = packed[kernel_grad.size : kernel_grad.size + bias_grad.size].reshape(bias_grad.shape)
-    def take(part):
+    def take(width):
         nonlocal sums
-        taken, sums = sums[:, : part.shape[1]], sums[:, part.shape[1] :]
+        taken, sums = sums[:, :width], sums[:, width:]
         return taken
 
-    value_point, gate_point, point_out_grad = [take(part) for part in points]
-    point_in_grad = jnp.stack([value_point, gate_point], axis=1)
-    point_out_grad = point_out_grad.T
-    up_two = jnp.concatenate([up_two, take(up_rest)], axis=1)
-    heads_grad = jnp.stack([take(part) for part in heads_grad])
-    table_grad, back_grad = take(table_grad), take(back_grad).T
-    up_one, down_one = take(up_one), take(down_one).T
+    hidden = first_up.shape[1]
+    table_grad = take(channels)
+    up_two, down_two = take(hidden), take(hidden).T
+    point_in_grad = jnp.stack([take(channels) for _ in range(2)], axis=1)
+    point_out_grad = take(channels).T
+    heads_grad = jnp.stack([take(channels) for _ in range(3)])
+    back_grad = take(channels).T
+    up_one, down_one = take(hidden), take(hidden).T
     return (
         output[None],
         grad_stream[None],

time: 554 us -> 498 us (0.90)
  matrix products: 166 us -> 111 us
  Pallas kernels: 236 us -> 255 us
  between operations: 16.8 us -> 2.8 us
  other arithmetic: 50.6 us -> 43.3 us
  waiting for transfers between devices: 24.2 us -> 31.4 us
  local copies, waits for them, and re-layouts: 29.7 us -> 23.7 us
    dot_general x18 -> x1, matrix products: 68.6 us -> 5.1 us  [contract_rows(): lax.dot_general(left, right, (((0,), (0,)), ((), ())), preferred_element_...]
    pallas_call x1, Pallas kernels: 190 us -> 209 us  [reduce_rows(): pl.pallas_call(functools.partial(reduce_kernel, size, len(given), pieces,...]
    unnamed x239 -> x175, local copies, waits for them, and re-layouts: 12.7 us -> 6.29 us
    reduce_sum x1, other arithmetic: 9.21 us -> 3.11 us  [conv_backward(): jnp.sum(grad_mixed * padded[tap_index:tap_index + slot_frames], axis=0)]
  transfers between devices with their start and end apart: 30 -> 28, of which waited for: 12 -> 18; matrix products, arithmetic and copies ran while one was open for 29% -> 9% of each run, Pallas kernels for 40% -> 0%
where the time goes in v4:
time: 498 us; the launch traced here: 488 us
  Pallas kernels  255 us (51%)
  matrix products  111 us (22%)
  other arithmetic  43.3 us (9%)
  waiting for transfers between devices  31.4 us (6%)
  local copies, waits for them, and re-layouts  23.7 us (5%)
  starting transfers between devices  20.8 us (4%)
    pallas_call x1, Pallas kernels, reduce_rows(): pl.pallas_call(functools.partial(reduce_kernel, size, len(given), pieces,...  209 us
    dot_general x20, matrix products, times_transposed(): lax.dot_general(left, right, (((1,), (1,)), ((), ())), preferred_element_...  53.9 us
    pallas_call x1, Pallas kernels, attend_back(): pl.pallas_call(functools.partial(attend_back_kernel, frames, block), out_...  25.6 us
    dot_general x4, matrix products, hidden_of(): pre_act = jnp.dot(act, weight_up, preferred_element_type=jnp.float32)  21.7 us
    pallas_call x1, Pallas kernels, attend(): pl.pallas_call(functools.partial(attend_kernel, frames, block), out_shape...  20.5 us
    ppermute x16, waiting for transfers between devices, swap(): return lax.ppermute(half, 'tensor', [(0, 1), (1, 0)])  20 us
    ppermute x12, starting transfers between devices, exchange(): lax.ppermute(values, axis, [(at, at ^ reach * other) for at in range(size)])  16.8 us
    ppermute x12, waiting for transfers between devices, exchange(): lax.ppermute(values, axis, [(at, at ^ reach * other) for at in range(size)])  11.4 us
  transfers between devices with their start and end apart: 28, of which 18 were waited for; matrix products, arithmetic and copies ran while one was open for 9% of the time, Pallas kernels for 0%

profile of v4, /device:TPU:0, one launch (start us, length us, event | category | flops | bytes accessed | tf_op | source)
XLA Modules:
  0.0 488.5 jit_solution(1652462079031296426)
XLA Ops:
  8.5 7.3 %multiply_convert_fusion.10 = (bf16[512,2048]{1,0:T(8,128)(2,1)S(1)}, f32[512,2048]{1,0:T(8,128)}) fusion(bf16[512,1024]{1,0:T(8,128)(2,1)S(1)} %collective-permute-done.refs_20_, bf16[1024,2048]{1,0:T(8,128)(2,1)} %param.26), kind=kOutput, calls=%fused_computation.13 | convolution fusion | flops 2152726528 | bytes 11534336 | tf_op jit(solution)/shard_map/dot_general | solution.py:455
  18.8 4.8 multiply_convert_fusion.11
  23.7 2.7 fusion.98
  30.3 2.8 subtract_convert_fusion
  33.1 4.1 convolution_convert_fusion.table
  43.9 2.6 add_convert_fusion.4
  46.5 20.5 %attend.1 = (bf16[1024,512]{1,0:T(8,128)(2,1)}, bf16[4,1024,1024]{2,1,0:T(8,128)(2,1)}) custom-call(s32[1]{0:T(128)} %copy.57.lengths, bf16[1024,512]{1,0:T(8,128)(2,1)} %get-tuple-element.136.content, bf16[1024,512]{1,0:T(8,128)(2,1)} %get-tuple-element.135.position, bf16[1024,512]{1,0:T(8,128)(2,1)} %convolution_convert_fusion.3.keys, ...), custom_call_target="tpu_custom_call" | custom-call | tf_op jit(solution)/shard_map/attend/pallas_call | solution.py:387
  69.0 2.7 collective-permute-done.3
  71.6 3.1 fusion.106
  77.1 5.6 %fusion.100 = (bf16[1024,1,512]{2,1,0:T(2,128)(2,1)S(1)}, bf16[1024,1,512]{2,1,0:T(2,128)(2,1)S(1)}) fusion(bf16[1024,2,512]{2,1,0:T(2,128)(2,1)} %param.32), kind=kLoop, calls=%fused_computation.248 | loop fusion | bytes 4194304 | tf_op jit(solution)/shard_map/slice | solution.py:605
  89.7 2.9 collective-permute-start.6
  94.3 2.9 collective-permute-done.7
  97.8 3.6 collective-permute-start.10
  103.2 2.7 collective-permute-done.9
  108.6 2.6 collective-permute-done.11
  116.0 4.7 multiply_convert_fusion.8
  123.3 4.8 multiply_convert_fusion.9
  128.1 2.6 fusion.97
  137.0 5.6 %multiply_convert_fusion.4.refs_3_ = bf16[512,2048]{1,0:T(8,128)(2,1)S(1)} fusion(bf16[512,1024]{1,0:T(8,128)(2,1)S(1)} %collective-permute-done.14.refs_5_, bf16[2048,1024]{1,0:T(8,128)(2,1)S(1)} %copy-done.79, f32[512,2048]{1,0:T(8,128)} %get-tuple-element.173), kind=kOutput, calls=%fused_computation.5 | convolution fusion | flops 2159017984 | bytes 11534336 | tf_op jit(solution)/shard_map/dot_general | solution.py:23
  142.6 5.3 %convolution_convert_fusion.8 = bf16[512,1024]{1,0:T(8,128)(2,1)S(1)} fusion(bf16[512,2048]{1,0:T(8,128)(2,1)S(1)} %multiply_convert_fusion.4.refs_3_, bf16[1024,2048]{1,0:T(8,128)(2,1)} %param.37), kind=kOutput, calls=%fused_computation.122 | convolution fusion | flops 2148007936 | bytes 7340032 | tf_op jit(solution)/shard_map/dot_general | solution.py:23
  148.4 5.2 %multiply_convert_fusion.6.refs_2_ = bf16[512,2048]{1,0:T(8,128)(2,1)S(1)} fusion(bf16[512,1024]{1,0:T(8,128)(2,1)S(1)} %multiply_convert_fusion.15.refs_4_, bf16[2048,1024]{1,0:T(8,128)(2,1)S(1)} %copy-done.79, f32[512,2048]{1,0:T(8,128)} %get-tuple-element.171), kind=kOutput, calls=%fused_computation.7 | convolution fusion | flops 2159017984 | bytes 11534336 | tf_op jit(solution)/shard_map/dot_general | solution.py:23
  153.6 6.0 %multiply_reduce_fusion.5 = (f32[1024]{0:T(1024)S(1)}, f32[512]{0:T(512)S(1)}, f32[512]{0:T(512)S(1)}, f32[1024]{0:T(1024)S(1)}, f32[512,1024]{1,0:T(8,128)S(1)}) fusion(f32[512,1024]{1,0:T(8,128)S(1)} %get-tuple-element.169, f32[512]{0:T(512)S(1)} %add_rsqrt_fusion.1, f32[512]{0:T(512)S(1)} %broadcast_multiply_fusion.11, ...), kind=kOutput, calls=%fused_computation.57 | convolution fusion | flops 2153247744 | bytes 11554816 | tf_op jit(solution)/shard_map/dot_general | solution.py:23
  159.6 2.9 fusion.96
  179.9 3.1 multiply_reduce_fusion
  198.8 25.6 %attend_back.1 = (bf16[1024,512]{1,0:T(8,128)(2,1)}, bf16[1024,512]{1,0:T(8,128)(2,1)}, bf16[1024,512]{1,0:T(8,128)(2,1)}, bf16[2048,512]{1,0:T(8,128)(2,1)}, f32[8,512]{1,0:T(8,128)}) custom-call(bf16[4,1024,1024]{2,1,0:T(8,128)(2,1)} %get-tuple-element.27.probs, bf16[1024,512]{1,0:T(8,128)(2,1)} %convolution_convert_fusion.1.grad_context, ...), custom_call_target="tpu_custom_call" | custom-call | tf_op jit(solution)/shard_map/attend_back/pallas_call | solution.py:438
  244.8 5.1 %convolution_convert_fusion.6 = bf16[1024,512]{1,0:T(8,128)(2,1)} fusion(bf16[2048,1024]{1,0:T(8,128)(2,1)S(1)} %bitcast.203, bf16[2048,512]{1,0:T(8,128)(2,1)} %get-tuple-element.31), kind=kOutput, calls=%fused_computation.120 | convolution fusion | flops 2148007936 | bytes 7340032 | tf_op jit(solution)/shard_map/dot_general | solution.py:17
  249.9 5.7 %multiply_convert_fusion.refs_22_ = bf16[512,2048]{1,0:T(8,128)(2,1)S(1)} fusion(bf16[512,1024]{1,0:T(8,128)(2,1)} %collective-permute-done.26.refs_24_, bf16[2048,1024]{1,0:T(8,128)(2,1)S(1)} %copy-done.82, f32[512,2048]{1,0:T(8,128)} %get-tuple-element.163), kind=kOutput, calls=%fused_computation.1 | convolution fusion | flops 2159017984 | bytes 11534336 | tf_op jit(solution)/shard_map/dot_general | solution.py:23
  255.6 2.6 convolution_convert_fusion.7
  258.5 3.1 multiply_convert_fusion.2.refs_21_
  261.7 4.2 fusion.15
  266.6 209.2 %reduce_rows.1 = (f32[64,12288]{1,0:T(8,128)}, f32[24,1024]{1,0:T(8,128)}) custom-call(bf16[512,1024]{1,0:T(8,128)(2,1)} %copy-done.21, bf16[512,1024]{1,0:T(8,128)(2,1)} %copy-done.49, bf16[512,2048]{1,0:T(8,128)(2,1)} %copy-done.42, bf16[512,2048]{1,0:T(8,128)(2,1)} %copy-done.41, bf16[512,1024]{1,0:T(8,128)(2,1)} %copy-done.18, ...), custom_call_target="tpu_custom_call" | custom-call | tf_op jit(solution)/shard_map/reduce_rows/pallas_call | solution.py:305
  480.2 3.0 slice_bitcast_fusion
  (327 shorter events, 116.2 us)
Async XLA Ops:
  0.7 107.1 %copy-start = (bf16[512,1024]{1,0:T(8,128)(2,1)S(1)}, bf16[512,1024]{1,0:T(8,128)(2,1)}, u32[]{:S(2)}) copy-start(bf16[512,1024]{1,0:T(8,128)(2,1)} %param.36) | copy-start | bytes 3145732
  5.2 21.6 %copy-start.61 = (f32[1,1024]{1,0:T(1,128)}, f32[1,1024]{1,0:T(1,128)S(1)}, u32[]{:S(2)}) copy-start(f32[1,1024]{1,0:T(1,128)S(1)} %get-tuple-element.149) | copy-start | bytes 12292
  5.7 2.8 collective-permute-start
  18.3 5.4 %collective-permute-start.1 = (bf16[512,1024]{1,0:T(8,128)(2,1)S(1)}, bf16[512,1024]{1,0:T(8,128)(2,1)S(1)}, u32[]{:S(2)}, u32[]{:S(2)}) collective-permute-start(bf16[512,1024]{1,0:T(8,128)(2,1)S(1)} %convolution_convert_fusion.10), channel_id=1, source_target_pairs={{0,1},{1,0},{2,3},{3,2},{4,5},{5,4},{6,7},{7,6},{8,9},{9,8},{10,11... | collective-permute-start | bytes 3145736 | tf_op jit(solution)/shard_map/ppermute | solution.py:46
  28.7 8.6 %collective-permute-start.2 = (bf16[512,1024]{1,0:T(8,128)(2,1)}, bf16[512,1024]{1,0:T(8,128)(2,1)}, u32[]{:S(2)}, u32[]{:S(2)}) collective-permute-start(bf16[512,1024]{1,0:T(8,128)(2,1)} %add_convert_fusion.6), channel_id=1, source_target_pairs={{0,1},{1,0},{2,3},{3,2},{4,5},{5,4},{6,7},{7,6},{8,9},{9,8},{10,11... | collective-permute-start | bytes 3145736 | tf_op jit(solution)/shard_map/ppermute | solution.py:46
  46.5 20.5 %copy-start.46 = (bf16[512,1024]{1,0:T(8,128)(2,1)S(1)}, bf16[512,1024]{1,0:T(8,128)(2,1)}, u32[]{:S(2)}) copy-start(bf16[512,1024]{1,0:T(8,128)(2,1)} %param.31) | copy-start | bytes 3145732
  68.8 2.9 collective-permute-start.3
  76.8 5.9 %collective-permute-start.4 = (bf16[512,1024]{1,0:T(8,128)(2,1)}, bf16[512,1024]{1,0:T(8,128)(2,1)}, u32[]{:S(2)}, u32[]{:S(2)}) collective-permute-start(bf16[512,1024]{1,0:T(8,128)(2,1)} %add_convert_fusion.3), channel_id=1, source_target_pairs={{0,1},{1,0},{2,3},{3,2},{4,5},{5,4},{6,7},{7,6},{8,9},{9,8},{10,11... | collective-permute-start | bytes 3145736 | tf_op jit(solution)/shard_map/ppermute | solution.py:46
  89.7 4.5 collective-permute-start.6
  92.6 4.6 collective-permute-start.7
  94.1 3.7 collective-permute-start.5
  97.8 5.5 %collective-permute-start.10 = (f32[3,512]{1,0:T(4,128)S(1)}, f32[3,512]{1,0:T(4,128)S(1)}, u32[]{:S(2)}, u32[]{:S(2)}) collective-permute-start(f32[3,512]{1,0:T(4,128)S(1)} %add_add_fusion.3), channel_id=1, source_target_pairs={{0,24},{2,26},{4,28},{6,30},{8,16},{10,18},{12,20},{14,22},{16,8},... | collective-permute-start | bytes 18440 | tf_op jit(solution)/shard_map/ppermute | solution.py:73
  101.4 4.5 collective-permute-start.9
  101.4 4.5 collective-permute-start.8
  108.5 2.7 collective-permute-start.11
  113.3 2.7 collective-permute-start.12
  123.1 5.0 %collective-permute-start.13 = (bf16[512,1024]{1,0:T(8,128)(2,1)S(1)}, bf16[512,1024]{1,0:T(8,128)(2,1)S(1)}, u32[]{:S(2)}, u32[]{:S(2)}) collective-permute-start(bf16[512,1024]{1,0:T(8,128)(2,1)S(1)} %convolution_convert_fusion.9), channel_id=1, source_target_pairs={{0,1},{1,0},{2,3},{3,2},{4,5},{5,4},{6,7},{7,6},{8,9},{9,8},{10,11... | collective-permute-start | bytes 3145736 | tf_op jit(solution)/shard_map/ppermute | solution.py:46
  134.3 2.7 collective-permute-start.14
  147.9 5.7 %collective-permute-start.15 = (bf16[512,1024]{1,0:T(8,128)(2,1)S(1)}, bf16[512,1024]{1,0:T(8,128)(2,1)S(1)}, u32[]{:S(2)}, u32[]{:S(2)}) collective-permute-start(bf16[512,1024]{1,0:T(8,128)(2,1)S(1)} %convolution_convert_fusion.8), channel_id=1, source_target_pairs={{0,1},{1,0},{2,3},{3,2},{4,5},{5,4},{6,7},{7,6},{8,9},{9,8},{10,11... | collective-permute-start | bytes 3145736 | tf_op jit(solution)/shard_map/ppermute | solution.py:46
  162.6 2.7 collective-permute-start.16
  167.7 3.7 collective-permute-start.18
  169.3 4.5 collective-permute-start.19
  170.2 3.6 collective-permute-start.17
  173.8 5.5 %collective-permute-start.22 = (f32[2,512]{1,0:T(2,128)S(1)}, f32[2,512]{1,0:T(2,128)S(1)}, u32[]{:S(2)}, u32[]{:S(2)}) collective-permute-start(f32[2,512]{1,0:T(2,128)S(1)} %add_add_fusion.5), channel_id=1, source_target_pairs={{0,24},{2,26},{4,28},{6,30},{8,16},{10,18},{12,20},{14,22},{16,8},... | collective-permute-start | bytes 12296 | tf_op jit(solution)/shard_map/ppermute | solution.py:73
  175.3 4.5 collective-permute-start.21
  176.0 3.9 collective-permute-start.20
  187.3 2.7 collective-permute-start.23
  193.7 2.7 collective-permute-start.24
  229.5 2.7 collective-permute-start.25
  236.2 22.2 %copy-start.19 = (bf16[512,1024]{1,0:T(8,128)(2,1)}, bf16[512,1024]{1,0:T(8,128)(2,1)S(1)}, u32[]{:S(2)}) copy-start(bf16[512,1024]{1,0:T(8,128)(2,1)S(1)} %get-tuple-element.99.refs_23_) | copy-start | bytes 3145732
  236.2 13.7 %collective-permute-start.26 = (bf16[512,1024]{1,0:T(8,128)(2,1)S(1)}, bf16[512,1024]{1,0:T(8,128)(2,1)}, u32[]{:S(2)}, u32[]{:S(2)}) collective-permute-start(bf16[512,1024]{1,0:T(8,128)(2,1)S(1)} %get-tuple-element.99.refs_23_), channel_id=1, source_target_pairs={{0,1},{1,0},{2,3},{3,2},{4,5},{5,4},{6,7},{7,6},{8,9},{9,8},{10,11... | collective-permute-start | bytes 3145736 | tf_op jit(solution)/shard_map/ppermute | solution.py:46
  258.2 3.4 collective-permute-start.27
  (83 other events, 342.5 us)
